TPU v7x, 256 devices: a whole 4x4x8 slice. The times are simulated.
256 devices in a mesh: blk: 64 (over z, y, core), par: 4 (over x).
Axes of the slice: x: 4, y: 4, z: 8, core: 2. Of those that a mesh axis runs over, the one named last changes fastest.
Arguments:
- potential: float32 [2048, 32, 1024], P('blk', 'par'), may hold values from 0 to 1
- fiber_angle: bfloat16 [2048, 32, 1024], P('blk', 'par'), may hold values from -3.140625 to 3.140625
- tissue: int32 [2048, 32, 1024], P('blk', 'par'), may hold values 0 or 1
- sensitivity: bfloat16 [2048, 32, 1024], P('blk', 'par'), may hold values from -6 to 6
- conductance: float32 [512], P(('blk', 'par')), may hold values from 0.5 to 1
- brick_slot: int32 [2048], replicated, may hold values from 0 to 2047, as said below
- neighbours: int32 [2048, 4], P('blk'), may hold values from 0 to 2047, as said below
- brick_cell: int32 [2048], P('blk'), may hold values from 0 to 511, as said below
Outputs:
- final_potential: float32 [2048, 32, 1024], P('blk', 'par')
- potential_gradient: float32 [2048, 32, 1024], P('blk', 'par')
- cell_gradient: float32 [512], P(('blk', 'par'))
Inputs may be any that keep to these rules, and one draw needn't show every extreme that they name: brick_slot is a permutation: slot s lies on blk index s // 32. The relation is symmetric: if brick c is beside brick a across x high, a is beside c across x low, and likewise for y. A brick's neighbours always lie on other blk indices. For any two blk indices, exactly 0 or exactly 4 faces of the bricks of the first have their neighbour on the second. `brick_cell`: every parameter cell holds exactly 4 bricks.
All inputs are finite; a program needn't handle non-finite values. No bound on the sum of `tissue` on one device may be relied on, other than what follows from the above.
Results may differ from a plain program's by a relative error of at most 0.0003.
Values sent between devices are 32-bit elements; how exact they have to be, the bound alone decides.
A program may use at most 128 MiB of HBM per device.

v0:
```python
import jax
import jax.numpy as jnp
from jax import lax
from jax.sharding import PartitionSpec as P

BX = 32
STEPS = 1


TIMESTEP = 0.12
THRESHOLD = 0.2
ACROSS = 0.3
ALONG = 1.0
VERTICAL = 0.6


def extended(x, sides, width):
    for axis, dim in sides:
        size, length = (lax.axis_size(axis), x.shape[dim])
        up = [(i, (i + 1) % size) for i in range(size - 1)]
        down = [(j, i) for i, j in up]
        last = lax.slice_in_dim(x, length - width, length, axis=dim)
        initial = lax.slice_in_dim(x, 0, width, axis=dim)
        before = lax.ppermute(last, axis, up)
        after = lax.ppermute(initial, axis, down)
        x = jnp.concatenate([before, x, after], axis=dim)
    return x


def layers(values, brick_edge):
    return jnp.stack(
        [
            values[..., :brick_edge],
            values[..., -brick_edge:],
            values[..., 0::brick_edge],
            values[..., brick_edge - 1 :: brick_edge],
        ],
        axis=1,
    )


def along_x(values, lower_face, upper_face, brick_edge):
    return (
        jnp.concatenate([lower_face, values[..., :-brick_edge]], -1),
        jnp.concatenate([values[..., brick_edge:], upper_face], -1),
    )


def along_y(values, lower_face, upper_face, brick_edge):
    y_index = jnp.arange(values.shape[-1]) % brick_edge
    zero_pad = jnp.zeros(values.shape[:-1] + (1,), values.dtype)
    shifted_down = jnp.concatenate([zero_pad, values[..., :-1]], -1)
    shifted_up = jnp.concatenate([values[..., 1:], zero_pad], -1)
    return (
        jnp.where(y_index == 0, jnp.repeat(lower_face, brick_edge, axis=-1), shifted_down),
        jnp.where(
            y_index == brick_edge - 1, jnp.repeat(upper_face, brick_edge, axis=-1), shifted_up
        ),
    )


def near_values(values, layer_set, padded, brick_edge):
    x_low, x_high = along_x(values, layer_set[:, 0], layer_set[:, 1], brick_edge)
    y_low, y_high = along_y(values, layer_set[:, 2], layer_set[:, 3], brick_edge)
    return (x_low, x_high, y_low, y_high, padded[:, :-2], padded[:, 2:])


def laplace(conduct, values, beside):
    summed = conduct[0] * (beside[0] - values)
    for facet in range(1, 6):
        summed = summed + conduct[facet] * (beside[facet] - values)
    return summed


def brick_terms(conduct, adjoint, beside_adjoint, earlier, beside_state):
    summed = -conduct[0] * (adjoint - beside_adjoint[0]) * (earlier - beside_state[0])
    for facet in range(1, 6):
        summed = summed - conduct[facet] * (adjoint - beside_adjoint[facet]) * (
            earlier - beside_state[facet]
        )
    return jnp.sum(summed, axis=(1, 2))


def weights(tissue, fiber_angle, brick_scale):
    present = tissue.astype(jnp.float32)
    cos_square = jnp.cos(fiber_angle.astype(jnp.float32)) ** 2
    weight_x = present * brick_scale * (ACROSS + (ALONG - ACROSS) * cos_square)
    weight_y = present * brick_scale * (ACROSS + (ALONG - ACROSS) * (1.0 - cos_square))
    weight_z = present * brick_scale * VERTICAL
    return (weight_x, weight_y, weight_z)


def conductances(weight_x, weight_y, weight_z, weight_near, padded_z, brick_edge):
    x_low, x_high = along_x(weight_x, weight_near[:, 0], weight_near[:, 1], brick_edge)
    y_low, y_high = along_y(weight_y, weight_near[:, 2], weight_near[:, 3], brick_edge)
    return (
        weight_x * x_low,
        weight_x * x_high,
        weight_y * y_low,
        weight_y * y_high,
        weight_z * padded_z[:, :-2],
        weight_z * padded_z[:, 2:],
    )


def body(
    potential, fiber_angle, tissue, sensitivity, conductance, brick_slot, neighbours, brick_cell
):
    bricks, z_layers, plane_cells = potential.shape
    brick_edge = BX
    blocks = lax.axis_size("blk")
    capacity = max(4, 8 * bricks // blocks)
    face_count = 4 * bricks
    face_cells = z_layers * brick_edge
    cell_count = conductance.shape[0] * blocks * lax.axis_size("par")
    opposite = jnp.array([1, 0, 3, 2], jnp.int32)
    near_slot = brick_slot[neighbours]
    near_blk = (near_slot // bricks).reshape(-1)
    far_key = (near_slot % bricks * 4 + opposite[None, :]).reshape(-1)
    own_key = jnp.arange(face_count, dtype=jnp.int32)
    matches = near_blk[:, None] == near_blk[None, :]
    send_rank = jnp.sum((matches & (own_key[None, :] < own_key[:, None])).astype(jnp.int32), axis=1)
    recv_rank = jnp.sum((matches & (far_key[None, :] < far_key[:, None])).astype(jnp.int32), axis=1)
    send_slot = near_blk * capacity + send_rank
    recv_slot = near_blk * capacity + recv_rank

    def pack_faces(layer_set):
        flattened = layer_set.reshape(face_count, face_cells)
        outgoing = (
            jnp.zeros((blocks * capacity, face_cells), flattened.dtype).at[send_slot].set(flattened)
        )
        return outgoing.reshape(blocks, capacity, face_cells)

    def unpack_faces(received):
        return received.reshape(blocks * capacity, face_cells)[recv_slot].reshape(
            bricks, 4, z_layers, brick_edge
        )

    params_all = lax.all_gather(conductance, ("blk", "par"), axis=0, tiled=True)
    brick_scale = params_all[brick_cell][:, None, None]
    weight_x, weight_y, weight_z = weights(tissue, fiber_angle, brick_scale)
    weight_layers = jnp.concatenate(
        [layers(weight_x, brick_edge)[:, :2], layers(weight_y, brick_edge)[:, 2:]], axis=1
    )
    weight_near = unpack_faces(
        lax.all_to_all(pack_faces(weight_layers), "blk", split_axis=0, concat_axis=0, tiled=True)
    )
    padded_weight = extended(weight_z, (("par", 1),), 1)
    conduct = conductances(weight_x, weight_y, weight_z, weight_near, padded_weight, brick_edge)
    current = potential
    section = 0
    state_near = unpack_faces(
        lax.all_to_all(
            pack_faces(layers(current, brick_edge)), "blk", split_axis=0, concat_axis=0, tiled=True
        )
    )
    state_padded = extended(current, (("par", 1),), 1)
    stored = [(current, state_near, state_padded)]
    beside = near_values(current, state_near, state_padded, brick_edge)
    ionic_term = current * (1.0 - current) * (current - THRESHOLD)
    current = current + TIMESTEP * (laplace(conduct, current, beside) + ionic_term)
    adjoint = sensitivity.astype(jnp.float32)
    grad_share = jnp.zeros(conductance.shape, jnp.float32)
    onehot_cells = (brick_cell[:, None] == jnp.arange(cell_count, dtype=jnp.int32)[None, :]).astype(
        jnp.float32
    )
    for section in reversed(range(STEPS)):
        earlier, state_near, state_padded = stored[section]
        state_sent, adjoint_sent = (
            lax.all_to_all(
                pack_faces(layers(earlier, brick_edge)),
                "blk",
                split_axis=0,
                concat_axis=0,
                tiled=True,
            ),
            lax.all_to_all(
                pack_faces(layers(adjoint, brick_edge)),
                "blk",
                split_axis=0,
                concat_axis=0,
                tiled=True,
            ),
        )
        state_near = unpack_faces(state_sent)
        adjoint_near = unpack_faces(adjoint_sent)
        both_padded = extended(jnp.stack([earlier, adjoint]), (("par", 2),), 1)
        state_padded = both_padded[0]
        adjoint_padded = both_padded[1]
        beside_state = near_values(earlier, state_near, state_padded, brick_edge)
        beside_adjoint = near_values(adjoint, adjoint_near, adjoint_padded, brick_edge)
        brick_part = brick_terms(conduct, adjoint, beside_adjoint, earlier, beside_state)
        grad_share = lax.psum_scatter(
            jnp.sum(brick_part[:, None] * onehot_cells, axis=0),
            ("blk", "par"),
            scatter_dimension=0,
            tiled=True,
        )
        ionic_slope = -3.0 * earlier * earlier + 2.0 * (1.0 + THRESHOLD) * earlier - THRESHOLD
        adjoint = adjoint + TIMESTEP * (
            laplace(conduct, adjoint, beside_adjoint) + ionic_slope * adjoint
        )
    cell_gradient = TIMESTEP * grad_share / (conductance * float(BX) ** 1.5)
    return (current, adjoint, cell_gradient)


def solution(mesh):
    placed = (
        P("blk", "par", None),
        P("blk", "par", None),
        P("blk", "par", None),
        P("blk", "par", None),
        P(("blk", "par")),
        P(),
        P("blk", None),
        P("blk"),
    )
    return jax.shard_map(
        body,
        mesh=mesh,
        in_specs=placed,
        out_specs=(P("blk", "par", None), P("blk", "par", None), P(("blk", "par"))),
        check_vma=False,
    )
```

profile of v0, /device:TPU:1, one launch (start us, length us, event | category | flops | bytes accessed | tf_op | source)
XLA Modules:
  0.0 338.5 jit_solution(6682684781175762221)
XLA Ops:
  0.7 0.9 dynamic-update-slice
  1.5 81.4 %all-reduce.6 = f32[512]{0:T(512)S(1)} all-reduce(f32[512]{0:T(512)S(1)} %dynamic-update-slice), channel_id=1, replica_groups=mesh['blk'=64,'par'=4] {'blk','par'}, use_global_device_ids=true, to_apply=%add.6 | all-reduce | flops 512 | bytes 4096
  84.3 5.6 %add_multiply_fusion = (f32[32,8,1024]{2,1,0:T(8,128)S(1)}, f32[32,8,1024]{2,1,0:T(8,128)S(1)}, f32[32,8,1024]{2,1,0:T(8,128)}) fusion(bf16[32,8,1024]{2,1,0:T(8,128)(2,1)} %param.10, s32[32,8,1024]{2,1,0:T(8,128)} %param.11, f32[32]{0:T(128)S(1)} %gather_fusion), kind=kLoop, calls=%fused_computation.89 | loop fusion | flops 3145728 | bytes 4718720 | tf_op jit(solution)/shard_map/mul | solution.py:88
  89.9 1.3 slice.174
  91.2 1.3 slice.175
  93.4 1.1 gather_fusion.1
  94.8 1.1 scatter_custom_fusion
  95.8 0.8 reshape.286
  96.6 6.6 %all-to-all-start = ((f32[64,4,256]{2,1,0:T(4,128)}), f32[64,4,256]{2,1,0:T(4,128)}, u32[]{:S(2)}, u32[]{:S(2)}) async-start(f32[64,4,256]{2,1,0:T(4,128)} %reshape.286), calls=%async_computation | async-start | bytes 524288 | tf_op jit(solution)/shard_map/all_to_all | solution.py:146
  103.2 1.1 fusion.69
  104.3 1.0 copy-done.7
  105.3 1.1 pad_maximum_fusion.13
  106.5 3.1 collective-permute-start.4
  109.6 1.3 collective-permute-start.5
  110.9 2.5 fusion.64
  113.3 4.0 %collective-permute-start = (f32[32,1,1024]{2,1,0:T(1,128)}, f32[32,1,1024]{2,1,0:T(1,128)S(1)}, u32[]{:S(2)}, u32[]{:S(2)}) collective-permute-start(f32[32,1,1024]{2,1,0:T(1,128)} %get-tuple-element.26), channel_id=1, source_target_pairs={{0,1},{1,2},{2,3},{4,5},{5,6},{6,7},{8,9},{9,10},{10,11},{12,13},{... | collective-permute-start | bytes 393224 | tf_op jit(solution)/shard_map/ppermute | solution.py:24
  117.3 1.3 collective-permute-start.2
  118.6 0.9 fusion.66
  119.5 4.6 %collective-permute-start.1 = (f32[32,1,1024]{2,1,0:T(1,128)}, f32[32,1,1024]{2,1,0:T(1,128)}, u32[]{:S(2)}, u32[]{:S(2)}) collective-permute-start(f32[32,1,1024]{2,1,0:T(1,128)} %get-tuple-element.33), channel_id=1, source_target_pairs={{0,1},{1,2},{2,3},{4,5},{5,6},{6,7},{8,9},{9,10},{10,11},{12,13},{... | collective-permute-start | bytes 393224 | tf_op jit(solution)/shard_map/ppermute | solution.py:24
  124.1 0.8 slice.206
  124.9 0.8 slice.207
  126.4 1.3 slice.180
  127.7 1.9 slice.181
  129.7 1.7 fusion.61
  131.4 1.7 fusion.62
  133.1 1.7 fusion.63
  134.8 1.1 slice_bitcast_fusion.7
  135.9 0.8 reshape.363
  136.8 1.4 scatter_custom_fusion.2
  138.2 0.8 reshape.298
  139.0 1.9 pad_maximum_fusion.10
  140.9 1.6 fusion.67
  142.5 1.7 fusion.65
  144.2 11.9 %all-to-all-start.2 = ((f32[64,4,256]{2,1,0:T(4,128)}), f32[64,4,256]{2,1,0:T(4,128)}, u32[]{:S(2)}, u32[]{:S(2)}) async-start(f32[64,4,256]{2,1,0:T(4,128)} %reshape.298), calls=%async_computation.2 | async-start | bytes 524288 | tf_op jit(solution)/shard_map/all_to_all | solution.py:177
  156.1 1.1 copy.42
  157.4 1.2 scatter_custom_fusion.1
  158.6 0.8 reshape.290
  159.4 1.6 fusion.68
  161.0 1.3 collective-permute-start.3
  162.3 3.8 %pad_maximum_fusion = f32[2,32,10,1024]{3,2,1,0:T(8,128)} fusion(f32[2,32,1,1024]{3,2,1,0:T(1,128)} %collective-permute-done.5, f32[1,32,8,1024]{3,2,1,0:T(8,128)S(1)} %copy-done.8, f32[1,32,8,1024]{3,2,1,0:T(8,128)S(1)} %bitcast.106, f32[2,32,1,1024]{3,2,1,0:T(1,128)} %collective-permute-done.4), kind=kLoop, calls=%fused_computation.8 | loop fusion | flops 1966080 | bytes 5242880 | tf_op jit(solution)/shard_map/concatenate | solution.py:26
  166.2 2.9 all-to-all-done.2
  169.1 7.6 %all-to-all-start.1 = ((f32[64,4,256]{2,1,0:T(4,128)}), f32[64,4,256]{2,1,0:T(4,128)}, u32[]{:S(2)}, u32[]{:S(2)}) async-start(f32[64,4,256]{2,1,0:T(4,128)} %reshape.290), calls=%async_computation.1 | async-start | bytes 524288 | tf_op jit(solution)/shard_map/all_to_all | solution.py:153
  176.7 4.8 %slice_bitcast_fusion.1 = (f32[32,10,1024]{2,1,0:T(8,128)}, f32[32,10,1024]{2,1,0:T(8,128)}) fusion(f32[2,32,10,1024]{3,2,1,0:T(8,128)} %pad_maximum_fusion), kind=kLoop, calls=%fused_computation.25 | loop fusion | bytes 5242880 | tf_op jit(solution)/shard_map/squeeze | solution.py:189
  181.5 1.0 reshape.287
  182.6 0.8 gather_fusion.2
  184.2 2.6 broadcast_in_dim.65
  186.8 4.6 %reshape.293 = f32[32,8,1024]{2,1,0:T(8,128)} reshape(f32[32,8,32,32]{3,2,1,0:T(8,128)} %broadcast_in_dim.65) | data formatting | bytes 2097152 | tf_op jit(solution)/shard_map/reshape | solution.py:55
  191.4 2.6 broadcast_in_dim.68
  194.0 4.6 %reshape.295 = f32[32,8,1024]{2,1,0:T(8,128)} reshape(f32[32,8,32,32]{3,2,1,0:T(8,128)} %broadcast_in_dim.68) | data formatting | bytes 2097152 | tf_op jit(solution)/shard_map/reshape | solution.py:57
  198.6 1.0 reshape.299
  201.2 2.6 broadcast_in_dim.70
  203.8 4.6 %reshape.301 = f32[32,8,1024]{2,1,0:T(8,128)} reshape(f32[32,8,32,32]{3,2,1,0:T(8,128)} %broadcast_in_dim.70) | data formatting | bytes 2097152 | tf_op jit(solution)/shard_map/reshape | solution.py:55
  208.4 2.6 broadcast_in_dim.71
  211.0 4.6 %reshape.302 = f32[32,8,1024]{2,1,0:T(8,128)} reshape(f32[32,8,32,32]{3,2,1,0:T(8,128)} %broadcast_in_dim.71) | data formatting | bytes 2097152 | tf_op jit(solution)/shard_map/reshape | solution.py:57
  215.6 1.0 reshape.291
  217.5 0.8 slice_bitcast_fusion.8
  218.3 2.6 broadcast_in_dim.66
  220.9 4.6 %reshape.294 = f32[32,8,1024]{2,1,0:T(8,128)} reshape(f32[32,8,32,32]{3,2,1,0:T(8,128)} %broadcast_in_dim.66) | data formatting | bytes 2097152 | tf_op jit(solution)/shard_map/reshape | solution.py:55
  225.5 3.5 %broadcast_in_dim.69 = f32[32,8,32,32]{3,2,1,0:T(8,128)} broadcast(f32[32,8,32]{2,1,0:T(8,128)} %get-tuple-element.45), dimensions={0,1,2} | broadcast | bytes 1081344 | tf_op jit(solution)/shard_map/broadcast_in_dim | solution.py:57
  229.0 4.6 %reshape.296 = f32[32,8,1024]{2,1,0:T(8,128)} reshape(f32[32,8,32,32]{3,2,1,0:T(8,128)} %broadcast_in_dim.69) | data formatting | bytes 2097152 | tf_op jit(solution)/shard_map/reshape | solution.py:57
  233.6 13.9 %fusion.24 = (f32[32]{0:T(128)S(1)}, f32[32,8,1024]{2,1,0:T(8,128)}, f32[32,8,1024]{2,1,0:T(8,128)}, f32[32,8,1024]{2,1,0:T(8,128)}, f32[32,8,1024]{2,1,0:T(8,128)}) fusion(bf16[32,8,1024]{2,1,0:T(8,128)(2,1)S(1)} %copy-done.3, f32[32,8,1024]{2,1,0:T(8,128)S(1)} %copy-done.2, f32[32,10,1024]{2,1,0:T(8,128)} %get-tuple-element.11, ...), kind=kLoop, calls=%fused_computation.51 | loop fusion | flops 13631456 | bytes 32239744 | tf_op jit(solution)/shard_map/reduce_sum | solution.py:81
  247.6 77.4 %all-reduce.7 = f32[512]{0:T(512)S(1)} all-reduce(f32[512]{0:T(512)S(1)} %select_reduce_fusion), channel_id=2, replica_groups=mesh['blk'=64,'par'=4] {'blk','par'}, use_global_device_ids=true, to_apply=%region_7.8.clone | all-reduce | flops 512 | bytes 4096
  325.1 8.5 %convert_add_fusion = f32[32,8,1024]{2,1,0:T(8,128)} fusion(bf16[32,8,1024]{2,1,0:T(8,128)(2,1)S(1)} %copy-done.3, f32[32,8,1024]{2,1,0:T(8,128)} %get-tuple-element.6, f32[32,8,1024]{2,1,0:T(8,128)} %get-tuple-element.7, f32[32,8,1024]{2,1,0:T(8,128)} %get-tuple-element.8, f32[32,8,1024]{2,1,0:T(8,128)} %get-tuple-element.9, ...), kind=kLoop, calls=%fused_computation.15 | loop fusion | flops 8912896 | bytes 16515072 | tf_op jit(solution)/shard_map/add | solution.py:200
  334.6 3.9 %fusion.3 = f32[32,8,1024]{2,1,0:T(8,128)} fusion(f32[32,8,1024]{2,1,0:T(8,128)S(1)} %copy-done.2, f32[32,1,1024]{2,1,0:T(1,128)} %collective-permute-done.3, f32[32,1,1024]{2,1,0:T(1,128)} %collective-permute-done.1, f32[32,8,1024]{2,1,0:T(8,128)S(1)} %copy-done.14, f32[32,8,1024]{2,1,0:T(8,128)S(1)} %copy-done.13, f32[32,8,1024]{2,1,0:T(8,128)S(1)} %copy-done.12, ...), kind=kLoop, calls=%fused_computation.30 | loop fusion | flops 8912896 | bytes 14155776 | tf_op jit(solution)/shard_map/add | solution.py:161
  (95 shorter events, 7.8 us)
Async XLA Ops:
  0.6 92.7 %copy-start = (s32[2048]{0:T(1024)S(1)}, s32[2048]{0:T(1024)}, u32[]{:S(2)}) copy-start(s32[2048]{0:T(1024)} %param.14) | copy-start | bytes 24580
  84.3 8.7 %copy-start.23 = (s32[32,4]{0,1:T(4,128)S(1)}, s32[32,4]{0,1:T(4,128)}, u32[]{:S(2)}) copy-start(s32[32,4]{0,1:T(4,128)} %param.15) | copy-start | bytes 1540
  84.3 9.0 %copy-start.25 = (s32[4]{0:T(128)S(1)}, s32[4]{0:T(128)}, u32[]{:S(2)}) copy-start(s32[4]{0:T(128)} %constant.91.clone) | copy-start | bytes 52
  89.9 3.4 %copy-start.4 = (f32[32,8,1024]{2,1,0:T(8,128)}, f32[32,8,1024]{2,1,0:T(8,128)S(1)}, u32[]{:S(2)}) copy-start(f32[32,8,1024]{2,1,0:T(8,128)S(1)} %get-tuple-element.15) | copy-start | bytes 3145732
  93.3 9.9 %copy-start.3 = (bf16[32,8,1024]{2,1,0:T(8,128)(2,1)S(1)}, bf16[32,8,1024]{2,1,0:T(8,128)(2,1)}, u32[]{:S(2)}) copy-start(bf16[32,8,1024]{2,1,0:T(8,128)(2,1)} %param.12) | copy-start | bytes 1572868
  94.5 10.8 %copy-start.2 = (f32[32,8,1024]{2,1,0:T(8,128)S(1)}, f32[32,8,1024]{2,1,0:T(8,128)}, u32[]{:S(2)}) copy-start(f32[32,8,1024]{2,1,0:T(8,128)} %param.9) | copy-start | bytes 3145732
  94.7 42.0 %copy-start.24 = (s32[128]{0:T(128)}, s32[128]{0:T(128)S(1)}, u32[]{:S(2)}) copy-start(s32[128]{0:T(128)S(1)} %get-tuple-element.54) | copy-start | bytes 1540
  96.6 47.5 %all-to-all-start = ((f32[64,4,256]{2,1,0:T(4,128)}), f32[64,4,256]{2,1,0:T(4,128)}, u32[]{:S(2)}, u32[]{:S(2)}) async-start(f32[64,4,256]{2,1,0:T(4,128)} %reshape.286), calls=%async_computation | async-start | bytes 524288 | tf_op jit(solution)/shard_map/all_to_all | solution.py:146
  104.3 1.0 copy-start.7
  106.5 54.6 %collective-permute-start.4 = (f32[2,32,1,1024]{3,2,1,0:T(1,128)}, f32[2,32,1,1024]{3,2,1,0:T(1,128)}, u32[]{:S(2)}, u32[]{:S(2)}) collective-permute-start(f32[2,32,1,1024]{3,2,1,0:T(1,128)} %get-tuple-element.12), channel_id=1, source_target_pairs={{0,1},{1,2},{2,3},{4,5},{5,6},{6,7},{8,9},{9,10},{10,11},{12,13},{... | collective-permute-start | bytes 786440 | tf_op jit(solution)/shard_map/ppermute | solution.py:24
  109.6 52.7 %collective-permute-start.5 = (f32[2,32,1,1024]{3,2,1,0:T(1,128)}, f32[2,32,1,1024]{3,2,1,0:T(1,128)}, u32[]{:S(2)}, u32[]{:S(2)}) collective-permute-start(f32[2,32,1,1024]{3,2,1,0:T(1,128)} %get-tuple-element.13), channel_id=1, source_target_pairs={{1,0},{2,1},{3,2},{5,4},{6,5},{7,6},{9,8},{10,9},{11,10},{13,12},{... | collective-permute-start | bytes 786440 | tf_op jit(solution)/shard_map/ppermute | solution.py:25
  113.3 120.2 %collective-permute-start = (f32[32,1,1024]{2,1,0:T(1,128)}, f32[32,1,1024]{2,1,0:T(1,128)S(1)}, u32[]{:S(2)}, u32[]{:S(2)}) collective-permute-start(f32[32,1,1024]{2,1,0:T(1,128)} %get-tuple-element.26), channel_id=1, source_target_pairs={{0,1},{1,2},{2,3},{4,5},{5,6},{6,7},{8,9},{9,10},{10,11},{12,13},{... | collective-permute-start | bytes 393224 | tf_op jit(solution)/shard_map/ppermute | solution.py:24
  117.3 116.2 %collective-permute-start.2 = (f32[32,1,1024]{2,1,0:T(1,128)}, f32[32,1,1024]{2,1,0:T(1,128)S(1)}, u32[]{:S(2)}, u32[]{:S(2)}) collective-permute-start(f32[32,1,1024]{2,1,0:T(1,128)} %get-tuple-element.25), channel_id=1, source_target_pairs={{1,0},{2,1},{3,2},{5,4},{6,5},{7,6},{9,8},{10,9},{11,10},{13,12},{... | collective-permute-start | bytes 393224 | tf_op jit(solution)/shard_map/ppermute | solution.py:25
  119.5 214.8 %collective-permute-start.1 = (f32[32,1,1024]{2,1,0:T(1,128)}, f32[32,1,1024]{2,1,0:T(1,128)}, u32[]{:S(2)}, u32[]{:S(2)}) collective-permute-start(f32[32,1,1024]{2,1,0:T(1,128)} %get-tuple-element.33), channel_id=1, source_target_pairs={{0,1},{1,2},{2,3},{4,5},{5,6},{6,7},{8,9},{9,10},{10,11},{12,13},{... | collective-permute-start | bytes 393224 | tf_op jit(solution)/shard_map/ppermute | solution.py:24
  129.7 1.7 copy-start.5
  144.2 24.9 %all-to-all-start.2 = ((f32[64,4,256]{2,1,0:T(4,128)}), f32[64,4,256]{2,1,0:T(4,128)}, u32[]{:S(2)}, u32[]{:S(2)}) async-start(f32[64,4,256]{2,1,0:T(4,128)} %reshape.298), calls=%async_computation.2 | async-start | bytes 524288 | tf_op jit(solution)/shard_map/all_to_all | solution.py:177
  159.4 3.0 copy-start.8
  161.0 173.2 %collective-permute-start.3 = (f32[32,1,1024]{2,1,0:T(1,128)}, f32[32,1,1024]{2,1,0:T(1,128)}, u32[]{:S(2)}, u32[]{:S(2)}) collective-permute-start(f32[32,1,1024]{2,1,0:T(1,128)} %get-tuple-element.34), channel_id=1, source_target_pairs={{1,0},{2,1},{3,2},{5,4},{6,5},{7,6},{9,8},{10,9},{11,10},{13,12},{... | collective-permute-start | bytes 393224 | tf_op jit(solution)/shard_map/ppermute | solution.py:25
  169.1 46.5 %all-to-all-start.1 = ((f32[64,4,256]{2,1,0:T(4,128)}), f32[64,4,256]{2,1,0:T(4,128)}, u32[]{:S(2)}, u32[]{:S(2)}) async-start(f32[64,4,256]{2,1,0:T(4,128)} %reshape.290), calls=%async_computation.1 | async-start | bytes 524288 | tf_op jit(solution)/shard_map/all_to_all | solution.py:153
  225.5 8.1 %copy-start.19 = (f32[32,8,32]{2,1,0:T(8,128)S(1)}, f32[32,8,32]{2,1,0:T(8,128)}, u32[]{:S(2)}) copy-start(f32[32,8,32]{2,1,0:T(8,128)} %get-tuple-element.48) | copy-start | bytes 98308
  225.5 8.1 %copy-start.20 = (f32[32,8,32]{2,1,0:T(8,128)S(1)}, f32[32,8,32]{2,1,0:T(8,128)}, u32[]{:S(2)}) copy-start(f32[32,8,32]{2,1,0:T(8,128)} %get-tuple-element.42) | copy-start | bytes 98308
  225.5 8.1 %copy-start.21 = (f32[32,8,32]{2,1,0:T(8,128)S(1)}, f32[32,8,32]{2,1,0:T(8,128)}, u32[]{:S(2)}) copy-start(f32[32,8,32]{2,1,0:T(8,128)} %get-tuple-element.44) | copy-start | bytes 98308
  225.5 8.1 %copy-start.22 = (f32[32,8,32]{2,1,0:T(8,128)S(1)}, f32[32,8,32]{2,1,0:T(8,128)}, u32[]{:S(2)}) copy-start(f32[32,8,32]{2,1,0:T(8,128)} %get-tuple-element.36) | copy-start | bytes 98308
  233.6 13.9 %copy-start.26 = (s32[32]{0:T(128)S(1)}, s32[32]{0:T(128)}, u32[]{:S(2)}) copy-start(s32[32]{0:T(128)} %param.16) | copy-start | bytes 388
  325.0 8.6 %copy-start.27 = (f32[2]{0:T(128)S(1)}, f32[2]{0:T(128)}, u32[]{:S(2)}) copy-start(f32[2]{0:T(128)} %param.13) | copy-start | bytes 28
  325.0 9.2 %copy-start.6 = (f32[32,8,1024]{2,1,0:T(8,128)S(1)}, f32[32,8,1024]{2,1,0:T(8,128)}, u32[]{:S(2)}) copy-start(f32[32,8,1024]{2,1,0:T(8,128)} %get-tuple-element.16) | copy-start | bytes 3145732
  325.0 9.2 %copy-start.9 = (f32[32,8,1024]{2,1,0:T(8,128)S(1)}, f32[32,8,1024]{2,1,0:T(8,128)}, u32[]{:S(2)}) copy-start(f32[32,8,1024]{2,1,0:T(8,128)} %reshape.294) | copy-start | bytes 3145732
  325.0 9.2 %copy-start.10 = (f32[32,8,1024]{2,1,0:T(8,128)S(1)}, f32[32,8,1024]{2,1,0:T(8,128)}, u32[]{:S(2)}) copy-start(f32[32,8,1024]{2,1,0:T(8,128)} %reshape.296) | copy-start | bytes 3145732
  325.0 9.3 %copy-start.11 = (f32[32,8,1024]{2,1,0:T(8,128)S(1)}, f32[32,8,1024]{2,1,0:T(8,128)}, u32[]{:S(2)}) copy-start(f32[32,8,1024]{2,1,0:T(8,128)} %get-tuple-element.6) | copy-start | bytes 3145732
  325.1 9.3 %copy-start.12 = (f32[32,8,1024]{2,1,0:T(8,128)S(1)}, f32[32,8,1024]{2,1,0:T(8,128)}, u32[]{:S(2)}) copy-start(f32[32,8,1024]{2,1,0:T(8,128)} %get-tuple-element.7) | copy-start | bytes 3145732
  325.1 9.3 %copy-start.13 = (f32[32,8,1024]{2,1,0:T(8,128)S(1)}, f32[32,8,1024]{2,1,0:T(8,128)}, u32[]{:S(2)}) copy-start(f32[32,8,1024]{2,1,0:T(8,128)} %get-tuple-element.8) | copy-start | bytes 3145732
  325.1 9.3 %copy-start.14 = (f32[32,8,1024]{2,1,0:T(8,128)S(1)}, f32[32,8,1024]{2,1,0:T(8,128)}, u32[]{:S(2)}) copy-start(f32[32,8,1024]{2,1,0:T(8,128)} %get-tuple-element.9) | copy-start | bytes 3145732
  325.1 9.3 %copy-start.15 = (f32[32,8,1023]{2,1,0:T(8,128)S(1)}, f32[32,8,1023]{2,1,0:T(8,128)}, u32[]{:S(2)}) copy-start(f32[32,8,1023]{2,1,0:T(8,128)} %get-tuple-element.23) | copy-start | bytes 3142660
  325.1 9.3 %copy-start.16 = (f32[32,8,1023]{2,1,0:T(8,128)S(1)}, f32[32,8,1023]{2,1,0:T(8,128)}, u32[]{:S(2)}) copy-start(f32[32,8,1023]{2,1,0:T(8,128)} %get-tuple-element.24) | copy-start | bytes 3142660
  325.1 9.3 %copy-start.17 = (f32[32,8,992]{2,1,0:T(8,128)S(1)}, f32[32,8,992]{2,1,0:T(8,128)}, u32[]{:S(2)}) copy-start(f32[32,8,992]{2,1,0:T(8,128)} %get-tuple-element.27) | copy-start | bytes 3047428
  325.1 9.5 %copy-start.18 = (f32[32,8,992]{2,1,0:T(8,128)S(1)}, f32[32,8,992]{2,1,0:T(8,128)}, u32[]{:S(2)}) copy-start(f32[32,8,992]{2,1,0:T(8,128)} %get-tuple-element.28) | copy-start | bytes 3047428
  333.7 4.8 %copy-start.1 = (s32[2048]{0:T(1024)S(1)}, s32[2048]{0:T(1024)}, u32[]{:S(2)}) copy-start(s32[2048]{0:T(1024)} %param.14) | copy-start | bytes 24580
where the time goes:
time: 340 us; the launch traced here: 338 us
  blocking collectives  159 us (47%)
  local copies, waits for them, and re-layouts  92.3 us (27%)
  other arithmetic  41.6 us (12%)
  starting transfers between devices  41.6 us (12%)
    unnamed x2, blocking collectives  159 us
    reduce_sum x1, other arithmetic, brick_terms(): return jnp.sum(summed, axis=(1, 2))  13.9 us
    reshape x3, local copies, waits for them, and re-layouts, along_y(): jnp.repeat(lower_face, brick_edge, axis=-1)  13.7 us
    reshape x3, local copies, waits for them, and re-layouts, along_y(): jnp.repeat(upper_face, brick_edge, axis=-1)  13.7 us
    all_to_all x1, starting transfers between devices, body(): lax.all_to_all(pack_faces(layers(adjoint, brick_edge)), 'blk', split_axis...  11.9 us
    ppermute x3, starting transfers between devices, extended(): before = lax.ppermute(last, axis, up)  11.7 us
    broadcast_in_dim x3, local copies, waits for them, and re-layouts, along_y(): jnp.repeat(upper_face, brick_edge, axis=-1)  8.67 us
    add x1, other arithmetic, body(): adjoint + TIMESTEP * (laplace(conduct, adjoint, beside_adjoint) + ionic_s...  8.52 us
  transfers between devices with their start and end apart: 9, of which 1 were waited for; matrix products, arithmetic and copies ran while one was open for 34% of the time, Pallas kernels for 0%

commit v1 on v0

--- a/solution.py
+++ b/solution.py
@@ -103,17 +103,43 @@
     )
 
 
+def z_extended(fields, axis):
+    size = lax.axis_size(axis)
+    up = [(i, (i + 1) % size) for i in range(size - 1)]
+    down = [(j, i) for i, j in up]
+    last = jnp.stack([f[:, -1:] for f in fields])
+    initial = jnp.stack([f[:, :1] for f in fields])
+    before = lax.ppermute(last, axis, up)
+    after = lax.ppermute(initial, axis, down)
+    return [jnp.concatenate([before[k], f, after[k]], axis=1) for k, f in enumerate(fields)]
+
+
 def body(
     potential, fiber_angle, tissue, sensitivity, conductance, brick_slot, neighbours, brick_cell
 ):
     bricks, z_layers, plane_cells = potential.shape
     brick_edge = BX
     blocks = lax.axis_size("blk")
+    parts = lax.axis_size("par")
+    devices = blocks * parts
     capacity = max(4, 8 * bricks // blocks)
     face_count = 4 * bricks
     face_cells = z_layers * brick_edge
-    cell_count = conductance.shape[0] * blocks * lax.axis_size("par")
+    own_cells = conductance.shape[0]
+    cell_count = own_cells * devices
     opposite = jnp.array([1, 0, 3, 2], jnp.int32)
+
+    row = jnp.concatenate([conductance, brick_cell.astype(jnp.float32)])
+    table = lax.all_to_all(
+        jnp.broadcast_to(row[None], (devices, row.shape[0])),
+        ("blk", "par"),
+        split_axis=0,
+        concat_axis=0,
+        tiled=True,
+    )
+    cond_all = table[:, :own_cells].reshape(-1)
+    cell_all = table[::parts, own_cells:].reshape(-1).astype(jnp.int32)
+
     near_slot = brick_slot[neighbours]
     near_blk = (near_slot // bricks).reshape(-1)
     far_key = (near_slot % bricks * 4 + opposite[None, :]).reshape(-1)
@@ -124,84 +150,58 @@
     send_slot = near_blk * capacity + send_rank
     recv_slot = near_blk * capacity + recv_rank
 
-    def pack_faces(layer_set):
-        flattened = layer_set.reshape(face_count, face_cells)
-        outgoing = (
-            jnp.zeros((blocks * capacity, face_cells), flattened.dtype).at[send_slot].set(flattened)
-        )
-        return outgoing.reshape(blocks, capacity, face_cells)
-
-    def unpack_faces(received):
-        return received.reshape(blocks * capacity, face_cells)[recv_slot].reshape(
-            bricks, 4, z_layers, brick_edge
-        )
-
-    params_all = lax.all_gather(conductance, ("blk", "par"), axis=0, tiled=True)
-    brick_scale = params_all[brick_cell][:, None, None]
-    weight_x, weight_y, weight_z = weights(tissue, fiber_angle, brick_scale)
-    weight_layers = jnp.concatenate(
-        [layers(weight_x, brick_edge)[:, :2], layers(weight_y, brick_edge)[:, 2:]], axis=1
-    )
-    weight_near = unpack_faces(
-        lax.all_to_all(pack_faces(weight_layers), "blk", split_axis=0, concat_axis=0, tiled=True)
-    )
-    padded_weight = extended(weight_z, (("par", 1),), 1)
+    present = tissue.astype(jnp.float32)
+    cos_square = jnp.cos(fiber_angle.astype(jnp.float32)) ** 2
+    factor_x = ACROSS + (ALONG - ACROSS) * cos_square
+    factor_y = ACROSS + (ALONG - ACROSS) * (1.0 - cos_square)
+    current = potential
+    adjoint = sensitivity.astype(jnp.float32)
+
+    face_weight = jnp.concatenate(
+        [layers(present * factor_x, brick_edge)[:, :2], layers(present * factor_y, brick_edge)[:, 2:]],
+        axis=1,
+    )
+    fields = jnp.stack([face_weight, layers(current, brick_edge), layers(adjoint, brick_edge)], axis=2)
+    flattened = fields.reshape(face_count, 3 * face_cells)
+    outgoing = jnp.zeros((blocks * capacity, 3 * face_cells), jnp.float32).at[send_slot].set(flattened)
+    received = lax.all_to_all(
+        outgoing.reshape(blocks, capacity, 3 * face_cells), "blk", split_axis=0, concat_axis=0, tiled=True
+    )
+    near = received.reshape(blocks * capacity, 3, z_layers, brick_edge)[recv_slot].reshape(
+        bricks, 4, 3, z_layers, brick_edge
+    )
+    present_padded, state_padded, adjoint_padded = z_extended([present, current, adjoint], "par")
+
+    theta = cond_all[brick_cell]
+    theta_near = cond_all[cell_all[near_slot]]
+    brick_scale = theta[:, None, None]
+    scaled = present * brick_scale
+    weight_x = scaled * factor_x
+    weight_y = scaled * factor_y
+    weight_z = scaled * VERTICAL
+    weight_near = theta_near[:, :, None, None] * near[:, :, 0]
+    padded_weight = present_padded * brick_scale * VERTICAL
     conduct = conductances(weight_x, weight_y, weight_z, weight_near, padded_weight, brick_edge)
-    current = potential
-    section = 0
-    state_near = unpack_faces(
+
+    state_near = near[:, :, 1]
+    adjoint_near = near[:, :, 2]
+    beside_state = near_values(current, state_near, state_padded, brick_edge)
+    beside_adjoint = near_values(adjoint, adjoint_near, adjoint_padded, brick_edge)
+    brick_part = brick_terms(conduct, adjoint, beside_adjoint, current, beside_state)
+    onehot_cells = brick_cell[:, None] == jnp.arange(cell_count, dtype=jnp.int32)[None, :]
+    shares = jnp.sum(jnp.where(onehot_cells, brick_part[:, None], 0.0), axis=0)
+    grad_share = jnp.sum(
         lax.all_to_all(
-            pack_faces(layers(current, brick_edge)), "blk", split_axis=0, concat_axis=0, tiled=True
-        )
-    )
-    state_padded = extended(current, (("par", 1),), 1)
-    stored = [(current, state_near, state_padded)]
-    beside = near_values(current, state_near, state_padded, brick_edge)
+            shares.reshape(devices, own_cells), ("blk", "par"), split_axis=0, concat_axis=0, tiled=True
+        ),
+        axis=0,
+    )
     ionic_term = current * (1.0 - current) * (current - THRESHOLD)
-    current = current + TIMESTEP * (laplace(conduct, current, beside) + ionic_term)
-    adjoint = sensitivity.astype(jnp.float32)
-    grad_share = jnp.zeros(conductance.shape, jnp.float32)
-    onehot_cells = (brick_cell[:, None] == jnp.arange(cell_count, dtype=jnp.int32)[None, :]).astype(
-        jnp.float32
-    )
-    for section in reversed(range(STEPS)):
-        earlier, state_near, state_padded = stored[section]
-        state_sent, adjoint_sent = (
-            lax.all_to_all(
-                pack_faces(layers(earlier, brick_edge)),
-                "blk",
-                split_axis=0,
-                concat_axis=0,
-                tiled=True,
-            ),
-            lax.all_to_all(
-                pack_faces(layers(adjoint, brick_edge)),
-                "blk",
-                split_axis=0,
-                concat_axis=0,
-                tiled=True,
-            ),
-        )
-        state_near = unpack_faces(state_sent)
-        adjoint_near = unpack_faces(adjoint_sent)
-        both_padded = extended(jnp.stack([earlier, adjoint]), (("par", 2),), 1)
-        state_padded = both_padded[0]
-        adjoint_padded = both_padded[1]
-        beside_state = near_values(earlier, state_near, state_padded, brick_edge)
-        beside_adjoint = near_values(adjoint, adjoint_near, adjoint_padded, brick_edge)
-        brick_part = brick_terms(conduct, adjoint, beside_adjoint, earlier, beside_state)
-        grad_share = lax.psum_scatter(
-            jnp.sum(brick_part[:, None] * onehot_cells, axis=0),
-            ("blk", "par"),
-            scatter_dimension=0,
-            tiled=True,
-        )
-        ionic_slope = -3.0 * earlier * earlier + 2.0 * (1.0 + THRESHOLD) * earlier - THRESHOLD
-        adjoint = adjoint + TIMESTEP * (
-            laplace(conduct, adjoint, beside_adjoint) + ionic_slope * adjoint
-        )
+    final = current + TIMESTEP * (laplace(conduct, current, beside_state) + ionic_term)
+    ionic_slope = -3.0 * current * current + 2.0 * (1.0 + THRESHOLD) * current - THRESHOLD
+    adjoint = adjoint + TIMESTEP * (laplace(conduct, adjoint, beside_adjoint) + ionic_slope * adjoint)
     cell_gradient = TIMESTEP * grad_share / (conductance * float(BX) ** 1.5)
-    return (current, adjoint, cell_gradient)
+    return (final, adjoint, cell_gradient)
 
 
 def solution(mesh):

time: 340 us -> 195 us (0.57)
  blocking collectives: 159 us -> 0 us
  local copies, waits for them, and re-layouts: 92.3 us -> 98.2 us
  waiting for transfers between devices: 2.91 us -> 8.13 us
    unnamed x2 -> x0, blocking collectives: 159 us -> none
    all_to_all x3, starting transfers between devices: 26.1 us -> 35.8 us  [the longest x1 15.6 us: body(): lax.all_to_all(jnp.broadcast_to(row[None], (devices, row.shape[0])), ('bl...]
    ppermute x6 -> x2, starting transfers between devices: 15.6 us -> 6.02 us  [the longest x1 4.74 us: z_extended(): before = lax.ppermute(last, axis, up)]
    all_to_all x3, waiting for transfers between devices: 2.9 us -> 8.13 us  [the longest x1 7.24 us: body(): lax.all_to_all(outgoing.reshape(blocks, capacity, 3 * face_cells), 'blk',...]
    gather x4 -> x6, local copies, waits for them, and re-layouts: 2.97 us -> 7.87 us  [the longest x1 3.82 us: body(): received.reshape(blocks * capacity, 3, z_layers, brick_edge)[recv_slot]]
    mul x1 -> x3, other arithmetic: 5.64 us -> 9.15 us  [the longest x1 6.09 us: body(): weight_y = scaled * factor_y]
    another operation x0 -> x3, local copies, waits for them, and re-layouts: none -> 3.48 us  [the longest x2 2.14 us: z_extended(): last = jnp.stack([f[:, -1:] for f in fields])]
    reshape x12 -> x4, local copies, waits for them, and re-layouts: 7.17 us -> 6.63 us  [the longest x1 2.77 us: body(): received.reshape(blocks * capacity, 3, z_layers, brick_edge)[recv_slot]]
  transfers between devices with their start and end apart: 9 -> 5, of which waited for: 1 -> 2; matrix products, arithmetic and copies ran while one was open for 34% -> 35% of each run, Pallas kernels for 0% -> 0%
where the time goes in v1:
time: 195 us; the launch traced here: 194 us
  local copies, waits for them, and re-layouts  98.2 us (50%)
  other arithmetic  44.9 us (23%)
  starting transfers between devices  41.9 us (21%)
  waiting for transfers between devices  8.13 us (4%)
    all_to_all x1, starting transfers between devices, body(): lax.all_to_all(jnp.broadcast_to(row[None], (devices, row.shape[0])), ('bl...  15.6 us
    reshape x3, local copies, waits for them, and re-layouts, along_y(): jnp.repeat(lower_face, brick_edge, axis=-1)  13.8 us
    reshape x3, local copies, waits for them, and re-layouts, along_y(): jnp.repeat(upper_face, brick_edge, axis=-1)  13.8 us
    reduce_sum x1, other arithmetic, brick_terms(): return jnp.sum(summed, axis=(1, 2))  13.7 us
    all_to_all x1, starting transfers between devices, body(): lax.all_to_all(outgoing.reshape(blocks, capacity, 3 * face_cells), 'blk',...  11.8 us
    broadcast_in_dim x3, local copies, waits for them, and re-layouts, along_y(): jnp.repeat(upper_face, brick_edge, axis=-1)  8.83 us
    add x1, other arithmetic, body(): adjoint + TIMESTEP * (laplace(conduct, adjoint, beside_adjoint) + ionic_s...  8.46 us
    all_to_all x1, starting transfers between devices, body(): lax.all_to_all(shares.reshape(devices, own_cells), ('blk', 'par'), split_...  8.38 us
  transfers between devices with their start and end apart: 5, of which 2 were waited for; matrix products, arithmetic and copies ran while one was open for 35% of the time, Pallas kernels for 0%

profile of v1, /device:TPU:1, one launch (start us, length us, event | category | flops | bytes accessed | tf_op | source)
XLA Modules:
  0.0 194.4 jit_solution(3645143998631491091)
XLA Ops:
  0.7 1.3 compare_select_fusion.5
  1.9 0.7 pad_maximum_fusion.11
  2.7 0.7 broadcast_in_dim.76
  3.4 15.6 %all-to-all-start = ((f32[256,1,34]{2,1,0:T(1,128)}), f32[256,1,34]{2,1,0:T(1,128)S(1)}, u32[]{:S(2)}, u32[]{:S(2)}) async-start(f32[256,1,34]{2,1,0:T(1,128)} %broadcast_in_dim.76), calls=%async_computation | async-start | bytes 262144 | tf_op jit(solution)/shard_map/all_to_all | solution.py:133
  19.0 1.8 slice_bitcast_fusion.30
  20.9 1.1 convert_element_type.30
  22.1 1.0 copy-done.19
  23.4 1.1 pad_maximum_fusion.10
  24.6 1.3 collective-permute-start.1
  25.8 1.1 pad_maximum_fusion.9
  27.0 4.7 %collective-permute-start = (f32[3,32,1,1024]{3,2,1,0:T(1,128)}, f32[3,32,1,1024]{3,2,1,0:T(1,128)}, u32[]{:S(2)}, u32[]{:S(2)}) collective-permute-start(f32[3,32,1,1024]{3,2,1,0:T(1,128)} %pad_maximum_fusion.9), channel_id=1, source_target_pairs={{0,1},{1,2},{2,3},{4,5},{5,6},{6,7},{8,9},{9,10},{10,11},{12,13},{... | collective-permute-start | bytes 1179656 | tf_op jit(solution)/shard_map/ppermute | solution.py:112
  31.7 1.4 slice.193
  33.1 1.4 slice.194
  34.4 1.3 slice.190
  35.8 1.3 slice.189
  37.1 0.8 slice_bitcast_fusion.32
  37.9 0.8 slice_bitcast_fusion.26
  38.6 1.6 fusion.66
  40.2 1.6 fusion.65
  42.1 1.1 gather_fusion.1
  46.3 0.7 gather_fusion
  47.0 6.1 %fusion.46 = (f32[32,8,1024]{2,1,0:T(8,128)S(1)}, f32[32,8,1024]{2,1,0:T(8,128)}, f32[32,8,1024]{2,1,0:T(8,128)}, f32[32,8,1024]{2,1,0:T(8,128)}) fusion(bf16[32,8,1024]{2,1,0:T(8,128)(2,1)} %param.10, f32[32]{0:T(128)S(1)} %gather_fusion, s32[32,8,1024]{2,1,0:T(8,128)} %param.11), kind=kLoop, calls=%fused_computation.91 | loop fusion | flops 3407872 | bytes 5767296 | tf_op jit(solution)/shard_map/mul | solution.py:180
  53.1 2.9 %slice.186 = f32[32,8,32]{2,1,0:T(8,128)} slice(f32[32,8,1024]{2,1,0:T(8,128)} %get-tuple-element.15), slice={[0:32:1], [0:8:1], [31:1024:32]} | slice | bytes 65536 | tf_op jit(solution)/shard_map/slice | solution.py:36
  56.0 2.9 %slice.185 = f32[32,8,32]{2,1,0:T(8,128)} slice(f32[32,8,1024]{2,1,0:T(8,128)} %get-tuple-element.15), slice={[0:32:1], [0:8:1], [0:1024:32]} | slice | bytes 65536 | tf_op jit(solution)/shard_map/slice | solution.py:35
  58.8 1.1 slice_bitcast_fusion.28
  59.9 1.2 maximum_bitcast_fusion
  61.2 1.3 copy.20
  62.6 2.6 %reshape.352 = f32[128,768]{1,0:T(8,128)} reshape(f32[32,4,3,8,32]{4,3,2,1,0:T(8,128)} %copy.20) | data formatting | bytes 786432 | tf_op jit(solution)/shard_map/reshape | solution.py:165
  65.1 1.7 scatter_custom_fusion
  66.8 1.2 reshape.299
  68.0 11.8 %all-to-all-start.1 = ((f32[64,4,768]{2,1,0:T(4,128)}), f32[64,4,768]{2,1,0:T(4,128)S(1)}, u32[]{:S(2)}, u32[]{:S(2)}) async-start(f32[64,4,768]{2,1,0:T(4,128)} %reshape.299), calls=%async_computation.1 | async-start | bytes 1572864 | tf_op jit(solution)/shard_map/all_to_all | solution.py:167
  79.8 2.7 %fusion.61 = (f32[32,8,1023]{2,1,0:T(8,128)}, f32[32,8,1023]{2,1,0:T(8,128)}, f32[32,8,1023]{2,1,0:T(8,128)}, f32[32,8,1023]{2,1,0:T(8,128)}) fusion(f32[32,8,1024]{2,1,0:T(8,128)S(1)} %get-tuple-element.12, f32[32,8,1024]{2,1,0:T(8,128)S(1)} %copy-done.3), kind=kLoop, calls=%fused_computation.178 | loop fusion | bytes 8380416 | tf_op jit(solution)/shard_map/slice | solution.py:53
  82.5 2.6 %fusion.62 = (f32[32,8,992]{2,1,0:T(8,128)}, f32[32,8,992]{2,1,0:T(8,128)}, f32[32,8,992]{2,1,0:T(8,128)}, f32[32,8,992]{2,1,0:T(8,128)}) fusion(f32[32,8,1024]{2,1,0:T(8,128)S(1)} %copy-done.4, f32[32,8,1024]{2,1,0:T(8,128)S(1)} %copy-done.3), kind=kLoop, calls=%fused_computation.179 | loop fusion | bytes 8126464 | tf_op jit(solution)/shard_map/slice | solution.py:45
  85.8 0.8 convert_element_type.27
  86.6 1.3 gather_fusion.2
  88.1 1.3 gather_fusion.3
  90.1 1.8 slice_bitcast_fusion.11
  91.9 1.8 slice_bitcast_fusion.14
  93.7 1.8 fusion
  95.5 7.2 %all-to-all-done.1 = f32[64,4,768]{2,1,0:T(4,128)S(1)} async-done(((f32[64,4,768]{2,1,0:T(4,128)}), f32[64,4,768]{2,1,0:T(4,128)S(1)}, u32[]{:S(2)}, u32[]{:S(2)}) %all-to-all-start.1) | async-done | bytes 786464 | tf_op jit(solution)/shard_map/all_to_all | solution.py:167
  102.8 2.8 %reshape.300 = f32[256,3,8,32]{3,2,1,0:T(8,128)} reshape(f32[64,4,768]{2,1,0:T(4,128)S(1)} %all-to-all-done.1) | data formatting | bytes 1572864 | tf_op jit(solution)/shard_map/reshape | solution.py:170
  105.5 3.8 %gather_fusion.4 = f32[128,3,8,32]{3,2,1,0:T(8,128)} fusion(f32[256,3,8,32]{3,2,1,0:T(8,128)} %reshape.300, s32[1024]{0:T(1024)} %pad_clamp_fusion), kind=kCustom, calls=%fused_computation.4 | custom fusion | bytes 786944 | tf_op jit(solution)/shard_map/gather | solution.py:170
  109.4 1.3 slice_bitcast_fusion.1
  110.6 1.2 fusion.48
  111.9 0.8 slice_bitcast_fusion.18
  112.7 0.7 slice_bitcast_fusion.5
  113.5 2.7 %broadcast_in_dim.87 = f32[32,8,32,32]{3,2,1,0:T(8,128)} broadcast(f32[32,8,32]{2,1,0:T(8,128)S(1)} %get-tuple-element.44), dimensions={0,1,2} | broadcast | bytes 1081344 | tf_op jit(solution)/shard_map/broadcast_in_dim | solution.py:57
  116.1 4.6 %reshape.307 = f32[32,8,1024]{2,1,0:T(8,128)} reshape(f32[32,8,32,32]{3,2,1,0:T(8,128)} %broadcast_in_dim.87) | data formatting | bytes 2097152 | tf_op jit(solution)/shard_map/reshape | solution.py:57
  120.7 3.5 %broadcast_in_dim.84 = f32[32,8,32,32]{3,2,1,0:T(8,128)} broadcast(f32[32,8,32]{2,1,0:T(8,128)} %get-tuple-element.38), dimensions={0,1,2} | broadcast | bytes 1081344 | tf_op jit(solution)/shard_map/broadcast_in_dim | solution.py:57
  124.2 4.6 %reshape.304 = f32[32,8,1024]{2,1,0:T(8,128)} reshape(f32[32,8,32,32]{3,2,1,0:T(8,128)} %broadcast_in_dim.84) | data formatting | bytes 2097152 | tf_op jit(solution)/shard_map/reshape | solution.py:57
  128.8 2.7 %broadcast_in_dim.85 = f32[32,8,32,32]{3,2,1,0:T(8,128)} broadcast(f32[32,8,32]{2,1,0:T(8,128)S(1)} %get-tuple-element.48), dimensions={0,1,2} | broadcast | bytes 1081344 | tf_op jit(solution)/shard_map/broadcast_in_dim | solution.py:57
  131.4 4.6 %reshape.305 = f32[32,8,1024]{2,1,0:T(8,128)} reshape(f32[32,8,32,32]{3,2,1,0:T(8,128)} %broadcast_in_dim.85) | data formatting | bytes 2097152 | tf_op jit(solution)/shard_map/reshape | solution.py:57
  136.0 2.6 %broadcast_in_dim.86 = f32[32,8,32,32]{3,2,1,0:T(8,128)} broadcast(f32[32,8,32]{2,1,0:T(8,128)S(1)} %copy-done.24), dimensions={0,1,2} | broadcast | bytes 1081344 | tf_op jit(solution)/shard_map/broadcast_in_dim | solution.py:55
  138.6 4.6 %reshape.306 = f32[32,8,1024]{2,1,0:T(8,128)} reshape(f32[32,8,32,32]{3,2,1,0:T(8,128)} %broadcast_in_dim.86) | data formatting | bytes 2097152 | tf_op jit(solution)/shard_map/reshape | solution.py:55
  143.2 2.6 %broadcast_in_dim.81 = f32[32,8,32,32]{3,2,1,0:T(8,128)} broadcast(f32[32,8,32]{2,1,0:T(8,128)S(1)} %get-tuple-element.39), dimensions={0,1,2} | broadcast | bytes 1081344 | tf_op jit(solution)/shard_map/broadcast_in_dim | solution.py:55
  145.8 4.6 %reshape.302 = f32[32,8,1024]{2,1,0:T(8,128)} reshape(f32[32,8,32,32]{3,2,1,0:T(8,128)} %broadcast_in_dim.81) | data formatting | bytes 2097152 | tf_op jit(solution)/shard_map/reshape | solution.py:55
  150.4 2.6 %broadcast_in_dim.82 = f32[32,8,32,32]{3,2,1,0:T(8,128)} broadcast(f32[32,8,32]{2,1,0:T(8,128)S(1)} %get-tuple-element.49), dimensions={0,1,2} | broadcast | bytes 1081344 | tf_op jit(solution)/shard_map/broadcast_in_dim | solution.py:55
  153.1 4.6 %reshape.303 = f32[32,8,1024]{2,1,0:T(8,128)} reshape(f32[32,8,32,32]{3,2,1,0:T(8,128)} %broadcast_in_dim.82) | data formatting | bytes 2097152 | tf_op jit(solution)/shard_map/reshape | solution.py:55
  157.7 13.7 %fusion.25 = (f32[32]{0:T(128)S(1)}, f32[32,8,1024]{2,1,0:T(8,128)}, f32[32,8,1024]{2,1,0:T(8,128)}, f32[32,8,1024]{2,1,0:T(8,128)}, f32[32,8,1024]{2,1,0:T(8,12...) fusion(bf16[32,8,1024]{2,1,0:T(8,128)(2,1)S(1)} %copy-done.2, f32[32,8,1024]{2,1,0:T(8,128)S(1)} %copy-done.3, ...), kind=kLoop, calls=%fused_computation.48 | loop fusion | flops 14942176 | bytes 33550592 | tf_op jit(solution)/shard_map/reduce_sum | solution.py:81
  171.6 0.8 all_to_all.18
  172.4 8.4 %all-to-all-start.2 = ((f32[256,1,2]{2,1,0:T(1,128)}), f32[256,1,2]{2,1,0:T(1,128)S(1)}, u32[]{:S(2)}, u32[]{:S(2)}) async-start(f32[256,1,2]{2,1,0:T(1,128)} %bitcast.49), calls=%async_computation.2 | async-start | bytes 262144 | tf_op jit(solution)/shard_map/all_to_all | solution.py:194
  180.9 8.5 %convert_add_fusion = f32[32,8,1024]{2,1,0:T(8,128)} fusion(bf16[32,8,1024]{2,1,0:T(8,128)(2,1)S(1)} %copy-done.2, f32[32,8,1024]{2,1,0:T(8,128)} %get-tuple-element.6, f32[32,8,1024]{2,1,0:T(8,128)} %get-tuple-element.7, f32[32,8,1024]{2,1,0:T(8,128)} %get-tuple-element.8, f32[32,8,1024]{2,1,0:T(8,128)} %get-tuple-element.9, ...), kind=kLoop, calls=%fused_computation.12 | loop fusion | flops 8388608 | bytes 16515072 | tf_op jit(solution)/shard_map/add | solution.py:202
  190.1 2.6 %fusion.4 = f32[32,8,1024]{2,1,0:T(8,128)} fusion(f32[32,8,1024]{2,1,0:T(8,128)S(1)} %copy-done.3, f32[32,8,1024]{2,1,0:T(8,128)S(1)} %copy-done.13, f32[32,1,1024]{2,1,0:T(1,128)S(1)} %get-tuple-element.59, f32[32,8,1024]{2,1,0:T(8,128)S(1)} %copy-done.12, f32[32,1,1024]{2,1,0:T(1,128)S(1)} %copy-done.21, f32[32,8,1024]{2,1,0:T(8,128)S(1)} %copy-done.11, ...), kind=kLoop, calls=%fused_computation.27 | loop fusion | flops 7864320 | bytes 14942208 | tf_op jit(solution)/shard_map/add | solution.py:200
  192.7 0.9 all-to-all-done.2
  (116 shorter events, 7.1 us)
Async XLA Ops:
  0.6 41.4 %copy-start = (s32[2048]{0:T(1024)S(1)}, s32[2048]{0:T(1024)}, u32[]{:S(2)}) copy-start(s32[2048]{0:T(1024)} %param.14) | copy-start | bytes 24580
  0.6 21.4 %copy-start.14 = (s32[32,8,1024]{2,1,0:T(8,128)S(1)}, s32[32,8,1024]{2,1,0:T(8,128)}, u32[]{:S(2)}) copy-start(s32[32,8,1024]{2,1,0:T(8,128)} %param.11) | copy-start | bytes 3145732
  3.4 42.8 %all-to-all-start = ((f32[256,1,34]{2,1,0:T(1,128)}), f32[256,1,34]{2,1,0:T(1,128)S(1)}, u32[]{:S(2)}, u32[]{:S(2)}) async-start(f32[256,1,34]{2,1,0:T(1,128)} %broadcast_in_dim.76), calls=%async_computation | async-start | bytes 262144 | tf_op jit(solution)/shard_map/all_to_all | solution.py:133
  22.0 15.8 %copy-start.5 = (f32[32,8,1024]{2,1,0:T(8,128)}, f32[32,8,1024]{2,1,0:T(8,128)S(1)}, u32[]{:S(2)}) copy-start(f32[32,8,1024]{2,1,0:T(8,128)S(1)} %convert_element_type.30) | copy-start | bytes 3145732
  22.0 9.7 %copy-start.2 = (bf16[32,8,1024]{2,1,0:T(8,128)(2,1)S(1)}, bf16[32,8,1024]{2,1,0:T(8,128)(2,1)}, u32[]{:S(2)}) copy-start(bf16[32,8,1024]{2,1,0:T(8,128)(2,1)} %param.12) | copy-start | bytes 1572868
  22.1 1.0 copy-start.19
  23.1 11.3 %copy-start.3 = (f32[32,8,1024]{2,1,0:T(8,128)S(1)}, f32[32,8,1024]{2,1,0:T(8,128)}, u32[]{:S(2)}) copy-start(f32[32,8,1024]{2,1,0:T(8,128)} %param.9) | copy-start | bytes 3145732
  24.6 65.6 %collective-permute-start.1 = (f32[3,32,1,1024]{3,2,1,0:T(1,128)}, f32[3,32,1,1024]{3,2,1,0:T(1,128)}, u32[]{:S(2)}, u32[]{:S(2)}) collective-permute-start(f32[3,32,1,1024]{3,2,1,0:T(1,128)} %pad_maximum_fusion.10), channel_id=1, source_target_pairs={{1,0},{2,1},{3,2},{5,4},{6,5},{7,6},{9,8},{10,9},{11,10},{13,12},{... | collective-permute-start | bytes 1179656 | tf_op jit(solution)/shard_map/ppermute | solution.py:113
  27.0 65.0 %collective-permute-start = (f32[3,32,1,1024]{3,2,1,0:T(1,128)}, f32[3,32,1,1024]{3,2,1,0:T(1,128)}, u32[]{:S(2)}, u32[]{:S(2)}) collective-permute-start(f32[3,32,1,1024]{3,2,1,0:T(1,128)} %pad_maximum_fusion.9), channel_id=1, source_target_pairs={{0,1},{1,2},{2,3},{4,5},{5,6},{6,7},{8,9},{9,10},{10,11},{12,13},{... | collective-permute-start | bytes 1179656 | tf_op jit(solution)/shard_map/ppermute | solution.py:112
  40.2 1.6 copy-start.36
  40.2 1.6 copy-start.38
  42.0 2.0 %copy-start.37 = (s32[4]{0:T(128)S(1)}, s32[4]{0:T(128)}, u32[]{:S(2)}) copy-start(s32[4]{0:T(128)} %constant.89.clone) | copy-start | bytes 52
  42.0 3.5 %copy-start.25 = (f32[32,8,32]{2,1,0:T(8,128)S(1)}, f32[32,8,32]{2,1,0:T(8,128)}, u32[]{:S(2)}) copy-start(f32[32,8,32]{2,1,0:T(8,128)} %slice.193) | copy-start | bytes 98308
  42.1 3.5 %copy-start.26 = (f32[32,8,32]{2,1,0:T(8,128)S(1)}, f32[32,8,32]{2,1,0:T(8,128)}, u32[]{:S(2)}) copy-start(f32[32,8,32]{2,1,0:T(8,128)} %slice.194) | copy-start | bytes 98308
  42.1 3.4 %copy-start.27 = (f32[32,1,8,32]{3,2,0,1:T(8,128)S(1)}, f32[32,1,8,32]{3,2,0,1:T(8,128)}, u32[]{:S(2)}) copy-start(f32[32,1,8,32]{3,2,0,1:T(8,128)} %get-tuple-element.30) | copy-start | bytes 98308
  42.1 3.4 %copy-start.28 = (f32[32,1,8,32]{3,2,0,1:T(8,128)S(1)}, f32[32,1,8,32]{3,2,0,1:T(8,128)}, u32[]{:S(2)}) copy-start(f32[32,1,8,32]{3,2,0,1:T(8,128)} %get-tuple-element.31) | copy-start | bytes 98308
  47.0 6.1 %copy-start.34 = (f32[32]{0:T(128)}, f32[32]{0:T(128)S(1)}, u32[]{:S(2)}) copy-start(f32[32]{0:T(128)S(1)} %gather_fusion) | copy-start | bytes 388
  68.0 34.8 %all-to-all-start.1 = ((f32[64,4,768]{2,1,0:T(4,128)}), f32[64,4,768]{2,1,0:T(4,128)S(1)}, u32[]{:S(2)}, u32[]{:S(2)}) async-start(f32[64,4,768]{2,1,0:T(4,128)} %reshape.299), calls=%async_computation.1 | async-start | bytes 1572864 | tf_op jit(solution)/shard_map/all_to_all | solution.py:167
  79.8 2.7 %copy-start.4 = (f32[32,8,1024]{2,1,0:T(8,128)S(1)}, f32[32,8,1024]{2,1,0:T(8,128)}, u32[]{:S(2)}) copy-start(f32[32,8,1024]{2,1,0:T(8,128)} %get-tuple-element.13) | copy-start | bytes 3145732
  88.1 5.6 %copy-start.35 = (f32[32]{0:T(128)S(1)}, f32[32]{0:T(128)}, u32[]{:S(2)}) copy-start(f32[32]{0:T(128)} %copy-done.34) | copy-start | bytes 388
  90.1 3.6 %copy-start.20 = (f32[32,8,1024]{2,1,0:T(8,128)S(1)}, f32[32,8,1024]{2,1,0:T(8,128)}, u32[]{:S(2)}) copy-start(f32[32,8,1024]{2,1,0:T(8,128)} %copy-done.19) | copy-start | bytes 3145732
  105.5 5.1 %copy-start.29 = (f32[32,4]{1,0:T(8,128)S(1)}, f32[32,4]{1,0:T(8,128)}, u32[]{:S(2)}) copy-start(f32[32,4]{1,0:T(8,128)} %reshape.333) | copy-start | bytes 1540
  131.4 4.6 %copy-start.24 = (f32[32,8,32]{2,1,0:T(8,128)S(1)}, f32[32,8,32]{2,1,0:T(8,128)}, u32[]{:S(2)}) copy-start(f32[32,8,32]{2,1,0:T(8,128)} %get-tuple-element.45) | copy-start | bytes 98308
  153.0 4.7 %copy-start.21 = (f32[32,1,1024]{2,1,0:T(1,128)S(1)}, f32[32,1,1024]{2,1,0:T(1,128)}, u32[]{:S(2)}) copy-start(f32[32,1,1024]{2,1,0:T(1,128)} %get-tuple-element.56) | copy-start | bytes 393220
  153.0 4.7 %copy-start.22 = (f32[32,1,1024]{2,1,0:T(1,128)S(1)}, f32[32,1,1024]{2,1,0:T(1,128)}, u32[]{:S(2)}) copy-start(f32[32,1,1024]{2,1,0:T(1,128)} %get-tuple-element.58) | copy-start | bytes 393220
  153.0 4.7 %copy-start.23 = (f32[32,1,1024]{2,1,0:T(1,128)S(1)}, f32[32,1,1024]{2,1,0:T(1,128)}, u32[]{:S(2)}) copy-start(f32[32,1,1024]{2,1,0:T(1,128)} %get-tuple-element.55) | copy-start | bytes 393220
  153.0 4.7 %copy-start.30 = (pred[1024]{0:T(1024)(128)(4,1)S(1)}, pred[1024]{0:T(1024)(128)(4,1)}, u32[]{:S(2)}) copy-start(pred[1024]{0:T(1024)(128)(4,1)} %get-tuple-element.70) | copy-start | bytes 3076
  153.0 4.7 %copy-start.32 = (pred[1024]{0:T(1024)(128)(4,1)S(1)}, pred[1024]{0:T(1024)(128)(4,1)}, u32[]{:S(2)}) copy-start(pred[1024]{0:T(1024)(128)(4,1)} %get-tuple-element.71) | copy-start | bytes 3076
  157.7 13.7 %copy-start.39 = (s32[32]{0:T(128)S(1)}, s32[32]{0:T(128)}, u32[]{:S(2)}) copy-start(s32[32]{0:T(128)} %param.16) | copy-start | bytes 388
  172.4 21.2 %all-to-all-start.2 = ((f32[256,1,2]{2,1,0:T(1,128)}), f32[256,1,2]{2,1,0:T(1,128)S(1)}, u32[]{:S(2)}, u32[]{:S(2)}) async-start(f32[256,1,2]{2,1,0:T(1,128)} %bitcast.49), calls=%async_computation.2 | async-start | bytes 262144 | tf_op jit(solution)/shard_map/all_to_all | solution.py:194
  180.8 8.6 %copy-start.6 = (f32[32,8,1024]{2,1,0:T(8,128)S(1)}, f32[32,8,1024]{2,1,0:T(8,128)}, u32[]{:S(2)}) copy-start(f32[32,8,1024]{2,1,0:T(8,128)} %reshape.305) | copy-start | bytes 3145732
  180.8 8.6 %copy-start.7 = (f32[32,8,1024]{2,1,0:T(8,128)S(1)}, f32[32,8,1024]{2,1,0:T(8,128)}, u32[]{:S(2)}) copy-start(f32[32,8,1024]{2,1,0:T(8,128)} %reshape.303) | copy-start | bytes 3145732
  180.8 8.6 %copy-start.8 = (f32[32,8,1024]{2,1,0:T(8,128)S(1)}, f32[32,8,1024]{2,1,0:T(8,128)}, u32[]{:S(2)}) copy-start(f32[32,8,1024]{2,1,0:T(8,128)} %get-tuple-element.6) | copy-start | bytes 3145732
  180.8 8.6 %copy-start.9 = (f32[32,8,1024]{2,1,0:T(8,128)S(1)}, f32[32,8,1024]{2,1,0:T(8,128)}, u32[]{:S(2)}) copy-start(f32[32,8,1024]{2,1,0:T(8,128)} %get-tuple-element.7) | copy-start | bytes 3145732
  180.8 8.6 %copy-start.10 = (f32[32,8,1024]{2,1,0:T(8,128)S(1)}, f32[32,8,1024]{2,1,0:T(8,128)}, u32[]{:S(2)}) copy-start(f32[32,8,1024]{2,1,0:T(8,128)} %get-tuple-element.8) | copy-start | bytes 3145732
  180.8 8.6 %copy-start.11 = (f32[32,8,1024]{2,1,0:T(8,128)S(1)}, f32[32,8,1024]{2,1,0:T(8,128)}, u32[]{:S(2)}) copy-start(f32[32,8,1024]{2,1,0:T(8,128)} %get-tuple-element.9) | copy-start | bytes 3145732
  180.8 8.6 %copy-start.12 = (f32[32,8,1024]{2,1,0:T(8,128)S(1)}, f32[32,8,1024]{2,1,0:T(8,128)}, u32[]{:S(2)}) copy-start(f32[32,8,1024]{2,1,0:T(8,128)} %get-tuple-element.10) | copy-start | bytes 3145732
  180.8 8.6 %copy-start.13 = (f32[32,8,1024]{2,1,0:T(8,128)S(1)}, f32[32,8,1024]{2,1,0:T(8,128)}, u32[]{:S(2)}) copy-start(f32[32,8,1024]{2,1,0:T(8,128)} %get-tuple-element.11) | copy-start | bytes 3145732
  180.8 8.6 %copy-start.15 = (f32[32,8,1023]{2,1,0:T(8,128)S(1)}, f32[32,8,1023]{2,1,0:T(8,128)}, u32[]{:S(2)}) copy-start(f32[32,8,1023]{2,1,0:T(8,128)} %get-tuple-element.72) | copy-start | bytes 3142660
  180.9 8.6 %copy-start.16 = (f32[32,8,1023]{2,1,0:T(8,128)S(1)}, f32[32,8,1023]{2,1,0:T(8,128)}, u32[]{:S(2)}) copy-start(f32[32,8,1023]{2,1,0:T(8,128)} %get-tuple-element.73) | copy-start | bytes 3142660
  180.9 8.6 %copy-start.17 = (f32[32,8,992]{2,1,0:T(8,128)S(1)}, f32[32,8,992]{2,1,0:T(8,128)}, u32[]{:S(2)}) copy-start(f32[32,8,992]{2,1,0:T(8,128)} %get-tuple-element.74) | copy-start | bytes 3047428
  180.9 9.2 %copy-start.18 = (f32[32,8,992]{2,1,0:T(8,128)S(1)}, f32[32,8,992]{2,1,0:T(8,128)}, u32[]{:S(2)}) copy-start(f32[32,8,992]{2,1,0:T(8,128)} %get-tuple-element.75) | copy-start | bytes 3047428
  180.9 9.2 %copy-start.31 = (pred[1024]{0:T(1024)(128)(4,1)S(1)}, pred[1024]{0:T(1024)(128)(4,1)}, u32[]{:S(2)}) copy-start(pred[1024]{0:T(1024)(128)(4,1)} %get-tuple-element.70) | copy-start | bytes 3076
  180.9 9.2 %copy-start.33 = (pred[1024]{0:T(1024)(128)(4,1)S(1)}, pred[1024]{0:T(1024)(128)(4,1)}, u32[]{:S(2)}) copy-start(pred[1024]{0:T(1024)(128)(4,1)} %get-tuple-element.71) | copy-start | bytes 3076
  190.1 3.8 %copy-start.40 = (f32[2]{0:T(128)S(1)}, f32[2]{0:T(128)}, u32[]{:S(2)}) copy-start(f32[2]{0:T(128)} %param.13) | copy-start | bytes 28
  190.1 4.3 %copy-start.1 = (s32[2048]{0:T(1024)S(1)}, s32[2048]{0:T(1024)}, u32[]{:S(2)}) copy-start(s32[2048]{0:T(1024)} %param.14) | copy-start | bytes 24580

commit v2 on v1

--- a/solution.py
+++ b/solution.py
@@ -2,6 +2,8 @@
 import jax.numpy as jnp
 from jax import lax
 from jax.sharding import PartitionSpec as P
+from jax.experimental import pallas as pl
+from jax.experimental.pallas import tpu as pltpu
 
 BX = 32
 STEPS = 1
@@ -103,15 +105,102 @@
     )
 
 
-def z_extended(fields, axis):
-    size = lax.axis_size(axis)
-    up = [(i, (i + 1) % size) for i in range(size - 1)]
-    down = [(j, i) for i, j in up]
-    last = jnp.stack([f[:, -1:] for f in fields])
-    initial = jnp.stack([f[:, :1] for f in fields])
-    before = lax.ppermute(last, axis, up)
-    after = lax.ppermute(initial, axis, down)
-    return [jnp.concatenate([before[k], f, after[k]], axis=1) for k, f in enumerate(fields)]
+GROUP = 8
+
+
+def expanders(edge, cells):
+    lane = jnp.arange(cells, dtype=jnp.int32)[None, :]
+    k = jnp.arange(edge, dtype=jnp.int32)[:, None]
+    return jnp.stack(
+        [lane == k, lane == cells - edge + k, lane == edge * k, lane == edge * k + edge - 1]
+    ).astype(jnp.float32)
+
+
+def cell_kernel(scale_ref, expand_ref, tissue_ref, angle_ref, u_ref, l_ref, face_ref, halo_ref,
+                u_out, l_out, part_out):
+    g = pl.program_id(0)
+    nz, cells = u_ref.shape[1], u_ref.shape[2]
+    edge = face_ref.shape[-1]
+    lane = lax.broadcasted_iota(jnp.int32, (nz, cells), 1)
+    row = lax.broadcasted_iota(jnp.int32, (nz, cells), 0)
+    ycoord = lane % edge
+    masks = (lane < edge, lane >= cells - edge, ycoord == 0, ycoord == edge - 1)
+    shifts = (edge, cells - edge, 1, cells - 1)
+    zlo = row == 0
+    zhi = row == nz - 1
+
+    def one(i, carry):
+        b = g * GROUP + i
+        th = scale_ref[b, 0]
+        present = tissue_ref[i].astype(jnp.float32)
+        c = jnp.cos(angle_ref[i].astype(jnp.float32))
+        c2 = c * c
+        scaled = present * th
+        wx = scaled * (ACROSS + (ALONG - ACROSS) * c2)
+        wy = scaled * (ACROSS + (ALONG - ACROSS) * (1.0 - c2))
+        wz = scaled * VERTICAL
+        u = u_ref[i]
+        l = l_ref[i].astype(jnp.float32)
+        halo = halo_ref[i]
+        conds, ub, lb = [], [], []
+        for f in range(4):
+            ext = jnp.dot(face_ref[i, f], expand_ref[f], precision=lax.Precision.HIGHEST,
+                          preferred_element_type=jnp.float32)
+            w_self = wx if f < 2 else wy
+            w_near = jnp.where(masks[f], scale_ref[b, 1 + f] * ext[:nz], pltpu.roll(w_self, shifts[f], 1))
+            conds.append(w_self * w_near)
+            ub.append(jnp.where(masks[f], ext[nz:2 * nz], pltpu.roll(u, shifts[f], 1)))
+            lb.append(jnp.where(masks[f], ext[2 * nz:], pltpu.roll(l, shifts[f], 1)))
+        wz_lo = jnp.where(zlo, (halo[0:1] * th) * VERTICAL, pltpu.roll(wz, 1, 0))
+        wz_hi = jnp.where(zhi, (halo[3:4] * th) * VERTICAL, pltpu.roll(wz, nz - 1, 0))
+        conds += [wz * wz_lo, wz * wz_hi]
+        ub += [jnp.where(zlo, halo[1:2], pltpu.roll(u, 1, 0)), jnp.where(zhi, halo[4:5], pltpu.roll(u, nz - 1, 0))]
+        lb += [jnp.where(zlo, halo[2:3], pltpu.roll(l, 1, 0)), jnp.where(zhi, halo[5:6], pltpu.roll(l, nz - 1, 0))]
+        lap_u = conds[0] * (ub[0] - u)
+        lap_l = conds[0] * (lb[0] - l)
+        terms = -conds[0] * (l - lb[0]) * (u - ub[0])
+        for k in range(1, 6):
+            lap_u = lap_u + conds[k] * (ub[k] - u)
+            lap_l = lap_l + conds[k] * (lb[k] - l)
+            terms = terms - conds[k] * (l - lb[k]) * (u - ub[k])
+        ionic = u * (1.0 - u) * (u - THRESHOLD)
+        slope = -3.0 * u * u + 2.0 * (1.0 + THRESHOLD) * u - THRESHOLD
+        u_out[i] = u + TIMESTEP * (lap_u + ionic)
+        l_out[i] = l + TIMESTEP * (lap_l + slope * l)
+        col = jnp.sum(terms, axis=0, keepdims=True)
+        acc = col[:, 0:128]
+        for t in range(1, cells // 128):
+            acc = acc + col[:, t * 128:(t + 1) * 128]
+        part_out[i] = acc
+        return carry
+
+    lax.fori_loop(0, GROUP, one, 0)
+
+
+def cell_step(scales, tissue, angle, potential, sensitivity, faces, halos, interpret=False):
+    bricks, nz, cells = potential.shape
+    edge = faces.shape[-1]
+    expand = expanders(edge, cells)
+    blk3 = lambda: pl.BlockSpec((GROUP, nz, cells), lambda g: (g, 0, 0))
+    return pl.pallas_call(
+        cell_kernel,
+        grid=(bricks // GROUP,),
+        in_specs=[
+            pl.BlockSpec(memory_space=pltpu.SMEM),
+            pl.BlockSpec((4, edge, cells), lambda g: (0, 0, 0)),
+            blk3(), blk3(), blk3(), blk3(),
+            pl.BlockSpec((GROUP, 4, 3 * nz, edge), lambda g: (g, 0, 0, 0)),
+            pl.BlockSpec((GROUP, 6, cells), lambda g: (g, 0, 0)),
+        ],
+        out_specs=[blk3(), blk3(), pl.BlockSpec((GROUP, 1, 128), lambda g: (g, 0, 0))],
+        out_shape=[
+            jax.ShapeDtypeStruct((bricks, nz, cells), jnp.float32),
+            jax.ShapeDtypeStruct((bricks, nz, cells), jnp.float32),
+            jax.ShapeDtypeStruct((bricks, 1, 128), jnp.float32),
+        ],
+        compiler_params=pltpu.CompilerParams(dimension_semantics=("parallel",)),
+        interpret=interpret,
+    )(scales, expand, tissue, angle, potential, sensitivity, faces, halos)
 
 
 def body(
@@ -150,44 +239,44 @@
     send_slot = near_blk * capacity + send_rank
     recv_slot = near_blk * capacity + recv_rank
 
-    present = tissue.astype(jnp.float32)
-    cos_square = jnp.cos(fiber_angle.astype(jnp.float32)) ** 2
-    factor_x = ACROSS + (ALONG - ACROSS) * cos_square
-    factor_y = ACROSS + (ALONG - ACROSS) * (1.0 - cos_square)
-    current = potential
     adjoint = sensitivity.astype(jnp.float32)
-
-    face_weight = jnp.concatenate(
-        [layers(present * factor_x, brick_edge)[:, :2], layers(present * factor_y, brick_edge)[:, 2:]],
+    tissue_faces = layers(tissue, brick_edge).astype(jnp.float32)
+    cos_faces = jnp.cos(layers(fiber_angle, brick_edge).astype(jnp.float32)) ** 2
+    factor_faces = jnp.concatenate(
+        [
+            ACROSS + (ALONG - ACROSS) * cos_faces[:, :2],
+            ACROSS + (ALONG - ACROSS) * (1.0 - cos_faces[:, 2:]),
+        ],
         axis=1,
     )
-    fields = jnp.stack([face_weight, layers(current, brick_edge), layers(adjoint, brick_edge)], axis=2)
+    fields = jnp.stack(
+        [tissue_faces * factor_faces, layers(potential, brick_edge), layers(adjoint, brick_edge)], axis=2
+    )
     flattened = fields.reshape(face_count, 3 * face_cells)
     outgoing = jnp.zeros((blocks * capacity, 3 * face_cells), jnp.float32).at[send_slot].set(flattened)
     received = lax.all_to_all(
         outgoing.reshape(blocks, capacity, 3 * face_cells), "blk", split_axis=0, concat_axis=0, tiled=True
     )
-    near = received.reshape(blocks * capacity, 3, z_layers, brick_edge)[recv_slot].reshape(
-        bricks, 4, 3, z_layers, brick_edge
-    )
-    present_padded, state_padded, adjoint_padded = z_extended([present, current, adjoint], "par")
+    faces = received.reshape(blocks * capacity, 3 * face_cells)[recv_slot].reshape(
+        bricks, 4, 3 * z_layers, brick_edge
+    )
+
+    size = lax.axis_size("par")
+    up = [(i, i + 1) for i in range(size - 1)]
+    down = [(j, i) for i, j in up]
+    last = jnp.stack([tissue[:, -1].astype(jnp.float32), potential[:, -1], adjoint[:, -1]], axis=1)
+    initial = jnp.stack([tissue[:, 0].astype(jnp.float32), potential[:, 0], adjoint[:, 0]], axis=1)
+    halos = jnp.concatenate([lax.ppermute(last, "par", up), lax.ppermute(initial, "par", down)], axis=1)
 
     theta = cond_all[brick_cell]
     theta_near = cond_all[cell_all[near_slot]]
-    brick_scale = theta[:, None, None]
-    scaled = present * brick_scale
-    weight_x = scaled * factor_x
-    weight_y = scaled * factor_y
-    weight_z = scaled * VERTICAL
-    weight_near = theta_near[:, :, None, None] * near[:, :, 0]
-    padded_weight = present_padded * brick_scale * VERTICAL
-    conduct = conductances(weight_x, weight_y, weight_z, weight_near, padded_weight, brick_edge)
-
-    state_near = near[:, :, 1]
-    adjoint_near = near[:, :, 2]
-    beside_state = near_values(current, state_near, state_padded, brick_edge)
-    beside_adjoint = near_values(adjoint, adjoint_near, adjoint_padded, brick_edge)
-    brick_part = brick_terms(conduct, adjoint, beside_adjoint, current, beside_state)
+    scales = jnp.concatenate(
+        [theta[:, None], theta_near, jnp.zeros((bricks, 3), jnp.float32)], axis=1
+    )
+    final, adjoint, parts_out = cell_step(
+        scales, tissue, fiber_angle, potential, sensitivity, faces, halos
+    )
+    brick_part = jnp.sum(parts_out, axis=(1, 2))
     onehot_cells = brick_cell[:, None] == jnp.arange(cell_count, dtype=jnp.int32)[None, :]
     shares = jnp.sum(jnp.where(onehot_cells, brick_part[:, None], 0.0), axis=0)
     grad_share = jnp.sum(
@@ -196,10 +285,6 @@
         ),
         axis=0,
     )
-    ionic_term = current * (1.0 - current) * (current - THRESHOLD)
-    final = current + TIMESTEP * (laplace(conduct, current, beside_state) + ionic_term)
-    ionic_slope = -3.0 * current * current + 2.0 * (1.0 + THRESHOLD) * current - THRESHOLD
-    adjoint = adjoint + TIMESTEP * (laplace(conduct, adjoint, beside_adjoint) + ionic_slope * adjoint)
     cell_gradient = TIMESTEP * grad_share / (conductance * float(BX) ** 1.5)
     return (final, adjoint, cell_gradient)
 

time: 195 us -> 137 us (0.70)
  local copies, waits for them, and re-layouts: 98.2 us -> 29.7 us
  other arithmetic: 44.9 us -> 14.6 us
  Pallas kernels: 0 us -> 22.1 us
  blocking collectives: 0 us -> 21 us
  starting transfers between devices: 41.9 us -> 33.5 us
  waiting for transfers between devices: 8.13 us -> 14.7 us
    reshape x7 -> x2, local copies, waits for them, and re-layouts: 30.3 us -> 1.93 us  [body(): received.reshape(blocks * capacity, 3 * face_cells)[recv_slot]]
    pallas_call x0 -> x1, Pallas kernels: none -> 22.1 us  [cell_step(): pl.pallas_call(cell_kernel, grid=(bricks // GROUP,), in_specs=[pl.BlockSp...]
    all_to_all x0 -> x1, blocking collectives: none -> 21 us  [body(): lax.all_to_all(shares.reshape(devices, own_cells), ('blk', 'par'), split_...]
    broadcast_in_dim x6 -> x2, local copies, waits for them, and re-layouts: 16.6 us -> 0.09 us  [the longest x1 0.09 us: body(): theta[:, None]]
    reduce_sum x1, other arithmetic: 13.7 us -> 1.04 us  [body(): brick_part = jnp.sum(parts_out, axis=(1, 2))]
    add x2 -> x1, other arithmetic: 11.1 us -> 0.01 us  [expanders(): cells - edge + k]
    mul x3 -> x2, other arithmetic: 9.15 us -> 0.1 us  [the longest x1 0.09 us: body(): tissue_faces * factor_faces]
    all_to_all x1 -> x0, starting transfers between devices: 8.38 us -> none  [body(): lax.all_to_all(shares.reshape(devices, own_cells), ('blk', 'par'), split_...]
  transfers between devices with their start and end apart: 5 -> 4, of which waited for: 2 -> 1; matrix products, arithmetic and copies ran while one was open for 35% -> 26% of each run, Pallas kernels for 0% -> 0%
where the time goes in v2:
time: 137 us
  starting transfers between devices  33.5 us (24%)
  local copies, waits for them, and re-layouts  29.7 us (22%)
  Pallas kernels  22.1 us (16%)
  blocking collectives  21 us (15%)
  waiting for transfers between devices  14.7 us (11%)
  other arithmetic  14.6 us (11%)
    pallas_call x1, Pallas kernels, cell_step(): pl.pallas_call(cell_kernel, grid=(bricks // GROUP,), in_specs=[pl.BlockSp...  22.1 us
    all_to_all x1, blocking collectives, body(): lax.all_to_all(shares.reshape(devices, own_cells), ('blk', 'par'), split_...  21 us
    all_to_all x1, starting transfers between devices, body(): lax.all_to_all(jnp.broadcast_to(row[None], (devices, row.shape[0])), ('bl...  15.6 us
    all_to_all x1, waiting for transfers between devices, body(): lax.all_to_all(outgoing.reshape(blocks, capacity, 3 * face_cells), 'blk',...  14.7 us
    all_to_all x1, starting transfers between devices, body(): lax.all_to_all(outgoing.reshape(blocks, capacity, 3 * face_cells), 'blk',...  11.8 us
    slice x4, local copies, waits for them, and re-layouts, layers(): values[..., brick_edge - 1::brick_edge]  6.01 us
    slice x4, local copies, waits for them, and re-layouts, layers(): values[..., 0::brick_edge]  5.92 us
    ppermute x1, starting transfers between devices, body(): lax.ppermute(last, 'par', up)  4.79 us
  transfers between devices with their start and end apart: 4, of which 1 were waited for; matrix products, arithmetic and copies ran while one was open for 26% of the time, Pallas kernels for 0%

profile of v2, /device:TPU:1, one launch (start us, length us, event | category | flops | bytes accessed | tf_op | source)
XLA Modules:
  0.0 136.9 jit_solution(7618366261299899907)
XLA Ops:
  0.6 1.2 compare_select_fusion.5
  1.9 0.7 pad_maximum_fusion.4
  2.6 0.7 broadcast_in_dim.20
  3.3 15.6 %all-to-all-start = ((f32[256,1,34]{2,1,0:T(1,128)}), f32[256,1,34]{2,1,0:T(1,128)S(1)}, u32[]{:S(2)}, u32[]{:S(2)}) async-start(f32[256,1,34]{2,1,0:T(1,128)} %broadcast_in_dim.20), calls=%async_computation | async-start | bytes 262144 | tf_op jit(solution)/shard_map/all_to_all | solution.py:222
  19.0 1.8 %slice_convert_fusion.1 = (f32[32,1,1024]{2,1,0:T(1,128)S(1)}, f32[32,1,1024]{2,1,0:T(1,128)S(1)}) fusion(s32[32,8,1024]{2,1,0:T(8,128)} %tissue_ref.1), kind=kLoop, calls=%fused_computation.28 | loop fusion | flops 65536 | bytes 524288 | tf_op jit(solution)/shard_map/convert_element_type | solution.py:267
  20.8 2.6 %fusion.13 = (f32[32,1,1024]{2,1,0:T(1,128)S(1)}, f32[32,1,1024]{2,1,0:T(1,128)S(1)}, f32[32,1,1024]{2,1,0:T(1,128)S(1)}, f32[32,1,1024]{2,1,0:T(1,128)S(1)}) fusion(f32[32,8,1024]{2,1,0:T(8,128)} %u_ref.1, bf16[32,8,1024]{2,1,0:T(8,128)(2,1)} %l_ref.1), kind=kLoop, calls=%fused_computation.80 | loop fusion | bytes 1048576 | tf_op jit(solution)/shard_map/slice | solution.py:267
  23.4 1.1 pad_maximum_fusion.3
  24.6 1.3 collective-permute-start.1
  25.9 1.2 pad_maximum_fusion.2
  27.0 4.8 %collective-permute-start = (f32[32,3,1024]{2,1,0:T(4,128)}, f32[32,3,1024]{2,1,0:T(4,128)}, u32[]{:S(2)}, u32[]{:S(2)}) collective-permute-start(f32[32,3,1024]{2,1,0:T(4,128)} %pad_maximum_fusion.2), channel_id=1, source_target_pairs={{0,1},{1,2},{2,3},{4,5},{5,6},{6,7},{8,9},{9,10},{10,11},{12,13},{... | collective-permute-start | bytes 1179656 | tf_op jit(solution)/shard_map/ppermute | solution.py:269
  31.8 1.4 slice.86
  33.2 1.4 %slice.87 = bf16[32,8,32]{2,1,0:T(8,128)(2,1)} slice(bf16[32,8,1024]{2,1,0:T(8,128)(2,1)S(1)} %copy-done.4), slice={[0:32:1], [0:8:1], [31:1024:32]} | slice | bytes 32768 | tf_op jit(solution)/shard_map/slice | solution.py:38
  34.5 1.3 slice.92
  35.9 1.3 slice.93
  37.2 1.9 %slice.82 = s32[32,8,32]{2,1,0:T(8,128)} slice(s32[32,8,1024]{2,1,0:T(8,128)S(1)} %copy-done.2), slice={[0:32:1], [0:8:1], [0:1024:32]} | slice | bytes 65536 | tf_op jit(solution)/shard_map/slice | solution.py:37
  39.1 1.9 %slice.83 = s32[32,8,32]{2,1,0:T(8,128)} slice(s32[32,8,1024]{2,1,0:T(8,128)S(1)} %copy-done.2), slice={[0:32:1], [0:8:1], [31:1024:32]} | slice | bytes 65536 | tf_op jit(solution)/shard_map/slice | solution.py:38
  41.1 1.4 slice.96
  42.4 1.4 slice.97
  43.8 0.7 slice_bitcast_fusion.7
  44.5 0.8 slice_bitcast_fusion.3
  45.3 0.8 slice_bitcast_fusion.5
  46.0 0.1 convert_element_type.49
  46.2 0.1 copy.22
  46.3 0.1 reshape.497
  46.4 1.1 gather_fusion.1
  47.6 0.1 gather.25
  47.8 0.1 add.166
  47.9 1.7 %cosine_multiply_fusion = f32[32,4,8,32]{3,2,0,1:T(8,128)S(1)} fusion(bf16[32,1,8,32]{3,2,0,1:T(8,128)(2,1)S(1)} %bitcast.79, bf16[32,1,8,32]{3,2,0,1:T(8,128)(2,1)S(1)} %bitcast.78, bf16[32,1,8,32]{3,2,0,1:T(8,128)(2,1)S(1)} %copy-done.16, bf16[32,1,8,32]{3,2,0,1:T(8,128)(2,1)S(1)} %copy-done.15), kind=kLoop, calls=%fused_computation.14 | loop fusion | flops 294912 | bytes 196608 | tf_op jit(solution)/shard_map/integer_pow | solution.py:244
  49.8 0.1 slice_bitcast_fusion.1
  49.9 0.1 fusion
  50.0 0.5 copy-done.5
  50.8 0.1 pad_maximum_fusion
  51.0 0.2 copy.24
  51.2 0.4 reshape.531
  51.6 0.2 convert_reduce_fusion
  51.8 1.2 scatter_custom_fusion
  53.0 1.1 reshape.484
  54.1 11.8 %all-to-all-start.1 = ((f32[64,4,768]{2,1,0:T(4,128)}), f32[64,4,768]{2,1,0:T(4,128)S(1)}, u32[]{:S(2)}, u32[]{:S(2)}) async-start(f32[64,4,768]{2,1,0:T(4,128)} %reshape.484), calls=%async_computation.1 | async-start | bytes 1572864 | tf_op jit(solution)/shard_map/all_to_all | solution.py:257
  65.9 0.1 reshape.505
  66.1 0.1 iota_compare_fusion.2
  66.2 0.1 iota_compare_fusion
  66.3 0.9 add_convert_fusion.1.expand_ref
  67.2 0.1 slice.79
  67.4 1.1 gather_fusion.2
  68.5 0.1 gather.27
  68.6 0.1 reshape.482
  68.8 0.7 gather_fusion
  69.5 0.1 copy.23
  69.6 0.1 reshape.513
  69.7 1.3 gather_fusion.3
  71.0 0.1 reshape.512
  71.1 0.7 maximum_maximum_fusion.scale_ref
  71.8 2.4 %pad_maximum_fusion.1.halo_ref = f32[32,6,1024]{2,1,0:T(8,128)} fusion(f32[32,3,1024]{2,1,0:T(4,128)} %collective-permute-done.1, f32[32,3,1024]{2,1,0:T(4,128)} %collective-permute-done), kind=kLoop, calls=%fused_computation.7 | loop fusion | flops 196608 | bytes 1572864 | tf_op jit(solution)/shard_map/concatenate | solution.py:269
  74.2 14.7 %all-to-all-done.1 = f32[64,4,768]{2,1,0:T(4,128)S(1)} async-done(((f32[64,4,768]{2,1,0:T(4,128)}), f32[64,4,768]{2,1,0:T(4,128)S(1)}, u32[]{:S(2)}, u32[]{:S(2)}) %all-to-all-start.1) | async-done | bytes 786464 | tf_op jit(solution)/shard_map/all_to_all | solution.py:257
  88.9 0.3 reshape.485
  89.2 0.8 gather_fusion.4
  90.0 1.7 %reshape.486.face_ref = f32[32,4,24,32]{3,2,1,0:T(8,128)} reshape(f32[128,768]{1,0:T(8,128)S(1)} %gather_fusion.4) | data formatting | bytes 786432 | tf_op jit(solution)/shard_map/reshape | solution.py:260
  91.7 22.1 %shard_map.112 = (f32[32,8,1024]{2,1,0:T(8,128)}, f32[32,8,1024]{2,1,0:T(8,128)}, f32[32,1,128]{2,1,0:T(1,128)}) custom-call(f32[32,8]{1,0:T(8,128)} %maximum_maximum_fusion.scale_ref, f32[4,32,1024]{2,1,0:T(8,128)} %add_convert_fusion.1.expand_ref, s32[32,8,1024]{2,1,0:T(8,128)} %tissue_ref.1, bf16[32,8,1024]{2,1,0:T(8,128)(2,1)} %angle_ref.1, ...), custom_call_target="tpu_custom_call" | custom-call | tf_op jit(solution)/shard_map/pallas_call | solution.py:185
  113.8 1.0 reduce_sum.53
  114.9 0.1 select_reduce_fusion
  115.0 0.1 all_to_all.18
  115.1 21.0 %all_to_all.23 = f32[256,1,2]{2,1,0:T(1,128)S(1)} all-to-all(f32[256,1,2]{2,1,0:T(1,128)S(1)} %bitcast.77), channel_id=1, replica_groups=mesh['blk'=64,'par'=4] {'blk','par'}, dimensions={0} | all-to-all | bytes 4096 | tf_op jit(solution)/shard_map/all_to_all | solution.py:283
  136.1 0.3 reduce_sum.55
  136.4 0.5 multiply_divide_fusion
  (66 shorter events, 0.7 us)
Async XLA Ops:
  0.6 45.8 %copy-start = (s32[2048]{0:T(1024)S(1)}, s32[2048]{0:T(1024)}, u32[]{:S(2)}) copy-start(s32[2048]{0:T(1024)} %param.14) | copy-start | bytes 24580
  3.3 50.8 %all-to-all-start = ((f32[256,1,34]{2,1,0:T(1,128)}), f32[256,1,34]{2,1,0:T(1,128)S(1)}, u32[]{:S(2)}, u32[]{:S(2)}) async-start(f32[256,1,34]{2,1,0:T(1,128)} %broadcast_in_dim.20), calls=%async_computation | async-start | bytes 262144 | tf_op jit(solution)/shard_map/all_to_all | solution.py:222
  20.8 11.0 %copy-start.4 = (bf16[32,8,1024]{2,1,0:T(8,128)(2,1)S(1)}, bf16[32,8,1024]{2,1,0:T(8,128)(2,1)}, u32[]{:S(2)}) copy-start(bf16[32,8,1024]{2,1,0:T(8,128)(2,1)} %angle_ref.1) | copy-start | bytes 1572868
  20.8 13.7 %copy-start.3 = (f32[32,8,1024]{2,1,0:T(8,128)S(1)}, f32[32,8,1024]{2,1,0:T(8,128)}, u32[]{:S(2)}) copy-start(f32[32,8,1024]{2,1,0:T(8,128)} %u_ref.1) | copy-start | bytes 3145732
  23.4 13.8 %copy-start.2 = (s32[32,8,1024]{2,1,0:T(8,128)S(1)}, s32[32,8,1024]{2,1,0:T(8,128)}, u32[]{:S(2)}) copy-start(s32[32,8,1024]{2,1,0:T(8,128)} %tissue_ref.1) | copy-start | bytes 3145732
  23.4 17.6 %copy-start.1 = (bf16[32,8,1024]{2,1,0:T(8,128)(2,1)S(1)}, bf16[32,8,1024]{2,1,0:T(8,128)(2,1)}, u32[]{:S(2)}) copy-start(bf16[32,8,1024]{2,1,0:T(8,128)(2,1)} %l_ref.1) | copy-start | bytes 1572868
  24.6 47.2 %collective-permute-start.1 = (f32[32,3,1024]{2,1,0:T(4,128)}, f32[32,3,1024]{2,1,0:T(4,128)}, u32[]{:S(2)}, u32[]{:S(2)}) collective-permute-start(f32[32,3,1024]{2,1,0:T(4,128)} %pad_maximum_fusion.3), channel_id=1, source_target_pairs={{1,0},{2,1},{3,2},{5,4},{6,5},{7,6},{9,8},{10,9},{11,10},{13,12},{... | collective-permute-start | bytes 1179656 | tf_op jit(solution)/shard_map/ppermute | solution.py:269
  27.0 44.8 %collective-permute-start = (f32[32,3,1024]{2,1,0:T(4,128)}, f32[32,3,1024]{2,1,0:T(4,128)}, u32[]{:S(2)}, u32[]{:S(2)}) collective-permute-start(f32[32,3,1024]{2,1,0:T(4,128)} %pad_maximum_fusion.2), channel_id=1, source_target_pairs={{0,1},{1,2},{2,3},{4,5},{5,6},{6,7},{8,9},{9,10},{10,11},{12,13},{... | collective-permute-start | bytes 1179656 | tf_op jit(solution)/shard_map/ppermute | solution.py:269
  42.4 3.7 %copy-start.17 = (s32[32,4]{0,1:T(4,128)S(1)}, s32[32,4]{0,1:T(4,128)}, u32[]{:S(2)}) copy-start(s32[32,4]{0,1:T(4,128)} %param.15) | copy-start | bytes 1540
  43.8 2.4 %copy-start.19 = (s32[32]{0:T(128)S(1)}, s32[32]{0:T(128)}, u32[]{:S(2)}) copy-start(s32[32]{0:T(128)} %get-tuple-element.31) | copy-start | bytes 388
  46.4 1.4 copy-start.18
  46.4 1.5 %copy-start.13 = (bf16[32,8,32]{2,1,0:T(8,128)(2,1)S(1)}, bf16[32,8,32]{2,1,0:T(8,128)(2,1)}, u32[]{:S(2)}) copy-start(bf16[32,8,32]{2,1,0:T(8,128)(2,1)} %slice.86) | copy-start | bytes 49156
  46.4 1.5 %copy-start.14 = (bf16[32,8,32]{2,1,0:T(8,128)(2,1)S(1)}, bf16[32,8,32]{2,1,0:T(8,128)(2,1)}, u32[]{:S(2)}) copy-start(bf16[32,8,32]{2,1,0:T(8,128)(2,1)} %slice.87) | copy-start | bytes 49156
  46.4 1.5 %copy-start.15 = (bf16[32,1,8,32]{3,2,0,1:T(8,128)(2,1)S(1)}, bf16[32,1,8,32]{3,2,0,1:T(8,128)(2,1)}, u32[]{:S(2)}) copy-start(bf16[32,1,8,32]{3,2,0,1:T(8,128)(2,1)} %get-tuple-element.25) | copy-start | bytes 49156
  46.4 1.5 %copy-start.16 = (bf16[32,1,8,32]{3,2,0,1:T(8,128)(2,1)S(1)}, bf16[32,1,8,32]{3,2,0,1:T(8,128)(2,1)}, u32[]{:S(2)}) copy-start(bf16[32,1,8,32]{3,2,0,1:T(8,128)(2,1)} %get-tuple-element.26) | copy-start | bytes 49156
  47.6 2.3 %copy-start.7 = (s32[32,8,32]{2,1,0:T(8,128)S(1)}, s32[32,8,32]{2,1,0:T(8,128)}, u32[]{:S(2)}) copy-start(s32[32,8,32]{2,1,0:T(8,128)} %slice.82) | copy-start | bytes 98308
  47.6 2.3 %copy-start.8 = (s32[32,8,32]{2,1,0:T(8,128)S(1)}, s32[32,8,32]{2,1,0:T(8,128)}, u32[]{:S(2)}) copy-start(s32[32,8,32]{2,1,0:T(8,128)} %slice.83) | copy-start | bytes 98308
  47.6 2.3 %copy-start.11 = (s32[32,1,1,8,32]{4,3,0,1,2:T(8,128)S(1)}, s32[32,1,1,8,32]{4,3,0,1,2:T(8,128)}, u32[]{:S(2)}) copy-start(s32[32,1,1,8,32]{4,3,0,1,2:T(8,128)} %get-tuple-element.15) | copy-start | bytes 98308
  47.6 2.3 %copy-start.12 = (s32[32,1,1,8,32]{4,3,0,1,2:T(8,128)S(1)}, s32[32,1,1,8,32]{4,3,0,1,2:T(8,128)}, u32[]{:S(2)}) copy-start(s32[32,1,1,8,32]{4,3,0,1,2:T(8,128)} %get-tuple-element.16) | copy-start | bytes 98308
  49.7 0.9 copy-start.5
  49.7 1.0 copy-start.6
  49.7 1.0 copy-start.9
  49.7 1.1 copy-start.10
  54.1 34.8 %all-to-all-start.1 = ((f32[64,4,768]{2,1,0:T(4,128)}), f32[64,4,768]{2,1,0:T(4,128)S(1)}, u32[]{:S(2)}, u32[]{:S(2)}) async-start(f32[64,4,768]{2,1,0:T(4,128)} %reshape.484), calls=%async_computation.1 | async-start | bytes 1572864 | tf_op jit(solution)/shard_map/all_to_all | solution.py:257
  91.7 23.2 %copy-start.20 = (s32[32]{0:T(128)S(1)}, s32[32]{0:T(128)}, u32[]{:S(2)}) copy-start(s32[32]{0:T(128)} %param.16) | copy-start | bytes 388
  91.7 44.7 %copy-start.21 = (f32[2]{0:T(128)S(1)}, f32[2]{0:T(128)}, u32[]{:S(2)}) copy-start(f32[2]{0:T(128)} %param.13) | copy-start | bytes 28

commit v3 on v2

--- a/solution.py
+++ b/solution.py
@@ -113,7 +113,7 @@
     k = jnp.arange(edge, dtype=jnp.int32)[:, None]
     return jnp.stack(
         [lane == k, lane == cells - edge + k, lane == edge * k, lane == edge * k + edge - 1]
-    ).astype(jnp.float32)
+    )
 
 
 def cell_kernel(scale_ref, expand_ref, tissue_ref, angle_ref, u_ref, l_ref, face_ref, halo_ref,
@@ -144,13 +144,19 @@
         halo = halo_ref[i]
         conds, ub, lb = [], [], []
         for f in range(4):
-            ext = jnp.dot(face_ref[i, f], expand_ref[f], precision=lax.Precision.HIGHEST,
-                          preferred_element_type=jnp.float32)
+            face = face_ref[i, f]
+            high = face.astype(jnp.bfloat16)
+            rest = face - high.astype(jnp.float32)
+            middle = rest.astype(jnp.bfloat16)
+            low = (rest - middle.astype(jnp.float32)).astype(jnp.bfloat16)
+            ext = jnp.dot(high, expand_ref[f], preferred_element_type=jnp.float32)
+            ext = ext + jnp.dot(middle, expand_ref[f], preferred_element_type=jnp.float32)
+            ext = ext + jnp.dot(low, expand_ref[f], preferred_element_type=jnp.float32)
             w_self = wx if f < 2 else wy
             w_near = jnp.where(masks[f], scale_ref[b, 1 + f] * ext[:nz], pltpu.roll(w_self, shifts[f], 1))
             conds.append(w_self * w_near)
             ub.append(jnp.where(masks[f], ext[nz:2 * nz], pltpu.roll(u, shifts[f], 1)))
-            lb.append(jnp.where(masks[f], ext[2 * nz:], pltpu.roll(l, shifts[f], 1)))
+            lb.append(jnp.where(masks[f], ext[2 * nz:3 * nz], pltpu.roll(l, shifts[f], 1)))
         wz_lo = jnp.where(zlo, (halo[0:1] * th) * VERTICAL, pltpu.roll(wz, 1, 0))
         wz_hi = jnp.where(zhi, (halo[3:4] * th) * VERTICAL, pltpu.roll(wz, nz - 1, 0))
         conds += [wz * wz_lo, wz * wz_hi]
@@ -158,16 +164,18 @@
         lb += [jnp.where(zlo, halo[2:3], pltpu.roll(l, 1, 0)), jnp.where(zhi, halo[5:6], pltpu.roll(l, nz - 1, 0))]
         lap_u = conds[0] * (ub[0] - u)
         lap_l = conds[0] * (lb[0] - l)
-        terms = -conds[0] * (l - lb[0]) * (u - ub[0])
+        terms = lap_l * (ub[0] - u)
         for k in range(1, 6):
-            lap_u = lap_u + conds[k] * (ub[k] - u)
-            lap_l = lap_l + conds[k] * (lb[k] - l)
-            terms = terms - conds[k] * (l - lb[k]) * (u - ub[k])
+            step_u = ub[k] - u
+            step_l = conds[k] * (lb[k] - l)
+            lap_u = lap_u + conds[k] * step_u
+            lap_l = lap_l + step_l
+            terms = terms + step_l * step_u
         ionic = u * (1.0 - u) * (u - THRESHOLD)
         slope = -3.0 * u * u + 2.0 * (1.0 + THRESHOLD) * u - THRESHOLD
         u_out[i] = u + TIMESTEP * (lap_u + ionic)
         l_out[i] = l + TIMESTEP * (lap_l + slope * l)
-        col = jnp.sum(terms, axis=0, keepdims=True)
+        col = -jnp.sum(terms, axis=0, keepdims=True)
         acc = col[:, 0:128]
         for t in range(1, cells // 128):
             acc = acc + col[:, t * 128:(t + 1) * 128]
@@ -180,7 +188,7 @@
 def cell_step(scales, tissue, angle, potential, sensitivity, faces, halos, interpret=False):
     bricks, nz, cells = potential.shape
     edge = faces.shape[-1]
-    expand = expanders(edge, cells)
+    expand = expanders(edge, cells).astype(jnp.bfloat16)
     blk3 = lambda: pl.BlockSpec((GROUP, nz, cells), lambda g: (g, 0, 0))
     return pl.pallas_call(
         cell_kernel,
@@ -189,7 +197,7 @@
             pl.BlockSpec(memory_space=pltpu.SMEM),
             pl.BlockSpec((4, edge, cells), lambda g: (0, 0, 0)),
             blk3(), blk3(), blk3(), blk3(),
-            pl.BlockSpec((GROUP, 4, 3 * nz, edge), lambda g: (g, 0, 0, 0)),
+            pl.BlockSpec((GROUP, 4, faces.shape[2], edge), lambda g: (g, 0, 0, 0)),
             pl.BlockSpec((GROUP, 6, cells), lambda g: (g, 0, 0)),
         ],
         out_specs=[blk3(), blk3(), pl.BlockSpec((GROUP, 1, 128), lambda g: (g, 0, 0))],
@@ -218,17 +226,6 @@
     cell_count = own_cells * devices
     opposite = jnp.array([1, 0, 3, 2], jnp.int32)
 
-    row = jnp.concatenate([conductance, brick_cell.astype(jnp.float32)])
-    table = lax.all_to_all(
-        jnp.broadcast_to(row[None], (devices, row.shape[0])),
-        ("blk", "par"),
-        split_axis=0,
-        concat_axis=0,
-        tiled=True,
-    )
-    cond_all = table[:, :own_cells].reshape(-1)
-    cell_all = table[::parts, own_cells:].reshape(-1).astype(jnp.int32)
-
     near_slot = brick_slot[neighbours]
     near_blk = (near_slot // bricks).reshape(-1)
     far_key = (near_slot % bricks * 4 + opposite[None, :]).reshape(-1)
@@ -240,8 +237,18 @@
     recv_slot = near_blk * capacity + recv_rank
 
     adjoint = sensitivity.astype(jnp.float32)
-    tissue_faces = layers(tissue, brick_edge).astype(jnp.float32)
-    cos_faces = jnp.cos(layers(fiber_angle, brick_edge).astype(jnp.float32)) ** 2
+    picker = expanders(brick_edge, plane_cells).reshape(4 * brick_edge, plane_cells).T.astype(jnp.float32)
+
+    def boundary(values):
+        picked = jnp.dot(
+            values.astype(jnp.float32).reshape(bricks * z_layers, plane_cells),
+            picker,
+            precision=lax.Precision.HIGHEST,
+        )
+        return picked.reshape(bricks, z_layers, 4, brick_edge).transpose(0, 2, 1, 3)
+
+    tissue_faces = boundary(tissue)
+    cos_faces = jnp.cos(boundary(fiber_angle)) ** 2
     factor_faces = jnp.concatenate(
         [
             ACROSS + (ALONG - ACROSS) * cos_faces[:, :2],
@@ -250,16 +257,31 @@
         axis=1,
     )
     fields = jnp.stack(
-        [tissue_faces * factor_faces, layers(potential, brick_edge), layers(adjoint, brick_edge)], axis=2
+        [tissue_faces * factor_faces, boundary(potential), boundary(sensitivity)], axis=2
     )
     flattened = fields.reshape(face_count, 3 * face_cells)
     outgoing = jnp.zeros((blocks * capacity, 3 * face_cells), jnp.float32).at[send_slot].set(flattened)
-    received = lax.all_to_all(
-        outgoing.reshape(blocks, capacity, 3 * face_cells), "blk", split_axis=0, concat_axis=0, tiled=True
-    )
+    shifted = [conductance] + [
+        lax.ppermute(conductance, "par", [(i, (i + s) % parts) for i in range(parts)])
+        for s in range(1, parts)
+    ]
+    source = (lax.axis_index("par") - jnp.arange(parts, dtype=jnp.int32)) % parts
+    extra = jnp.concatenate([jnp.stack(shifted)[source].reshape(-1), brick_cell.astype(jnp.float32)])
+    width = capacity * 3 * face_cells
+    extra_width = -(-extra.shape[0] // 128) * 128
+    extra = jnp.pad(extra, (0, extra_width - extra.shape[0]))
+    sending = jnp.concatenate(
+        [outgoing.reshape(blocks, width), jnp.broadcast_to(extra[None], (blocks, extra_width))], axis=1
+    )
+    arrived = lax.all_to_all(sending, "blk", split_axis=0, concat_axis=0, tiled=True)
+    received = arrived[:, :width]
+    par_cells = own_cells * parts
+    cond_all = arrived[:, width : width + par_cells].reshape(-1)
+    cell_all = arrived[:, width + par_cells : width + par_cells + bricks].reshape(-1).astype(jnp.int32)
     faces = received.reshape(blocks * capacity, 3 * face_cells)[recv_slot].reshape(
         bricks, 4, 3 * z_layers, brick_edge
     )
+    faces = jnp.pad(faces, ((0, 0), (0, 0), (0, 32 - 3 * z_layers % 32), (0, 0)))
 
     size = lax.axis_size("par")
     up = [(i, i + 1) for i in range(size - 1)]

time: 137 us -> 109 us (0.80)
  local copies, waits for them, and re-layouts: 29.7 us -> 17.1 us
  starting transfers between devices: 33.5 us -> 25 us
  other arithmetic: 14.6 us -> 8.75 us
  Pallas kernels: 22.1 us -> 17 us
  matrix products: 0 us -> 3.59 us
  blocking collectives: 21 us -> 22.9 us
    all_to_all x2 -> x1, starting transfers between devices: 27.4 us -> 13.2 us  [body(): lax.all_to_all(sending, 'blk', split_axis=0, concat_axis=0, tiled=True)]
    slice x9 -> x2, local copies, waits for them, and re-layouts: 12 us -> 0.06 us  [the longest x1 0.05 us: body(): received = arrived[:, :width]]
    all_to_all x2 -> x1, waiting for transfers between devices: 14.7 us -> 3.52 us  [body(): lax.all_to_all(sending, 'blk', split_axis=0, concat_axis=0, tiled=True)]
    ppermute x1, waiting for transfers between devices: 0.01 us -> 8.72 us  [body(): lax.ppermute(initial, 'par', down)]
    ppermute x0 -> x3, starting transfers between devices: none -> 6.32 us  [body(): lax.ppermute(conductance, 'par', [(i, (i + s) % parts) for i in range(par...]
    pallas_call x1, Pallas kernels: 22.1 us -> 17 us  [cell_step(): pl.pallas_call(cell_kernel, grid=(bricks // GROUP,), in_specs=[pl.BlockSp...]
    dot_general x0 -> x4, matrix products: none -> 3.59 us  [boundary(): jnp.dot(values.astype(jnp.float32).reshape(bricks * z_layers, plane_cells...]
    another operation x5 -> x1, local copies, waits for them, and re-layouts: 2.51 us -> 0.1 us  [body(): jnp.stack([tissue_faces * factor_faces, boundary(potential), boundary(sen...]
  transfers between devices with their start and end apart: 4 -> 6, of which waited for: 1 -> 3; matrix products, arithmetic and copies ran while one was open for 26% -> 16% of each run, Pallas kernels for 0% -> 0%
where the time goes in v3:
time: 109 us
  starting transfers between devices  25 us (23%)
  blocking collectives  22.9 us (21%)
  local copies, waits for them, and re-layouts  17.1 us (16%)
  Pallas kernels  17 us (16%)
  waiting for transfers between devices  13.5 us (12%)
  other arithmetic  8.75 us (8%)
  matrix products  3.59 us (3%)
  between operations  1.16 us (1%)
    all_to_all x1, blocking collectives, body(): lax.all_to_all(shares.reshape(devices, own_cells), ('blk', 'par'), split_...  22.9 us
    pallas_call x1, Pallas kernels, cell_step(): pl.pallas_call(cell_kernel, grid=(bricks // GROUP,), in_specs=[pl.BlockSp...  17 us
    all_to_all x1, starting transfers between devices, body(): lax.all_to_all(sending, 'blk', split_axis=0, concat_axis=0, tiled=True)  13.2 us
    ppermute x1, waiting for transfers between devices, body(): lax.ppermute(initial, 'par', down)  8.72 us
    ppermute x3, starting transfers between devices, body(): lax.ppermute(conductance, 'par', [(i, (i + s) % parts) for i in range(par...  6.32 us
    ppermute x1, starting transfers between devices, body(): lax.ppermute(last, 'par', up)  4.2 us
    dot_general x4, matrix products, boundary(): jnp.dot(values.astype(jnp.float32).reshape(bricks * z_layers, plane_cells...  3.59 us
    all_to_all x1, waiting for transfers between devices, body(): lax.all_to_all(sending, 'blk', split_axis=0, concat_axis=0, tiled=True)  3.52 us
  transfers between devices with their start and end apart: 6, of which 3 were waited for; matrix products, arithmetic and copies ran while one was open for 16% of the time, Pallas kernels for 0%

profile of v3, /device:TPU:1, one launch (start us, length us, event | category | flops | bytes accessed | tf_op | source)
XLA Modules:
  0.0 109.0 jit_solution(643218543373118350)
XLA Ops:
  0.7 3.6 %collective-permute-start.1 = (f32[2]{0:T(128)}, f32[2]{0:T(128)S(1)}, u32[]{:S(2)}, u32[]{:S(2)}) collective-permute-start(f32[2]{0:T(128)} %param.13), channel_id=1, source_target_pairs={{0,2},{1,3},{2,0},{3,1},{4,6},{5,7},{6,4},{7,5},{8,10},{9,11},{10,... | collective-permute-start | bytes 32 | tf_op jit(solution)/shard_map/ppermute | solution.py:265
  4.3 0.3 collective-permute-start
  4.6 2.4 %collective-permute-start.2 = (f32[2]{0:T(128)}, f32[2]{0:T(128)S(1)}, u32[]{:S(2)}, u32[]{:S(2)}) collective-permute-start(f32[2]{0:T(128)} %param.13), channel_id=1, source_target_pairs={{0,3},{1,0},{2,1},{3,2},{4,7},{5,4},{6,5},{7,6},{8,11},{9,8},{10,9... | collective-permute-start | bytes 32 | tf_op jit(solution)/shard_map/ppermute | solution.py:265
  7.0 0.7 compare_select_fusion.4
  7.8 0.7 compare_select_fusion.2
  8.5 0.1 reshape.486
  8.6 0.7 add.192
  9.3 0.1 add.193
  9.4 0.1 iota_compare_fusion.2
  9.5 0.1 iota_compare_fusion
  9.6 0.8 fusion.21
  10.4 1.4 %convolution_bitcast_fusion = f32[256,128]{0,1:T(8,128)S(1)} fusion(pred[128,1024]{1,0:T(32,128)(4,1)S(1)} %bitcast.83, bf16[32,8,1024]{2,1,0:T(8,128)(2,1)} %l_ref.1), kind=kOutput, calls=%fused_computation.8 | convolution fusion | flops 67108864 | bytes 786432 | tf_op jit(solution)/shard_map/dot_general | solution.py:243
  12.0 0.7 convolution_bitcast_fusion.1
  12.7 0.1 copy.33
  12.8 0.7 fusion.1
  13.5 0.7 convolution_bitcast_fusion.2
  14.4 0.1 copy.32
  14.5 0.3 integer_pow.14
  14.7 0.4 fusion.12
  15.1 0.3 reshape.472
  15.4 0.3 reshape.475
  15.7 0.3 reshape.477
  15.9 0.3 fusion.5
  16.3 0.4 pad_maximum_fusion
  16.7 0.1 copy.35
  16.8 0.4 reshape.536
  17.2 1.1 %gather_fusion = s32[128]{0:T(128)S(1)} fusion(s32[2048]{0:T(1024)S(1)} %copy-done, s32[1024]{0:T(1024)S(1)} %pad_clamp_fusion.5), kind=kCustom, calls=%fused_computation | custom fusion | bytes 1536 | tf_op jit(solution)/shard_map/gather | solution.py:229
  18.4 0.2 convert_reduce_fusion
  18.6 1.2 %scatter_custom_fusion = f32[256,768]{1,0:T(8,128)S(1)} fusion(s32[128]{0:T(128)S(1)} %get-tuple-element.22, f32[128,768]{1,0:T(8,128)S(1)} %reshape.536, f32[]{:T(128)} %constant.33.clone.1), kind=kCustom, calls=%fused_computation.27 | custom fusion | bytes 786436 | tf_op jit(solution)/shard_map/scatter | solution.py:263
  19.8 0.2 reshape.479
  20.1 0.6 gather_fusion.1
  20.9 1.5 %all_to_all.14 = f32[64,1,3200]{2,1,0:T(1,128)} reshape(f32[64,3200]{1,0:T(8,128)S(1)} %pad_maximum_fusion.2) | data formatting | bytes 1638400 | tf_op jit(solution)/shard_map/all_to_all | solution.py:276
  22.4 13.2 %all-to-all-start = ((f32[64,1,3200]{2,1,0:T(1,128)}), f32[64,1,3200]{2,1,0:T(1,128)S(1)}, u32[]{:S(2)}, u32[]{:S(2)}) async-start(f32[64,1,3200]{2,1,0:T(1,128)} %all_to_all.14), calls=%async_computation | async-start | bytes 1638400 | tf_op jit(solution)/shard_map/all_to_all | solution.py:276
  35.6 0.2 slice_convert_fusion.1
  35.7 2.2 %fusion.22 = (f32[32,1,1024]{2,1,0:T(1,128)S(1)}, f32[32,1,1024]{2,1,0:T(1,128)S(1)}, f32[32,1,1024]{2,1,0:T(1,128)S(1)}, f32[32,1,1024]{2,1,0:T(1,128)S(1)}) fusion(f32[32,8,1024]{2,1,0:T(8,128)} %u_ref.1, bf16[32,8,1024]{2,1,0:T(8,128)(2,1)S(1)} %copy-done.3), kind=kLoop, calls=%fused_computation.93 | loop fusion | bytes 1048576 | tf_op jit(solution)/shard_map/slice | solution.py:289
  37.9 0.3 pad_maximum_fusion.4
  38.3 1.3 %collective-permute-start.4 = (f32[32,3,1024]{2,1,0:T(4,128)S(1)}, f32[32,3,1024]{2,1,0:T(4,128)S(1)}, u32[]{:S(2)}, u32[]{:S(2)}) collective-permute-start(f32[32,3,1024]{2,1,0:T(4,128)S(1)} %pad_maximum_fusion.4), channel_id=1, source_target_pairs={{1,0},{2,1},{3,2},{5,4},{6,5},{7,6},{9,8},{10,9},{11,10},{13,12},{... | collective-permute-start | bytes 1179656 | tf_op jit(solution)/shard_map/ppermute | solution.py:291
  39.6 0.3 pad_maximum_fusion.3
  39.9 4.2 %collective-permute-start.3 = (f32[32,3,1024]{2,1,0:T(4,128)S(1)}, f32[32,3,1024]{2,1,0:T(4,128)S(1)}, u32[]{:S(2)}, u32[]{:S(2)}) collective-permute-start(f32[32,3,1024]{2,1,0:T(4,128)S(1)} %pad_maximum_fusion.3), channel_id=1, source_target_pairs={{0,1},{1,2},{2,3},{4,5},{5,6},{6,7},{8,9},{9,10},{10,11},{12,13},{... | collective-permute-start | bytes 1179656 | tf_op jit(solution)/shard_map/ppermute | solution.py:291
  44.2 0.1 gather.31
  44.4 0.1 reshape.510
  44.5 8.7 %collective-permute-done.4 = f32[32,3,1024]{2,1,0:T(4,128)S(1)} collective-permute-done((f32[32,3,1024]{2,1,0:T(4,128)S(1)}, f32[32,3,1024]{2,1,0:T(4,128)S(1)}, u32[]{:S(2)}, u32[]{:S(2)}) %collective-permute-start.4) | collective-permute-done | bytes 393248 | tf_op jit(solution)/shard_map/ppermute | solution.py:291
  53.2 1.3 %collective-permute-done.3 = f32[32,3,1024]{2,1,0:T(4,128)S(1)} collective-permute-done((f32[32,3,1024]{2,1,0:T(4,128)S(1)}, f32[32,3,1024]{2,1,0:T(4,128)S(1)}, u32[]{:S(2)}, u32[]{:S(2)}) %collective-permute-start.3) | collective-permute-done | bytes 393248 | tf_op jit(solution)/shard_map/ppermute | solution.py:291
  54.5 1.2 %pad_maximum_fusion.1.halo_ref = f32[32,6,1024]{2,1,0:T(8,128)} fusion(f32[32,3,1024]{2,1,0:T(4,128)S(1)} %collective-permute-done.4, f32[32,3,1024]{2,1,0:T(4,128)S(1)} %collective-permute-done.3), kind=kLoop, calls=%fused_computation.14 | loop fusion | flops 196608 | bytes 1572864 | tf_op jit(solution)/shard_map/concatenate | solution.py:291
  55.7 3.5 %all-to-all-done = f32[64,1,3200]{2,1,0:T(1,128)S(1)} async-done(((f32[64,1,3200]{2,1,0:T(1,128)}), f32[64,1,3200]{2,1,0:T(1,128)S(1)}, u32[]{:S(2)}, u32[]{:S(2)}) %all-to-all-start) | async-done | bytes 819232 | tf_op jit(solution)/shard_map/all_to_all | solution.py:276
  59.5 1.1 %gather_fusion.3 = s32[128]{0:T(128)S(1)} fusion(s32[2048]{0:T(1024)S(1)} %convert_element_type.43, s32[1024]{0:T(1024)S(1)} %pad_clamp_fusion.2), kind=kCustom, calls=%fused_computation.3 | custom fusion | bytes 1536 | tf_op jit(solution)/shard_map/gather | solution.py:294
  60.7 0.1 gather.33
  60.8 0.1 reshape.518
  60.9 0.1 reshape.481
  61.0 1.3 %gather_fusion.4 = f32[128]{0:T(128)S(1)} fusion(f32[512]{0:T(512)S(1)} %reshape.481, s32[1024]{0:T(1024)S(1)} %pad_clamp_fusion.1), kind=kCustom, calls=%fused_computation.4 | custom fusion | bytes 1536 | tf_op jit(solution)/shard_map/gather | solution.py:294
  62.3 0.7 gather_fusion.2
  63.0 0.2 reshape.482
  63.3 0.1 reshape.517
  63.4 0.8 gather_fusion.5
  64.2 0.5 reshape.483
  64.7 1.6 %pad.9.face_ref = f32[32,4,32,32]{3,2,1,0:T(8,128)} pad(f32[32,4,24,32]{3,2,1,0:T(8,128)S(1)} %reshape.483, f32[]{:T(128)} %constant.33.clone.1), padding=0_0x0_0x0_8x0_0 | pad | bytes 917508 | tf_op jit(solution)/shard_map/jit(_pad)/pad | solution.py:284
  66.3 0.7 maximum_maximum_fusion.scale_ref
  67.0 17.0 %shard_map.112 = (f32[32,8,1024]{2,1,0:T(8,128)}, f32[32,8,1024]{2,1,0:T(8,128)}, f32[32,1,128]{2,1,0:T(1,128)}) custom-call(f32[32,8]{1,0:T(8,128)} %maximum_maximum_fusion.scale_ref, bf16[4,32,1024]{2,1,0:T(8,128)(2,1)} %get-tuple-element.11.expand_ref, s32[32,8,1024]{2,1,0:T(8,128)} %tissue_ref.1, bf16[32,8,1024]{2,1,0:T(8,128)(2,1)} %angle_ref.1, ...), custom_call_target="tpu_custom_call" | custom-call | tf_op jit(solution)/shard_map/pallas_call | solution.py:193
  84.0 1.0 reduce_sum.53
  85.1 0.1 select_reduce_fusion
  85.2 0.1 all_to_all.17
  85.3 22.9 %all_to_all.21 = f32[256,1,2]{2,1,0:T(1,128)S(1)} all-to-all(f32[256,1,2]{2,1,0:T(1,128)S(1)} %bitcast.90), channel_id=1, replica_groups=mesh['blk'=64,'par'=4] {'blk','par'}, dimensions={0} | all-to-all | bytes 4096 | tf_op jit(solution)/shard_map/all_to_all | solution.py:305
  108.2 0.3 reduce_sum.55
  108.5 0.5 multiply_divide_fusion
  (47 shorter events, 1.1 us)
Async XLA Ops:
  0.6 16.6 %copy-start = (s32[2048]{0:T(1024)S(1)}, s32[2048]{0:T(1024)}, u32[]{:S(2)}) copy-start(s32[2048]{0:T(1024)} %param.14) | copy-start | bytes 24580
  0.6 11.3 %copy-start.2 = (f32[32,8,1024]{2,1,0:T(8,128)S(1)}, f32[32,8,1024]{2,1,0:T(8,128)}, u32[]{:S(2)}) copy-start(f32[32,8,1024]{2,1,0:T(8,128)} %u_ref.1) | copy-start | bytes 3145732
  0.7 19.4 %collective-permute-start.1 = (f32[2]{0:T(128)}, f32[2]{0:T(128)S(1)}, u32[]{:S(2)}, u32[]{:S(2)}) collective-permute-start(f32[2]{0:T(128)} %param.13), channel_id=1, source_target_pairs={{0,2},{1,3},{2,0},{3,1},{4,6},{5,7},{6,4},{7,5},{8,10},{9,11},{10,... | collective-permute-start | bytes 32 | tf_op jit(solution)/shard_map/ppermute | solution.py:265
  4.3 15.8 %collective-permute-start = (f32[2]{0:T(128)}, f32[2]{0:T(128)S(1)}, u32[]{:S(2)}, u32[]{:S(2)}) collective-permute-start(f32[2]{0:T(128)} %param.13), channel_id=1, source_target_pairs={{0,1},{1,2},{2,3},{3,0},{4,5},{5,6},{6,7},{7,4},{8,9},{9,10},{10,1... | collective-permute-start | bytes 32 | tf_op jit(solution)/shard_map/ppermute | solution.py:265
  4.6 15.5 %collective-permute-start.2 = (f32[2]{0:T(128)}, f32[2]{0:T(128)S(1)}, u32[]{:S(2)}, u32[]{:S(2)}) collective-permute-start(f32[2]{0:T(128)} %param.13), channel_id=1, source_target_pairs={{0,3},{1,0},{2,1},{3,2},{4,7},{5,4},{6,5},{7,6},{8,11},{9,8},{10,9... | collective-permute-start | bytes 32 | tf_op jit(solution)/shard_map/ppermute | solution.py:265
  9.6 3.2 %copy-start.4 = (bf16[32,8,1024]{2,1,0:T(8,128)(2,1)S(1)}, bf16[32,8,1024]{2,1,0:T(8,128)(2,1)}, u32[]{:S(2)}) copy-start(bf16[32,8,1024]{2,1,0:T(8,128)(2,1)} %angle_ref.1) | copy-start | bytes 1572868
  10.4 3.1 %copy-start.1 = (s32[32,8,1024]{2,1,0:T(8,128)S(1)}, s32[32,8,1024]{2,1,0:T(8,128)}, u32[]{:S(2)}) copy-start(s32[32,8,1024]{2,1,0:T(8,128)} %tissue_ref.1) | copy-start | bytes 3145732
  18.4 1.7 %copy-start.6 = (f32[2]{0:T(128)S(1)}, f32[2]{0:T(128)}, u32[]{:S(2)}) copy-start(f32[2]{0:T(128)} %param.13) | copy-start | bytes 28
  20.9 14.8 %copy-start.3 = (bf16[32,8,1024]{2,1,0:T(8,128)(2,1)S(1)}, bf16[32,8,1024]{2,1,0:T(8,128)(2,1)}, u32[]{:S(2)}) copy-start(bf16[32,8,1024]{2,1,0:T(8,128)(2,1)} %l_ref.1) | copy-start | bytes 1572868
  22.4 36.8 %all-to-all-start = ((f32[64,1,3200]{2,1,0:T(1,128)}), f32[64,1,3200]{2,1,0:T(1,128)S(1)}, u32[]{:S(2)}, u32[]{:S(2)}) async-start(f32[64,1,3200]{2,1,0:T(1,128)} %all_to_all.14), calls=%async_computation | async-start | bytes 1638400 | tf_op jit(solution)/shard_map/all_to_all | solution.py:276
  38.3 14.9 %collective-permute-start.4 = (f32[32,3,1024]{2,1,0:T(4,128)S(1)}, f32[32,3,1024]{2,1,0:T(4,128)S(1)}, u32[]{:S(2)}, u32[]{:S(2)}) collective-permute-start(f32[32,3,1024]{2,1,0:T(4,128)S(1)} %pad_maximum_fusion.4), channel_id=1, source_target_pairs={{1,0},{2,1},{3,2},{5,4},{6,5},{7,6},{9,8},{10,9},{11,10},{13,12},{... | collective-permute-start | bytes 1179656 | tf_op jit(solution)/shard_map/ppermute | solution.py:291
  39.9 14.5 %collective-permute-start.3 = (f32[32,3,1024]{2,1,0:T(4,128)S(1)}, f32[32,3,1024]{2,1,0:T(4,128)S(1)}, u32[]{:S(2)}, u32[]{:S(2)}) collective-permute-start(f32[32,3,1024]{2,1,0:T(4,128)S(1)} %pad_maximum_fusion.3), channel_id=1, source_target_pairs={{0,1},{1,2},{2,3},{4,5},{5,6},{6,7},{8,9},{9,10},{10,11},{12,13},{... | collective-permute-start | bytes 1179656 | tf_op jit(solution)/shard_map/ppermute | solution.py:291
  67.0 18.1 %copy-start.5 = (s32[32]{0:T(128)S(1)}, s32[32]{0:T(128)}, u32[]{:S(2)}) copy-start(s32[32]{0:T(128)} %param.16) | copy-start | bytes 388

commit v4 on v3

--- a/solution.py
+++ b/solution.py
@@ -211,6 +211,157 @@
     )(scales, expand, tissue, angle, potential, sensitivity, faces, halos)
 
 
+def group_sum(values):
+    col = jnp.sum(values, axis=0, keepdims=True)
+    acc = col[:, 0:128]
+    for t in range(1, values.shape[1] // 128):
+        acc = acc + col[:, t * 128:(t + 1) * 128]
+    return acc
+
+
+def inner_kernel(tissue_ref, angle_ref, u_ref, l_ref, lu_out, ll_out, gx_out, gy_out, part_out):
+    nz, cells = u_ref.shape[1], u_ref.shape[2]
+    edge = BX
+    lane = lax.broadcasted_iota(jnp.int32, (nz, cells), 1)
+    row = lax.broadcasted_iota(jnp.int32, (nz, cells), 0)
+    ycoord = lane % edge
+    inside = (lane >= edge, lane < cells - edge, ycoord != 0, ycoord != edge - 1, row != 0, row != nz - 1)
+    shifts = ((edge, 1), (cells - edge, 1), (1, 1), (cells - 1, 1), (1, 0), (nz - 1, 0))
+
+    def one(i, carry):
+        present = tissue_ref[i].astype(jnp.float32)
+        c = jnp.cos(angle_ref[i].astype(jnp.float32))
+        c2 = c * c
+        gx = present * (ACROSS + (ALONG - ACROSS) * c2)
+        gy = present * (ACROSS + (ALONG - ACROSS) * (1.0 - c2))
+        gz = present * VERTICAL
+        u = u_ref[i]
+        l = l_ref[i].astype(jnp.float32)
+        lap_u = jnp.zeros_like(u)
+        lap_l = jnp.zeros_like(u)
+        terms = jnp.zeros_like(u)
+        for k in range(6):
+            g = gx if k < 2 else (gy if k < 4 else gz)
+            shift, axis = shifts[k]
+            conduct = jnp.where(inside[k], g * pltpu.roll(g, shift, axis), 0.0)
+            step_u = pltpu.roll(u, shift, axis) - u
+            step_l = conduct * (pltpu.roll(l, shift, axis) - l)
+            lap_u = lap_u + conduct * step_u
+            lap_l = lap_l + step_l
+            terms = terms + step_l * step_u
+        lu_out[i] = lap_u
+        ll_out[i] = lap_l
+        gx_out[i] = gx
+        gy_out[i] = gy
+        part_out[i] = group_sum(terms)
+        return carry
+
+    lax.fori_loop(0, GROUP, one, 0)
+
+
+def outer_kernel(scale_ref, expand_ref, u_ref, l_ref, lu_ref, ll_ref, gx_ref, gy_ref, inner_ref, face_ref,
+                 halo_ref, u_out, l_out, part_out):
+    g = pl.program_id(0)
+    nz, cells = u_ref.shape[1], u_ref.shape[2]
+    edge = BX
+    lane = lax.broadcasted_iota(jnp.int32, (nz, cells), 1)
+    row = lax.broadcasted_iota(jnp.int32, (nz, cells), 0)
+    ycoord = lane % edge
+    masks = (lane < edge, lane >= cells - edge, ycoord == 0, ycoord == edge - 1)
+
+    def one(i, carry):
+        b = g * GROUP + i
+        th = scale_ref[b, 0]
+        u = u_ref[i]
+        l = l_ref[i].astype(jnp.float32)
+        gx = gx_ref[i]
+        gy = gy_ref[i]
+        halo = halo_ref[i]
+        edge_u, edge_l, edge_t = [], [], []
+        for side, r in ((0, 0), (1, nz - 1)):
+            own_z = (gx[r:r + 1] != 0.0).astype(jnp.float32) * VERTICAL
+            conduct = own_z * (halo[3 * side:3 * side + 1] * VERTICAL)
+            step_u = halo[3 * side + 1:3 * side + 2] - u[r:r + 1]
+            step_l = conduct * (halo[3 * side + 2:3 * side + 3] - l[r:r + 1])
+            edge_u.append(conduct * step_u)
+            edge_l.append(step_l)
+            edge_t.append(step_l * step_u)
+        lap_u = lu_ref[i] + jnp.where(row == 0, edge_u[0], 0.0) + jnp.where(row == nz - 1, edge_u[1], 0.0)
+        lap_l = ll_ref[i] + jnp.where(row == 0, edge_l[0], 0.0) + jnp.where(row == nz - 1, edge_l[1], 0.0)
+        inner = inner_ref[i] + group_sum(edge_t[0]) + group_sum(edge_t[1])
+        face_u = jnp.zeros_like(u)
+        face_l = jnp.zeros_like(u)
+        face_t = jnp.zeros_like(u)
+        for f in range(4):
+            face = face_ref[i, f]
+            high = face.astype(jnp.bfloat16)
+            rest = face - high.astype(jnp.float32)
+            middle = rest.astype(jnp.bfloat16)
+            low = (rest - middle.astype(jnp.float32)).astype(jnp.bfloat16)
+            ext = jnp.dot(high, expand_ref[f], preferred_element_type=jnp.float32)
+            ext = ext + jnp.dot(middle, expand_ref[f], preferred_element_type=jnp.float32)
+            ext = ext + jnp.dot(low, expand_ref[f], preferred_element_type=jnp.float32)
+            g_self = gx if f < 2 else gy
+            conduct = jnp.where(masks[f], scale_ref[b, 1 + f] * (g_self * ext[:nz]), 0.0)
+            step_u = ext[nz:2 * nz] - u
+            step_l = conduct * (ext[2 * nz:3 * nz] - l)
+            face_u = face_u + conduct * step_u
+            face_l = face_l + step_l
+            face_t = face_t + step_l * step_u
+        square = th * th
+        ionic = u * (1.0 - u) * (u - THRESHOLD)
+        slope = -3.0 * u * u + 2.0 * (1.0 + THRESHOLD) * u - THRESHOLD
+        u_out[i] = u + TIMESTEP * ((square * lap_u + th * face_u) + ionic)
+        l_out[i] = l + TIMESTEP * ((square * lap_l + th * face_l) + slope * l)
+        part_out[i] = -(square * inner + th * group_sum(face_t))
+        return carry
+
+    lax.fori_loop(0, GROUP, one, 0)
+
+
+def inner_step(tissue, angle, potential, sensitivity, interpret=False):
+    bricks, nz, cells = potential.shape
+    blk3 = lambda: pl.BlockSpec((GROUP, nz, cells), lambda g: (g, 0, 0))
+    full = jax.ShapeDtypeStruct((bricks, nz, cells), jnp.float32)
+    return pl.pallas_call(
+        inner_kernel,
+        grid=(bricks // GROUP,),
+        in_specs=[blk3(), blk3(), blk3(), blk3()],
+        out_specs=[blk3(), blk3(), blk3(), blk3(), pl.BlockSpec((GROUP, 1, 128), lambda g: (g, 0, 0))],
+        out_shape=[full, full, full, full, jax.ShapeDtypeStruct((bricks, 1, 128), jnp.float32)],
+        compiler_params=pltpu.CompilerParams(dimension_semantics=("parallel",)),
+        interpret=interpret,
+    )(tissue, angle, potential, sensitivity)
+
+
+def outer_step(scales, potential, sensitivity, inner, faces, halos, interpret=False):
+    bricks, nz, cells = potential.shape
+    edge = faces.shape[-1]
+    expand = expanders(edge, cells).astype(jnp.bfloat16)
+    blk3 = lambda: pl.BlockSpec((GROUP, nz, cells), lambda g: (g, 0, 0))
+    lap_u, lap_l, gx, gy, inner_part = inner
+    return pl.pallas_call(
+        outer_kernel,
+        grid=(bricks // GROUP,),
+        in_specs=[
+            pl.BlockSpec(memory_space=pltpu.SMEM),
+            pl.BlockSpec((4, edge, cells), lambda g: (0, 0, 0)),
+            blk3(), blk3(), blk3(), blk3(), blk3(), blk3(),
+            pl.BlockSpec((GROUP, 1, 128), lambda g: (g, 0, 0)),
+            pl.BlockSpec((GROUP, 4, faces.shape[2], edge), lambda g: (g, 0, 0, 0)),
+            pl.BlockSpec((GROUP, 6, cells), lambda g: (g, 0, 0)),
+        ],
+        out_specs=[blk3(), blk3(), pl.BlockSpec((GROUP, 1, 128), lambda g: (g, 0, 0))],
+        out_shape=[
+            jax.ShapeDtypeStruct((bricks, nz, cells), jnp.float32),
+            jax.ShapeDtypeStruct((bricks, nz, cells), jnp.float32),
+            jax.ShapeDtypeStruct((bricks, 1, 128), jnp.float32),
+        ],
+        compiler_params=pltpu.CompilerParams(dimension_semantics=("parallel",)),
+        interpret=interpret,
+    )(scales, expand, potential, sensitivity, lap_u, lap_l, gx, gy, inner_part, faces, halos)
+
+
 def body(
     potential, fiber_angle, tissue, sensitivity, conductance, brick_slot, neighbours, brick_cell
 ):
@@ -237,6 +388,7 @@
     recv_slot = near_blk * capacity + recv_rank
 
     adjoint = sensitivity.astype(jnp.float32)
+    inner = inner_step(tissue, fiber_angle, potential, sensitivity)
     picker = expanders(brick_edge, plane_cells).reshape(4 * brick_edge, plane_cells).T.astype(jnp.float32)
 
     def boundary(values):
@@ -295,9 +447,7 @@
     scales = jnp.concatenate(
         [theta[:, None], theta_near, jnp.zeros((bricks, 3), jnp.float32)], axis=1
     )
-    final, adjoint, parts_out = cell_step(
-        scales, tissue, fiber_angle, potential, sensitivity, faces, halos
-    )
+    final, adjoint, parts_out = outer_step(scales, potential, sensitivity, inner, faces, halos)
     brick_part = jnp.sum(parts_out, axis=(1, 2))
     onehot_cells = brick_cell[:, None] == jnp.arange(cell_count, dtype=jnp.int32)[None, :]
     shares = jnp.sum(jnp.where(onehot_cells, brick_part[:, None], 0.0), axis=0)

time: 109 us -> 107 us (0.982)
  waiting for transfers between devices: 13.5 us -> 2.5 us
  Pallas kernels: 17 us -> 26.4 us
  local copies, waits for them, and re-layouts: 17.1 us -> 15.3 us
  other arithmetic: 8.75 us -> 10.4 us
    pallas_call x1 -> x2, Pallas kernels: 17 us -> 26.4 us  [the longest x1 15.2 us: outer_step(): pl.pallas_call(outer_kernel, grid=(bricks // GROUP,), in_specs=[pl.BlockS...]
    ppermute x1, waiting for transfers between devices: 8.72 us -> 0.01 us  [body(): lax.ppermute(initial, 'par', down)]
    slice x1, local copies, waits for them, and re-layouts: 2.19 us -> 0.34 us  [body(): potential[:, -1]]
    convert_element_type x1, other arithmetic: 0.16 us -> 1.82 us  [body(): tissue[:, -1].astype(jnp.float32)]
    ppermute x1, waiting for transfers between devices: 1.25 us -> 0.01 us  [body(): lax.ppermute(last, 'par', up)]
  transfers between devices with their start and end apart: 6 -> 6, of which waited for: 3 -> 1; matrix products, arithmetic and copies ran while one was open for 16% -> 16% of each run, Pallas kernels for 0% -> 10%
where the time goes in v4:
time: 107 us
  Pallas kernels  26.4 us (25%)
  starting transfers between devices  25 us (23%)
  blocking collectives  22.7 us (21%)
  local copies, waits for them, and re-layouts  15.3 us (14%)
  other arithmetic  10.4 us (10%)
  matrix products  3.59 us (3%)
  waiting for transfers between devices  2.5 us (2%)
  between operations  1.17 us (1%)
    all_to_all x1, blocking collectives, body(): lax.all_to_all(shares.reshape(devices, own_cells), ('blk', 'par'), split_...  22.7 us
    pallas_call x1, Pallas kernels, outer_step(): pl.pallas_call(outer_kernel, grid=(bricks // GROUP,), in_specs=[pl.BlockS...  15.2 us
    all_to_all x1, starting transfers between devices, body(): lax.all_to_all(sending, 'blk', split_axis=0, concat_axis=0, tiled=True)  13.2 us
    pallas_call x1, Pallas kernels, inner_step(): pl.pallas_call(inner_kernel, grid=(bricks // GROUP,), in_specs=[blk3(), b...  11.2 us
    ppermute x3, starting transfers between devices, body(): lax.ppermute(conductance, 'par', [(i, (i + s) % parts) for i in range(par...  6.32 us
    ppermute x1, starting transfers between devices, body(): lax.ppermute(last, 'par', up)  4.2 us
    dot_general x4, matrix products, boundary(): jnp.dot(values.astype(jnp.float32).reshape(bricks * z_layers, plane_cells...  3.59 us
    gather x4, local copies, waits for them, and re-layouts, body(): theta_near = cond_all[cell_all[near_slot]]  2.6 us
  transfers between devices with their start and end apart: 6, of which 1 were waited for; matrix products, arithmetic and copies ran while one was open for 16% of the time, Pallas kernels for 10%

profile of v4, /device:TPU:1, one launch (start us, length us, event | category | flops | bytes accessed | tf_op | source)
XLA Modules:
  0.0 107.0 jit_solution(10731615367405700195)
XLA Ops:
  0.7 3.6 %collective-permute-start.1 = (f32[2]{0:T(128)}, f32[2]{0:T(128)S(1)}, u32[]{:S(2)}, u32[]{:S(2)}) collective-permute-start(f32[2]{0:T(128)} %param.13), channel_id=1, source_target_pairs={{0,2},{1,3},{2,0},{3,1},{4,6},{5,7},{6,4},{7,5},{8,10},{9,11},{10,... | collective-permute-start | bytes 32 | tf_op jit(solution)/shard_map/ppermute | solution.py:417
  4.3 0.3 collective-permute-start
  4.6 2.4 %collective-permute-start.2 = (f32[2]{0:T(128)}, f32[2]{0:T(128)S(1)}, u32[]{:S(2)}, u32[]{:S(2)}) collective-permute-start(f32[2]{0:T(128)} %param.13), channel_id=1, source_target_pairs={{0,3},{1,0},{2,1},{3,2},{4,7},{5,4},{6,5},{7,6},{8,11},{9,8},{10,9... | collective-permute-start | bytes 32 | tf_op jit(solution)/shard_map/ppermute | solution.py:417
  7.0 0.7 compare_select_fusion.4
  7.8 0.7 compare_select_fusion.2
  8.5 0.1 reshape.486
  8.6 0.7 add.192
  9.3 0.1 add.193
  9.4 0.1 iota_compare_fusion.2
  9.5 0.1 iota_compare_fusion
  9.6 0.8 fusion.21
  10.4 1.4 %convolution_bitcast_fusion = f32[256,128]{0,1:T(8,128)S(1)} fusion(pred[128,1024]{1,0:T(32,128)(4,1)S(1)} %bitcast.83, bf16[32,8,1024]{2,1,0:T(8,128)(2,1)} %l_ref.3), kind=kOutput, calls=%fused_computation.8 | convolution fusion | flops 67108864 | bytes 786432 | tf_op jit(solution)/shard_map/dot_general | solution.py:395
  11.8 0.1 copy.34
  12.0 0.7 convolution_bitcast_fusion.1
  12.7 0.1 copy.33
  12.8 0.7 fusion.1
  13.5 0.7 convolution_bitcast_fusion.2
  14.3 0.1 copy.32
  14.4 0.3 integer_pow.14
  14.7 0.4 fusion.12
  15.1 0.3 reshape.472
  15.4 0.3 reshape.475
  15.7 0.3 reshape.477
  15.9 0.3 fusion.5
  16.3 0.4 pad_maximum_fusion
  16.7 0.1 copy.35
  16.8 0.4 reshape.536
  17.2 1.1 %gather_fusion = s32[128]{0:T(128)S(1)} fusion(s32[2048]{0:T(1024)S(1)} %copy-done, s32[1024]{0:T(1024)S(1)} %pad_clamp_fusion.5), kind=kCustom, calls=%fused_computation | custom fusion | bytes 1536 | tf_op jit(solution)/shard_map/gather | solution.py:380
  18.4 0.2 convert_reduce_fusion
  18.6 1.2 %scatter_custom_fusion = f32[256,768]{1,0:T(8,128)S(1)} fusion(s32[128]{0:T(128)S(1)} %get-tuple-element.32, f32[128,768]{1,0:T(8,128)S(1)} %reshape.536, f32[]{:T(128)} %constant.33.clone.1), kind=kCustom, calls=%fused_computation.27 | custom fusion | bytes 786436 | tf_op jit(solution)/shard_map/scatter | solution.py:415
  19.8 0.2 reshape.479
  20.1 0.6 gather_fusion.1
  20.9 1.5 %all_to_all.14 = f32[64,1,3200]{2,1,0:T(1,128)} reshape(f32[64,3200]{1,0:T(8,128)S(1)} %pad_maximum_fusion.2) | data formatting | bytes 1638400 | tf_op jit(solution)/shard_map/all_to_all | solution.py:428
  22.4 13.2 %all-to-all-start = ((f32[64,1,3200]{2,1,0:T(1,128)}), f32[64,1,3200]{2,1,0:T(1,128)S(1)}, u32[]{:S(2)}, u32[]{:S(2)}) async-start(f32[64,1,3200]{2,1,0:T(1,128)} %all_to_all.14), calls=%async_computation | async-start | bytes 1638400 | tf_op jit(solution)/shard_map/all_to_all | solution.py:428
  35.5 1.8 %slice_convert_fusion.1 = (f32[32,1,1024]{2,1,0:T(1,128)S(1)}, f32[32,1,1024]{2,1,0:T(1,128)S(1)}) fusion(s32[32,8,1024]{2,1,0:T(8,128)} %tissue_ref.1), kind=kLoop, calls=%fused_computation.35 | loop fusion | flops 65536 | bytes 524288 | tf_op jit(solution)/shard_map/convert_element_type | solution.py:441
  37.4 0.3 fusion.22
  37.7 0.3 pad_maximum_fusion.4
  38.1 1.3 %collective-permute-start.4 = (f32[32,3,1024]{2,1,0:T(4,128)S(1)}, f32[32,3,1024]{2,1,0:T(4,128)S(1)}, u32[]{:S(2)}, u32[]{:S(2)}) collective-permute-start(f32[32,3,1024]{2,1,0:T(4,128)S(1)} %pad_maximum_fusion.4), channel_id=1, source_target_pairs={{1,0},{2,1},{3,2},{5,4},{6,5},{7,6},{9,8},{10,9},{11,10},{13,12},{... | collective-permute-start | bytes 1179656 | tf_op jit(solution)/shard_map/ppermute | solution.py:443
  39.4 0.3 pad_maximum_fusion.3
  39.7 4.2 %collective-permute-start.3 = (f32[32,3,1024]{2,1,0:T(4,128)S(1)}, f32[32,3,1024]{2,1,0:T(4,128)S(1)}, u32[]{:S(2)}, u32[]{:S(2)}) collective-permute-start(f32[32,3,1024]{2,1,0:T(4,128)S(1)} %pad_maximum_fusion.3), channel_id=1, source_target_pairs={{0,1},{1,2},{2,3},{4,5},{5,6},{6,7},{8,9},{9,10},{10,11},{12,13},{... | collective-permute-start | bytes 1179656 | tf_op jit(solution)/shard_map/ppermute | solution.py:443
  43.9 0.1 gather.31
  44.0 11.2 %shard_map.112 = (f32[32,8,1024]{2,1,0:T(8,128)}, f32[32,8,1024]{2,1,0:T(8,128)}, f32[32,8,1024]{2,1,0:T(8,128)}, f32[32,8,1024]{2,1,0:T(8,128)}, f32[32,1,128]{2,1,0:T(1,128)}) custom-call(s32[32,8,1024]{2,1,0:T(8,128)} %tissue_ref.1, bf16[32,8,1024]{2,1,0:T(8,128)(2,1)} %angle_ref.1, f32[32,8,1024]{2,1,0:T(8,128)} %u_ref.3, bf16[32,8,1024]{2,1,0:T(8,128)(2,1)} %l_ref.3), custom_call_target="tpu_custom_call" | custom-call | tf_op jit(solution)/shard_map/pallas_call | solution.py:326
  55.3 0.1 reshape.510
  55.5 1.2 %pad_maximum_fusion.1.halo_ref = f32[32,6,1024]{2,1,0:T(8,128)} fusion(f32[32,3,1024]{2,1,0:T(4,128)S(1)} %collective-permute-done.4, f32[32,3,1024]{2,1,0:T(4,128)S(1)} %collective-permute-done.3), kind=kLoop, calls=%fused_computation.14 | loop fusion | flops 196608 | bytes 1572864 | tf_op jit(solution)/shard_map/concatenate | solution.py:443
  56.7 2.5 %all-to-all-done = f32[64,1,3200]{2,1,0:T(1,128)S(1)} async-done(((f32[64,1,3200]{2,1,0:T(1,128)}), f32[64,1,3200]{2,1,0:T(1,128)S(1)}, u32[]{:S(2)}, u32[]{:S(2)}) %all-to-all-start) | async-done | bytes 819232 | tf_op jit(solution)/shard_map/all_to_all | solution.py:428
  59.5 1.1 %gather_fusion.3 = s32[128]{0:T(128)S(1)} fusion(s32[2048]{0:T(1024)S(1)} %convert_element_type.43, s32[1024]{0:T(1024)S(1)} %pad_clamp_fusion.2), kind=kCustom, calls=%fused_computation.3 | custom fusion | bytes 1536 | tf_op jit(solution)/shard_map/gather | solution.py:446
  60.6 0.1 gather.33
  60.7 0.1 reshape.518
  60.9 0.1 reshape.481
  61.0 1.3 %gather_fusion.4 = f32[128]{0:T(128)S(1)} fusion(f32[512]{0:T(512)S(1)} %reshape.481, s32[1024]{0:T(1024)S(1)} %pad_clamp_fusion.1), kind=kCustom, calls=%fused_computation.4 | custom fusion | bytes 1536 | tf_op jit(solution)/shard_map/gather | solution.py:446
  62.2 0.7 gather_fusion.2
  62.9 0.2 reshape.482
  63.3 0.1 reshape.517
  63.4 0.8 gather_fusion.5
  64.2 0.5 reshape.483
  64.7 1.6 %pad.9.face_ref = f32[32,4,32,32]{3,2,1,0:T(8,128)} pad(f32[32,4,24,32]{3,2,1,0:T(8,128)S(1)} %reshape.483, f32[]{:T(128)} %constant.33.clone.1), padding=0_0x0_0x0_8x0_0 | pad | bytes 917508 | tf_op jit(solution)/shard_map/jit(_pad)/pad | solution.py:436
  66.3 0.7 maximum_maximum_fusion.scale_ref
  67.0 15.2 %shard_map.113 = (f32[32,8,1024]{2,1,0:T(8,128)}, f32[32,8,1024]{2,1,0:T(8,128)}, f32[32,1,128]{2,1,0:T(1,128)}) custom-call(f32[32,8]{1,0:T(8,128)} %maximum_maximum_fusion.scale_ref, bf16[4,32,1024]{2,1,0:T(8,128)(2,1)} %get-tuple-element.21.expand_ref, f32[32,8,1024]{2,1,0:T(8,128)} %u_ref.3, bf16[32,8,1024]{2,1,0:T(8,128)(2,1)} %l_ref.3, ...), custom_call_target="tpu_custom_call" | custom-call | tf_op jit(solution)/shard_map/pallas_call | solution.py:343
  82.2 1.0 reduce_sum.53
  83.3 0.1 select_reduce_fusion
  83.3 0.1 all_to_all.17
  83.5 22.7 %all_to_all.21 = f32[256,1,2]{2,1,0:T(1,128)S(1)} all-to-all(f32[256,1,2]{2,1,0:T(1,128)S(1)} %bitcast.90), channel_id=1, replica_groups=mesh['blk'=64,'par'=4] {'blk','par'}, dimensions={0} | all-to-all | bytes 4096 | tf_op jit(solution)/shard_map/all_to_all | solution.py:455
  106.2 0.3 reduce_sum.55
  106.5 0.5 multiply_divide_fusion
  (48 shorter events, 1.0 us)
Async XLA Ops:
  0.6 16.6 %copy-start = (s32[2048]{0:T(1024)S(1)}, s32[2048]{0:T(1024)}, u32[]{:S(2)}) copy-start(s32[2048]{0:T(1024)} %param.14) | copy-start | bytes 24580
  0.6 11.3 %copy-start.1 = (f32[32,8,1024]{2,1,0:T(8,128)S(1)}, f32[32,8,1024]{2,1,0:T(8,128)}, u32[]{:S(2)}) copy-start(f32[32,8,1024]{2,1,0:T(8,128)} %u_ref.3) | copy-start | bytes 3145732
  0.7 19.4 %collective-permute-start.1 = (f32[2]{0:T(128)}, f32[2]{0:T(128)S(1)}, u32[]{:S(2)}, u32[]{:S(2)}) collective-permute-start(f32[2]{0:T(128)} %param.13), channel_id=1, source_target_pairs={{0,2},{1,3},{2,0},{3,1},{4,6},{5,7},{6,4},{7,5},{8,10},{9,11},{10,... | collective-permute-start | bytes 32 | tf_op jit(solution)/shard_map/ppermute | solution.py:417
  4.3 15.8 %collective-permute-start = (f32[2]{0:T(128)}, f32[2]{0:T(128)S(1)}, u32[]{:S(2)}, u32[]{:S(2)}) collective-permute-start(f32[2]{0:T(128)} %param.13), channel_id=1, source_target_pairs={{0,1},{1,2},{2,3},{3,0},{4,5},{5,6},{6,7},{7,4},{8,9},{9,10},{10,1... | collective-permute-start | bytes 32 | tf_op jit(solution)/shard_map/ppermute | solution.py:417
  4.6 15.5 %collective-permute-start.2 = (f32[2]{0:T(128)}, f32[2]{0:T(128)S(1)}, u32[]{:S(2)}, u32[]{:S(2)}) collective-permute-start(f32[2]{0:T(128)} %param.13), channel_id=1, source_target_pairs={{0,3},{1,0},{2,1},{3,2},{4,7},{5,4},{6,5},{7,6},{8,11},{9,8},{10,9... | collective-permute-start | bytes 32 | tf_op jit(solution)/shard_map/ppermute | solution.py:417
  9.6 3.1 %copy-start.4 = (bf16[32,8,1024]{2,1,0:T(8,128)(2,1)S(1)}, bf16[32,8,1024]{2,1,0:T(8,128)(2,1)}, u32[]{:S(2)}) copy-start(bf16[32,8,1024]{2,1,0:T(8,128)(2,1)} %angle_ref.1) | copy-start | bytes 1572868
  10.4 3.1 %copy-start.3 = (s32[32,8,1024]{2,1,0:T(8,128)S(1)}, s32[32,8,1024]{2,1,0:T(8,128)}, u32[]{:S(2)}) copy-start(s32[32,8,1024]{2,1,0:T(8,128)} %tissue_ref.1) | copy-start | bytes 3145732
  18.4 1.7 %copy-start.6 = (f32[2]{0:T(128)S(1)}, f32[2]{0:T(128)}, u32[]{:S(2)}) copy-start(f32[2]{0:T(128)} %param.13) | copy-start | bytes 28
  20.9 16.5 %copy-start.2 = (bf16[32,8,1024]{2,1,0:T(8,128)(2,1)S(1)}, bf16[32,8,1024]{2,1,0:T(8,128)(2,1)}, u32[]{:S(2)}) copy-start(bf16[32,8,1024]{2,1,0:T(8,128)(2,1)} %l_ref.3) | copy-start | bytes 1572868
  22.4 36.8 %all-to-all-start = ((f32[64,1,3200]{2,1,0:T(1,128)}), f32[64,1,3200]{2,1,0:T(1,128)S(1)}, u32[]{:S(2)}, u32[]{:S(2)}) async-start(f32[64,1,3200]{2,1,0:T(1,128)} %all_to_all.14), calls=%async_computation | async-start | bytes 1638400 | tf_op jit(solution)/shard_map/all_to_all | solution.py:428
  38.1 17.4 %collective-permute-start.4 = (f32[32,3,1024]{2,1,0:T(4,128)S(1)}, f32[32,3,1024]{2,1,0:T(4,128)S(1)}, u32[]{:S(2)}, u32[]{:S(2)}) collective-permute-start(f32[32,3,1024]{2,1,0:T(4,128)S(1)} %pad_maximum_fusion.4), channel_id=1, source_target_pairs={{1,0},{2,1},{3,2},{5,4},{6,5},{7,6},{9,8},{10,9},{11,10},{13,12},{... | collective-permute-start | bytes 1179656 | tf_op jit(solution)/shard_map/ppermute | solution.py:443
  39.7 15.7 %collective-permute-start.3 = (f32[32,3,1024]{2,1,0:T(4,128)S(1)}, f32[32,3,1024]{2,1,0:T(4,128)S(1)}, u32[]{:S(2)}, u32[]{:S(2)}) collective-permute-start(f32[32,3,1024]{2,1,0:T(4,128)S(1)} %pad_maximum_fusion.3), channel_id=1, source_target_pairs={{0,1},{1,2},{2,3},{4,5},{5,6},{6,7},{8,9},{9,10},{10,11},{12,13},{... | collective-permute-start | bytes 1179656 | tf_op jit(solution)/shard_map/ppermute | solution.py:443
  67.0 16.3 %copy-start.5 = (s32[32]{0:T(128)S(1)}, s32[32]{0:T(128)}, u32[]{:S(2)}) copy-start(s32[32]{0:T(128)} %param.16) | copy-start | bytes 388

commit v5 on v4

--- a/solution.py
+++ b/solution.py
@@ -294,17 +294,23 @@
         face_t = jnp.zeros_like(u)
         for f in range(4):
             face = face_ref[i, f]
-            high = face.astype(jnp.bfloat16)
-            rest = face - high.astype(jnp.float32)
-            middle = rest.astype(jnp.bfloat16)
-            low = (rest - middle.astype(jnp.float32)).astype(jnp.bfloat16)
-            ext = jnp.dot(high, expand_ref[f], preferred_element_type=jnp.float32)
-            ext = ext + jnp.dot(middle, expand_ref[f], preferred_element_type=jnp.float32)
-            ext = ext + jnp.dot(low, expand_ref[f], preferred_element_type=jnp.float32)
+            pieces = []
+            for part in (face[:2 * nz],):
+                high = part.astype(jnp.bfloat16).astype(jnp.float32)
+                rest = part - high
+                middle = rest.astype(jnp.bfloat16).astype(jnp.float32)
+                low = (rest - middle).astype(jnp.bfloat16).astype(jnp.float32)
+                pieces += [high, middle, low]
+            pieces += [face[2 * nz:3 * nz], jnp.zeros_like(face[:nz])]
+            stacked = jnp.concatenate(pieces, axis=0).astype(jnp.bfloat16)
+            ext = jnp.dot(stacked, expand_ref[f], preferred_element_type=jnp.float32)
+            near_w = (ext[0:nz] + ext[2 * nz:3 * nz]) + ext[4 * nz:5 * nz]
+            near_u = (ext[nz:2 * nz] + ext[3 * nz:4 * nz]) + ext[5 * nz:6 * nz]
+            near_l = ext[6 * nz:7 * nz]
             g_self = gx if f < 2 else gy
-            conduct = jnp.where(masks[f], scale_ref[b, 1 + f] * (g_self * ext[:nz]), 0.0)
-            step_u = ext[nz:2 * nz] - u
-            step_l = conduct * (ext[2 * nz:3 * nz] - l)
+            conduct = jnp.where(masks[f], scale_ref[b, 1 + f] * (g_self * near_w), 0.0)
+            step_u = near_u - u
+            step_l = conduct * (near_l - l)
             face_u = face_u + conduct * step_u
             face_l = face_l + step_l
             face_t = face_t + step_l * step_u
@@ -433,7 +439,6 @@
     faces = received.reshape(blocks * capacity, 3 * face_cells)[recv_slot].reshape(
         bricks, 4, 3 * z_layers, brick_edge
     )
-    faces = jnp.pad(faces, ((0, 0), (0, 0), (0, 32 - 3 * z_layers % 32), (0, 0)))
 
     size = lax.axis_size("par")
     up = [(i, i + 1) for i in range(size - 1)]

time: 107 us -> 105 us (0.981)
  Pallas kernels: 26.4 us -> 24.6 us
    pallas_call x1, Pallas kernels: 15.2 us -> 13.5 us  [outer_step(): pl.pallas_call(outer_kernel, grid=(bricks // GROUP,), in_specs=[pl.BlockS...]
    pad x1 -> x0, local copies, waits for them, and re-layouts: 1.62 us -> none  [body(): jnp.pad(faces, ((0, 0), (0, 0), (0, 32 - 3 * z_layers % 32), (0, 0)))]
    reshape x2, local copies, waits for them, and re-layouts: 0.69 us -> 1.84 us  [body(): received.reshape(blocks * capacity, 3 * face_cells)[recv_slot]]
  transfers between devices with their start and end apart: 6 -> 6, of which waited for: 1 -> 1; matrix products, arithmetic and copies ran while one was open for 16% -> 16% of each run, Pallas kernels for 10% -> 11%
where the time goes in v5:
time: 105 us
  starting transfers between devices  25 us (24%)
  Pallas kernels  24.6 us (23%)
  blocking collectives  22.7 us (22%)
  local copies, waits for them, and re-layouts  14.8 us (14%)
  other arithmetic  10.4 us (10%)
  matrix products  3.59 us (3%)
  waiting for transfers between devices  2.49 us (2%)
  between operations  1.16 us (1%)
    all_to_all x1, blocking collectives, body(): lax.all_to_all(shares.reshape(devices, own_cells), ('blk', 'par'), split_...  22.7 us
    pallas_call x1, Pallas kernels, outer_step(): pl.pallas_call(outer_kernel, grid=(bricks // GROUP,), in_specs=[pl.BlockS...  13.5 us
    all_to_all x1, starting transfers between devices, body(): lax.all_to_all(sending, 'blk', split_axis=0, concat_axis=0, tiled=True)  13.2 us
    pallas_call x1, Pallas kernels, inner_step(): pl.pallas_call(inner_kernel, grid=(bricks // GROUP,), in_specs=[blk3(), b...  11.2 us
    ppermute x3, starting transfers between devices, body(): lax.ppermute(conductance, 'par', [(i, (i + s) % parts) for i in range(par...  6.32 us
    ppermute x1, starting transfers between devices, body(): lax.ppermute(last, 'par', up)  4.2 us
    dot_general x4, matrix products, boundary(): jnp.dot(values.astype(jnp.float32).reshape(bricks * z_layers, plane_cells...  3.59 us
    gather x4, local copies, waits for them, and re-layouts, body(): theta_near = cond_all[cell_all[near_slot]]  2.6 us
  transfers between devices with their start and end apart: 6, of which 1 were waited for; matrix products, arithmetic and copies ran while one was open for 16% of the time, Pallas kernels for 11%

profile of v5, /device:TPU:1, one launch (start us, length us, event | category | flops | bytes accessed | tf_op | source)
XLA Modules:
  0.0 104.7 jit_solution(483654930376901603)
XLA Ops:
  0.7 3.6 %collective-permute-start.1 = (f32[2]{0:T(128)}, f32[2]{0:T(128)S(1)}, u32[]{:S(2)}, u32[]{:S(2)}) collective-permute-start(f32[2]{0:T(128)} %param.13), channel_id=1, source_target_pairs={{0,2},{1,3},{2,0},{3,1},{4,6},{5,7},{6,4},{7,5},{8,10},{9,11},{10,... | collective-permute-start | bytes 32 | tf_op jit(solution)/shard_map/ppermute | solution.py:423
  4.3 0.3 collective-permute-start
  4.6 2.4 %collective-permute-start.2 = (f32[2]{0:T(128)}, f32[2]{0:T(128)S(1)}, u32[]{:S(2)}, u32[]{:S(2)}) collective-permute-start(f32[2]{0:T(128)} %param.13), channel_id=1, source_target_pairs={{0,3},{1,0},{2,1},{3,2},{4,7},{5,4},{6,5},{7,6},{8,11},{9,8},{10,9... | collective-permute-start | bytes 32 | tf_op jit(solution)/shard_map/ppermute | solution.py:423
  7.0 0.7 compare_select_fusion.4
  7.8 0.7 compare_select_fusion.2
  8.5 0.1 reshape.486
  8.6 0.7 add.190
  9.3 0.1 add.191
  9.4 0.1 iota_compare_fusion.2
  9.5 0.1 iota_compare_fusion
  9.6 0.8 fusion.21
  10.4 1.4 %convolution_bitcast_fusion = f32[256,128]{0,1:T(8,128)S(1)} fusion(pred[128,1024]{1,0:T(32,128)(4,1)S(1)} %bitcast.83, bf16[32,8,1024]{2,1,0:T(8,128)(2,1)} %l_ref.3), kind=kOutput, calls=%fused_computation.8 | convolution fusion | flops 67108864 | bytes 786432 | tf_op jit(solution)/shard_map/dot_general | solution.py:401
  11.9 0.1 copy.34
  12.0 0.7 convolution_bitcast_fusion.1
  12.7 0.1 copy.33
  12.8 0.7 fusion.1
  13.5 0.7 convolution_bitcast_fusion.2
  14.3 0.1 copy.31
  14.4 0.1 copy.32
  14.5 0.3 integer_pow.14
  14.7 0.4 fusion.12
  15.1 0.3 reshape.472
  15.4 0.3 reshape.475
  15.7 0.3 reshape.477
  15.9 0.3 fusion.5
  16.3 0.4 pad_maximum_fusion
  16.7 0.1 copy.35
  16.8 0.4 reshape.536
  17.2 1.1 %gather_fusion = s32[128]{0:T(128)S(1)} fusion(s32[2048]{0:T(1024)S(1)} %copy-done, s32[1024]{0:T(1024)S(1)} %pad_clamp_fusion.5), kind=kCustom, calls=%fused_computation | custom fusion | bytes 1536 | tf_op jit(solution)/shard_map/gather | solution.py:386
  18.4 0.2 convert_reduce_fusion
  18.6 1.2 %scatter_custom_fusion = f32[256,768]{1,0:T(8,128)S(1)} fusion(s32[128]{0:T(128)S(1)} %get-tuple-element.32, f32[128,768]{1,0:T(8,128)S(1)} %reshape.536, f32[]{:T(128)} %constant.33.clone.1), kind=kCustom, calls=%fused_computation.27 | custom fusion | bytes 786436 | tf_op jit(solution)/shard_map/scatter | solution.py:421
  19.8 0.2 reshape.479
  20.1 0.6 gather_fusion.1
  20.9 1.5 %all_to_all.14 = f32[64,1,3200]{2,1,0:T(1,128)} reshape(f32[64,3200]{1,0:T(8,128)S(1)} %pad_maximum_fusion.2) | data formatting | bytes 1638400 | tf_op jit(solution)/shard_map/all_to_all | solution.py:434
  22.4 13.2 %all-to-all-start = ((f32[64,1,3200]{2,1,0:T(1,128)}), f32[64,1,3200]{2,1,0:T(1,128)S(1)}, u32[]{:S(2)}, u32[]{:S(2)}) async-start(f32[64,1,3200]{2,1,0:T(1,128)} %all_to_all.14), calls=%async_computation | async-start | bytes 1638400 | tf_op jit(solution)/shard_map/all_to_all | solution.py:434
  35.6 1.8 %slice_convert_fusion.1 = (f32[32,1,1024]{2,1,0:T(1,128)S(1)}, f32[32,1,1024]{2,1,0:T(1,128)S(1)}) fusion(s32[32,8,1024]{2,1,0:T(8,128)} %tissue_ref.1), kind=kLoop, calls=%fused_computation.35 | loop fusion | flops 65536 | bytes 524288 | tf_op jit(solution)/shard_map/convert_element_type | solution.py:446
  37.4 0.3 fusion.22
  37.7 0.3 pad_maximum_fusion.4
  38.1 1.3 %collective-permute-start.4 = (f32[32,3,1024]{2,1,0:T(4,128)S(1)}, f32[32,3,1024]{2,1,0:T(4,128)S(1)}, u32[]{:S(2)}, u32[]{:S(2)}) collective-permute-start(f32[32,3,1024]{2,1,0:T(4,128)S(1)} %pad_maximum_fusion.4), channel_id=1, source_target_pairs={{1,0},{2,1},{3,2},{5,4},{6,5},{7,6},{9,8},{10,9},{11,10},{13,12},{... | collective-permute-start | bytes 1179656 | tf_op jit(solution)/shard_map/ppermute | solution.py:448
  39.4 0.3 pad_maximum_fusion.3
  39.7 4.2 %collective-permute-start.3 = (f32[32,3,1024]{2,1,0:T(4,128)S(1)}, f32[32,3,1024]{2,1,0:T(4,128)S(1)}, u32[]{:S(2)}, u32[]{:S(2)}) collective-permute-start(f32[32,3,1024]{2,1,0:T(4,128)S(1)} %pad_maximum_fusion.3), channel_id=1, source_target_pairs={{0,1},{1,2},{2,3},{4,5},{5,6},{6,7},{8,9},{9,10},{10,11},{12,13},{... | collective-permute-start | bytes 1179656 | tf_op jit(solution)/shard_map/ppermute | solution.py:448
  44.0 0.1 gather.31
  44.1 11.2 %shard_map.112 = (f32[32,8,1024]{2,1,0:T(8,128)}, f32[32,8,1024]{2,1,0:T(8,128)}, f32[32,8,1024]{2,1,0:T(8,128)}, f32[32,8,1024]{2,1,0:T(8,128)}, f32[32,1,128]{2,1,0:T(1,128)}) custom-call(s32[32,8,1024]{2,1,0:T(8,128)} %tissue_ref.1, bf16[32,8,1024]{2,1,0:T(8,128)(2,1)} %angle_ref.1, f32[32,8,1024]{2,1,0:T(8,128)} %u_ref.3, bf16[32,8,1024]{2,1,0:T(8,128)(2,1)} %l_ref.3), custom_call_target="tpu_custom_call" | custom-call | tf_op jit(solution)/shard_map/pallas_call | solution.py:332
  55.3 0.1 reshape.510
  55.5 1.2 %pad_maximum_fusion.1.halo_ref = f32[32,6,1024]{2,1,0:T(8,128)} fusion(f32[32,3,1024]{2,1,0:T(4,128)S(1)} %collective-permute-done.4, f32[32,3,1024]{2,1,0:T(4,128)S(1)} %collective-permute-done.3), kind=kLoop, calls=%fused_computation.14 | loop fusion | flops 196608 | bytes 1572864 | tf_op jit(solution)/shard_map/concatenate | solution.py:448
  56.7 2.5 %all-to-all-done = f32[64,1,3200]{2,1,0:T(1,128)S(1)} async-done(((f32[64,1,3200]{2,1,0:T(1,128)}), f32[64,1,3200]{2,1,0:T(1,128)S(1)}, u32[]{:S(2)}, u32[]{:S(2)}) %all-to-all-start) | async-done | bytes 819232 | tf_op jit(solution)/shard_map/all_to_all | solution.py:434
  59.5 1.1 %gather_fusion.3 = s32[128]{0:T(128)S(1)} fusion(s32[2048]{0:T(1024)S(1)} %convert_element_type.41, s32[1024]{0:T(1024)S(1)} %pad_clamp_fusion.2), kind=kCustom, calls=%fused_computation.3 | custom fusion | bytes 1536 | tf_op jit(solution)/shard_map/gather | solution.py:451
  60.6 0.1 gather.33
  60.8 0.1 reshape.518
  60.9 0.1 reshape.481
  61.0 1.3 %gather_fusion.4 = f32[128]{0:T(128)S(1)} fusion(f32[512]{0:T(512)S(1)} %reshape.481, s32[1024]{0:T(1024)S(1)} %pad_clamp_fusion.1), kind=kCustom, calls=%fused_computation.4 | custom fusion | bytes 1536 | tf_op jit(solution)/shard_map/gather | solution.py:451
  62.2 0.7 gather_fusion.2
  63.0 0.2 reshape.482
  63.3 0.1 reshape.517
  63.4 0.8 gather_fusion.5
  64.2 1.6 %reshape.483.face_ref = f32[32,4,24,32]{3,2,1,0:T(8,128)} reshape(f32[128,768]{1,0:T(8,128)S(1)} %gather_fusion.5) | data formatting | bytes 786432 | tf_op jit(solution)/shard_map/reshape | solution.py:439
  65.8 0.7 maximum_maximum_fusion.scale_ref
  66.5 13.5 %shard_map.113 = (f32[32,8,1024]{2,1,0:T(8,128)}, f32[32,8,1024]{2,1,0:T(8,128)}, f32[32,1,128]{2,1,0:T(1,128)}) custom-call(f32[32,8]{1,0:T(8,128)} %maximum_maximum_fusion.scale_ref, bf16[4,32,1024]{2,1,0:T(8,128)(2,1)} %get-tuple-element.21.expand_ref, f32[32,8,1024]{2,1,0:T(8,128)} %u_ref.3, bf16[32,8,1024]{2,1,0:T(8,128)(2,1)} %l_ref.3, ...), custom_call_target="tpu_custom_call" | custom-call | tf_op jit(solution)/shard_map/pallas_call | solution.py:349
  80.0 1.0 reduce_sum.53
  81.0 0.1 select_reduce_fusion
  81.1 0.1 all_to_all.17
  81.2 22.7 %all_to_all.21 = f32[256,1,2]{2,1,0:T(1,128)S(1)} all-to-all(f32[256,1,2]{2,1,0:T(1,128)S(1)} %bitcast.90), channel_id=1, replica_groups=mesh['blk'=64,'par'=4] {'blk','par'}, dimensions={0} | all-to-all | bytes 4096 | tf_op jit(solution)/shard_map/all_to_all | solution.py:460
  103.9 0.3 reduce_sum.55
  104.2 0.5 multiply_divide_fusion
  (47 shorter events, 0.9 us)
Async XLA Ops:
  0.6 16.6 %copy-start = (s32[2048]{0:T(1024)S(1)}, s32[2048]{0:T(1024)}, u32[]{:S(2)}) copy-start(s32[2048]{0:T(1024)} %param.14) | copy-start | bytes 24580
  0.6 11.3 %copy-start.1 = (f32[32,8,1024]{2,1,0:T(8,128)S(1)}, f32[32,8,1024]{2,1,0:T(8,128)}, u32[]{:S(2)}) copy-start(f32[32,8,1024]{2,1,0:T(8,128)} %u_ref.3) | copy-start | bytes 3145732
  0.7 19.4 %collective-permute-start.1 = (f32[2]{0:T(128)}, f32[2]{0:T(128)S(1)}, u32[]{:S(2)}, u32[]{:S(2)}) collective-permute-start(f32[2]{0:T(128)} %param.13), channel_id=1, source_target_pairs={{0,2},{1,3},{2,0},{3,1},{4,6},{5,7},{6,4},{7,5},{8,10},{9,11},{10,... | collective-permute-start | bytes 32 | tf_op jit(solution)/shard_map/ppermute | solution.py:423
  4.3 15.8 %collective-permute-start = (f32[2]{0:T(128)}, f32[2]{0:T(128)S(1)}, u32[]{:S(2)}, u32[]{:S(2)}) collective-permute-start(f32[2]{0:T(128)} %param.13), channel_id=1, source_target_pairs={{0,1},{1,2},{2,3},{3,0},{4,5},{5,6},{6,7},{7,4},{8,9},{9,10},{10,1... | collective-permute-start | bytes 32 | tf_op jit(solution)/shard_map/ppermute | solution.py:423
  4.6 15.5 %collective-permute-start.2 = (f32[2]{0:T(128)}, f32[2]{0:T(128)S(1)}, u32[]{:S(2)}, u32[]{:S(2)}) collective-permute-start(f32[2]{0:T(128)} %param.13), channel_id=1, source_target_pairs={{0,3},{1,0},{2,1},{3,2},{4,7},{5,4},{6,5},{7,6},{8,11},{9,8},{10,9... | collective-permute-start | bytes 32 | tf_op jit(solution)/shard_map/ppermute | solution.py:423
  9.6 3.2 %copy-start.4 = (bf16[32,8,1024]{2,1,0:T(8,128)(2,1)S(1)}, bf16[32,8,1024]{2,1,0:T(8,128)(2,1)}, u32[]{:S(2)}) copy-start(bf16[32,8,1024]{2,1,0:T(8,128)(2,1)} %angle_ref.1) | copy-start | bytes 1572868
  10.4 3.1 %copy-start.3 = (s32[32,8,1024]{2,1,0:T(8,128)S(1)}, s32[32,8,1024]{2,1,0:T(8,128)}, u32[]{:S(2)}) copy-start(s32[32,8,1024]{2,1,0:T(8,128)} %tissue_ref.1) | copy-start | bytes 3145732
  18.4 1.7 %copy-start.6 = (f32[2]{0:T(128)S(1)}, f32[2]{0:T(128)}, u32[]{:S(2)}) copy-start(f32[2]{0:T(128)} %param.13) | copy-start | bytes 28
  20.9 16.5 %copy-start.2 = (bf16[32,8,1024]{2,1,0:T(8,128)(2,1)S(1)}, bf16[32,8,1024]{2,1,0:T(8,128)(2,1)}, u32[]{:S(2)}) copy-start(bf16[32,8,1024]{2,1,0:T(8,128)(2,1)} %l_ref.3) | copy-start | bytes 1572868
  22.4 36.8 %all-to-all-start = ((f32[64,1,3200]{2,1,0:T(1,128)}), f32[64,1,3200]{2,1,0:T(1,128)S(1)}, u32[]{:S(2)}, u32[]{:S(2)}) async-start(f32[64,1,3200]{2,1,0:T(1,128)} %all_to_all.14), calls=%async_computation | async-start | bytes 1638400 | tf_op jit(solution)/shard_map/all_to_all | solution.py:434
  38.1 17.4 %collective-permute-start.4 = (f32[32,3,1024]{2,1,0:T(4,128)S(1)}, f32[32,3,1024]{2,1,0:T(4,128)S(1)}, u32[]{:S(2)}, u32[]{:S(2)}) collective-permute-start(f32[32,3,1024]{2,1,0:T(4,128)S(1)} %pad_maximum_fusion.4), channel_id=1, source_target_pairs={{1,0},{2,1},{3,2},{5,4},{6,5},{7,6},{9,8},{10,9},{11,10},{13,12},{... | collective-permute-start | bytes 1179656 | tf_op jit(solution)/shard_map/ppermute | solution.py:448
  39.7 15.7 %collective-permute-start.3 = (f32[32,3,1024]{2,1,0:T(4,128)S(1)}, f32[32,3,1024]{2,1,0:T(4,128)S(1)}, u32[]{:S(2)}, u32[]{:S(2)}) collective-permute-start(f32[32,3,1024]{2,1,0:T(4,128)S(1)} %pad_maximum_fusion.3), channel_id=1, source_target_pairs={{0,1},{1,2},{2,3},{4,5},{5,6},{6,7},{8,9},{9,10},{10,11},{12,13},{... | collective-permute-start | bytes 1179656 | tf_op jit(solution)/shard_map/ppermute | solution.py:448
  66.5 14.5 %copy-start.5 = (s32[32]{0:T(128)S(1)}, s32[32]{0:T(128)}, u32[]{:S(2)}) copy-start(s32[32]{0:T(128)} %param.16) | copy-start | bytes 388

commit v6 on v5

--- a/solution.py
+++ b/solution.py
@@ -260,10 +260,26 @@
 
 
 def outer_kernel(scale_ref, expand_ref, u_ref, l_ref, lu_ref, ll_ref, gx_ref, gy_ref, inner_ref, face_ref,
-                 halo_ref, u_out, l_out, part_out):
+                 halo_ref, u_out, l_out, part_out, ext_ref):
     g = pl.program_id(0)
     nz, cells = u_ref.shape[1], u_ref.shape[2]
     edge = BX
+    rows = 8 * nz
+    for f in range(4):
+        face = face_ref[:, f]
+        part = face[:, :2 * nz]
+        high = part.astype(jnp.bfloat16).astype(jnp.float32)
+        rest = part - high
+        middle = rest.astype(jnp.bfloat16).astype(jnp.float32)
+        low = (rest - middle).astype(jnp.bfloat16).astype(jnp.float32)
+        stacked = jnp.concatenate(
+            [high, middle, low, face[:, 2 * nz:3 * nz], jnp.zeros_like(face[:, :nz])], axis=1
+        )
+        ext_ref[f] = jnp.dot(
+            stacked.reshape(GROUP * rows, edge).astype(jnp.bfloat16),
+            expand_ref[f],
+            preferred_element_type=jnp.float32,
+        )
     lane = lax.broadcasted_iota(jnp.int32, (nz, cells), 1)
     row = lax.broadcasted_iota(jnp.int32, (nz, cells), 0)
     ycoord = lane % edge
@@ -293,17 +309,7 @@
         face_l = jnp.zeros_like(u)
         face_t = jnp.zeros_like(u)
         for f in range(4):
-            face = face_ref[i, f]
-            pieces = []
-            for part in (face[:2 * nz],):
-                high = part.astype(jnp.bfloat16).astype(jnp.float32)
-                rest = part - high
-                middle = rest.astype(jnp.bfloat16).astype(jnp.float32)
-                low = (rest - middle).astype(jnp.bfloat16).astype(jnp.float32)
-                pieces += [high, middle, low]
-            pieces += [face[2 * nz:3 * nz], jnp.zeros_like(face[:nz])]
-            stacked = jnp.concatenate(pieces, axis=0).astype(jnp.bfloat16)
-            ext = jnp.dot(stacked, expand_ref[f], preferred_element_type=jnp.float32)
+            ext = ext_ref[f, pl.ds(pl.multiple_of(i * rows, rows), rows), :]
             near_w = (ext[0:nz] + ext[2 * nz:3 * nz]) + ext[4 * nz:5 * nz]
             near_u = (ext[nz:2 * nz] + ext[3 * nz:4 * nz]) + ext[5 * nz:6 * nz]
             near_l = ext[6 * nz:7 * nz]
@@ -363,6 +369,7 @@
             jax.ShapeDtypeStruct((bricks, nz, cells), jnp.float32),
             jax.ShapeDtypeStruct((bricks, 1, 128), jnp.float32),
         ],
+        scratch_shapes=[pltpu.VMEM((4, GROUP * 8 * nz, cells), jnp.float32)],
         compiler_params=pltpu.CompilerParams(dimension_semantics=("parallel",)),
         interpret=interpret,
     )(scales, expand, potential, sensitivity, lap_u, lap_l, gx, gy, inner_part, faces, halos)

time: 105 us -> 104 us (level)
  transfers between devices with their start and end apart: 6 -> 6, of which waited for: 1 -> 1; matrix products, arithmetic and copies ran while one was open for 16% -> 17% of each run, Pallas kernels for 11% -> 11%
where the time goes in v6:
time: 104 us
  starting transfers between devices  25 us (24%)
  Pallas kernels  23.9 us (23%)
  blocking collectives  22.7 us (22%)
  local copies, waits for them, and re-layouts  14.8 us (14%)
  other arithmetic  10.4 us (10%)
  matrix products  3.59 us (3%)
  waiting for transfers between devices  2.49 us (2%)
  between operations  1.16 us (1%)
    all_to_all x1, blocking collectives, body(): lax.all_to_all(shares.reshape(devices, own_cells), ('blk', 'par'), split_...  22.7 us
    all_to_all x1, starting transfers between devices, body(): lax.all_to_all(sending, 'blk', split_axis=0, concat_axis=0, tiled=True)  13.2 us
    pallas_call x1, Pallas kernels, outer_step(): pl.pallas_call(outer_kernel, grid=(bricks // GROUP,), in_specs=[pl.BlockS...  12.7 us
    pallas_call x1, Pallas kernels, inner_step(): pl.pallas_call(inner_kernel, grid=(bricks // GROUP,), in_specs=[blk3(), b...  11.2 us
    ppermute x3, starting transfers between devices, body(): lax.ppermute(conductance, 'par', [(i, (i + s) % parts) for i in range(par...  6.32 us
    ppermute x1, starting transfers between devices, body(): lax.ppermute(last, 'par', up)  4.2 us
    dot_general x4, matrix products, boundary(): jnp.dot(values.astype(jnp.float32).reshape(bricks * z_layers, plane_cells...  3.59 us
    gather x4, local copies, waits for them, and re-layouts, body(): theta_near = cond_all[cell_all[near_slot]]  2.6 us
  transfers between devices with their start and end apart: 6, of which 1 were waited for; matrix products, arithmetic and copies ran while one was open for 17% of the time, Pallas kernels for 11%

profile of v6, /device:TPU:1, one launch (start us, length us, event | category | flops | bytes accessed | tf_op | source)
XLA Modules:
  0.0 104.0 jit_solution(5166194828083085428)
XLA Ops:
  0.7 3.6 %collective-permute-start.1 = (f32[2]{0:T(128)}, f32[2]{0:T(128)S(1)}, u32[]{:S(2)}, u32[]{:S(2)}) collective-permute-start(f32[2]{0:T(128)} %param.13), channel_id=1, source_target_pairs={{0,2},{1,3},{2,0},{3,1},{4,6},{5,7},{6,4},{7,5},{8,10},{9,11},{10,... | collective-permute-start | bytes 32 | tf_op jit(solution)/shard_map/ppermute | solution.py:430
  4.3 0.3 collective-permute-start
  4.6 2.4 %collective-permute-start.2 = (f32[2]{0:T(128)}, f32[2]{0:T(128)S(1)}, u32[]{:S(2)}, u32[]{:S(2)}) collective-permute-start(f32[2]{0:T(128)} %param.13), channel_id=1, source_target_pairs={{0,3},{1,0},{2,1},{3,2},{4,7},{5,4},{6,5},{7,6},{8,11},{9,8},{10,9... | collective-permute-start | bytes 32 | tf_op jit(solution)/shard_map/ppermute | solution.py:430
  7.0 0.7 compare_select_fusion.4
  7.8 0.7 compare_select_fusion.2
  8.5 0.1 reshape.486
  8.6 0.7 add.190
  9.3 0.1 add.191
  9.4 0.1 iota_compare_fusion.2
  9.5 0.1 iota_compare_fusion
  9.6 0.8 fusion.21
  10.4 1.4 %convolution_bitcast_fusion = f32[256,128]{0,1:T(8,128)S(1)} fusion(pred[128,1024]{1,0:T(32,128)(4,1)S(1)} %bitcast.83, bf16[32,8,1024]{2,1,0:T(8,128)(2,1)} %l_ref.3), kind=kOutput, calls=%fused_computation.8 | convolution fusion | flops 67108864 | bytes 786432 | tf_op jit(solution)/shard_map/dot_general | solution.py:408
  11.9 0.1 copy.34
  12.0 0.7 convolution_bitcast_fusion.1
  12.7 0.1 copy.33
  12.8 0.7 fusion.1
  13.5 0.7 convolution_bitcast_fusion.2
  14.3 0.1 copy.31
  14.4 0.1 copy.32
  14.5 0.3 integer_pow.14
  14.7 0.4 fusion.12
  15.1 0.3 reshape.472
  15.4 0.3 reshape.475
  15.7 0.3 reshape.477
  15.9 0.3 fusion.5
  16.3 0.4 pad_maximum_fusion
  16.7 0.1 copy.35
  16.8 0.4 reshape.536
  17.2 1.1 %gather_fusion = s32[128]{0:T(128)S(1)} fusion(s32[2048]{0:T(1024)S(1)} %copy-done, s32[1024]{0:T(1024)S(1)} %pad_clamp_fusion.5), kind=kCustom, calls=%fused_computation | custom fusion | bytes 1536 | tf_op jit(solution)/shard_map/gather | solution.py:393
  18.4 0.2 convert_reduce_fusion
  18.6 1.2 %scatter_custom_fusion = f32[256,768]{1,0:T(8,128)S(1)} fusion(s32[128]{0:T(128)S(1)} %get-tuple-element.32, f32[128,768]{1,0:T(8,128)S(1)} %reshape.536, f32[]{:T(128)} %constant.33.clone.1), kind=kCustom, calls=%fused_computation.27 | custom fusion | bytes 786436 | tf_op jit(solution)/shard_map/scatter | solution.py:428
  19.8 0.2 reshape.479
  20.1 0.6 gather_fusion.1
  20.9 1.5 %all_to_all.14 = f32[64,1,3200]{2,1,0:T(1,128)} reshape(f32[64,3200]{1,0:T(8,128)S(1)} %pad_maximum_fusion.2) | data formatting | bytes 1638400 | tf_op jit(solution)/shard_map/all_to_all | solution.py:441
  22.4 13.2 %all-to-all-start = ((f32[64,1,3200]{2,1,0:T(1,128)}), f32[64,1,3200]{2,1,0:T(1,128)S(1)}, u32[]{:S(2)}, u32[]{:S(2)}) async-start(f32[64,1,3200]{2,1,0:T(1,128)} %all_to_all.14), calls=%async_computation | async-start | bytes 1638400 | tf_op jit(solution)/shard_map/all_to_all | solution.py:441
  35.6 1.8 %slice_convert_fusion.1 = (f32[32,1,1024]{2,1,0:T(1,128)S(1)}, f32[32,1,1024]{2,1,0:T(1,128)S(1)}) fusion(s32[32,8,1024]{2,1,0:T(8,128)} %tissue_ref.1), kind=kLoop, calls=%fused_computation.35 | loop fusion | flops 65536 | bytes 524288 | tf_op jit(solution)/shard_map/convert_element_type | solution.py:453
  37.4 0.3 fusion.22
  37.7 0.3 pad_maximum_fusion.4
  38.1 1.3 %collective-permute-start.4 = (f32[32,3,1024]{2,1,0:T(4,128)S(1)}, f32[32,3,1024]{2,1,0:T(4,128)S(1)}, u32[]{:S(2)}, u32[]{:S(2)}) collective-permute-start(f32[32,3,1024]{2,1,0:T(4,128)S(1)} %pad_maximum_fusion.4), channel_id=1, source_target_pairs={{1,0},{2,1},{3,2},{5,4},{6,5},{7,6},{9,8},{10,9},{11,10},{13,12},{... | collective-permute-start | bytes 1179656 | tf_op jit(solution)/shard_map/ppermute | solution.py:455
  39.4 0.3 pad_maximum_fusion.3
  39.7 4.2 %collective-permute-start.3 = (f32[32,3,1024]{2,1,0:T(4,128)S(1)}, f32[32,3,1024]{2,1,0:T(4,128)S(1)}, u32[]{:S(2)}, u32[]{:S(2)}) collective-permute-start(f32[32,3,1024]{2,1,0:T(4,128)S(1)} %pad_maximum_fusion.3), channel_id=1, source_target_pairs={{0,1},{1,2},{2,3},{4,5},{5,6},{6,7},{8,9},{9,10},{10,11},{12,13},{... | collective-permute-start | bytes 1179656 | tf_op jit(solution)/shard_map/ppermute | solution.py:455
  44.0 0.1 gather.31
  44.1 11.2 %shard_map.112 = (f32[32,8,1024]{2,1,0:T(8,128)}, f32[32,8,1024]{2,1,0:T(8,128)}, f32[32,8,1024]{2,1,0:T(8,128)}, f32[32,8,1024]{2,1,0:T(8,128)}, f32[32,1,128]{2,1,0:T(1,128)}) custom-call(s32[32,8,1024]{2,1,0:T(8,128)} %tissue_ref.1, bf16[32,8,1024]{2,1,0:T(8,128)(2,1)} %angle_ref.1, f32[32,8,1024]{2,1,0:T(8,128)} %u_ref.3, bf16[32,8,1024]{2,1,0:T(8,128)(2,1)} %l_ref.3), custom_call_target="tpu_custom_call" | custom-call | tf_op jit(solution)/shard_map/pallas_call | solution.py:338
  55.3 0.1 reshape.510
  55.5 1.2 %pad_maximum_fusion.1.halo_ref = f32[32,6,1024]{2,1,0:T(8,128)} fusion(f32[32,3,1024]{2,1,0:T(4,128)S(1)} %collective-permute-done.4, f32[32,3,1024]{2,1,0:T(4,128)S(1)} %collective-permute-done.3), kind=kLoop, calls=%fused_computation.14 | loop fusion | flops 196608 | bytes 1572864 | tf_op jit(solution)/shard_map/concatenate | solution.py:455
  56.7 2.5 %all-to-all-done = f32[64,1,3200]{2,1,0:T(1,128)S(1)} async-done(((f32[64,1,3200]{2,1,0:T(1,128)}), f32[64,1,3200]{2,1,0:T(1,128)S(1)}, u32[]{:S(2)}, u32[]{:S(2)}) %all-to-all-start) | async-done | bytes 819232 | tf_op jit(solution)/shard_map/all_to_all | solution.py:441
  59.5 1.1 %gather_fusion.3 = s32[128]{0:T(128)S(1)} fusion(s32[2048]{0:T(1024)S(1)} %convert_element_type.41, s32[1024]{0:T(1024)S(1)} %pad_clamp_fusion.2), kind=kCustom, calls=%fused_computation.3 | custom fusion | bytes 1536 | tf_op jit(solution)/shard_map/gather | solution.py:458
  60.6 0.1 gather.33
  60.8 0.1 reshape.518
  60.9 0.1 reshape.481
  61.0 1.3 %gather_fusion.4 = f32[128]{0:T(128)S(1)} fusion(f32[512]{0:T(512)S(1)} %reshape.481, s32[1024]{0:T(1024)S(1)} %pad_clamp_fusion.1), kind=kCustom, calls=%fused_computation.4 | custom fusion | bytes 1536 | tf_op jit(solution)/shard_map/gather | solution.py:458
  62.2 0.7 gather_fusion.2
  63.0 0.2 reshape.482
  63.3 0.1 reshape.517
  63.4 0.8 gather_fusion.5
  64.2 1.6 %reshape.483.face_ref = f32[32,4,24,32]{3,2,1,0:T(8,128)} reshape(f32[128,768]{1,0:T(8,128)S(1)} %gather_fusion.5) | data formatting | bytes 786432 | tf_op jit(solution)/shard_map/reshape | solution.py:446
  65.8 0.7 maximum_maximum_fusion.scale_ref
  66.5 12.7 %shard_map.113 = (f32[32,8,1024]{2,1,0:T(8,128)}, f32[32,8,1024]{2,1,0:T(8,128)}, f32[32,1,128]{2,1,0:T(1,128)}) custom-call(f32[32,8]{1,0:T(8,128)} %maximum_maximum_fusion.scale_ref, bf16[4,32,1024]{2,1,0:T(8,128)(2,1)} %get-tuple-element.21.expand_ref, f32[32,8,1024]{2,1,0:T(8,128)} %u_ref.3, bf16[32,8,1024]{2,1,0:T(8,128)(2,1)} %l_ref.3, ...), custom_call_target="tpu_custom_call" | custom-call | tf_op jit(solution)/shard_map/pallas_call | solution.py:355
  79.2 1.0 %reduce_sum.53 = f32[32]{0:T(128)S(1)} reduce(f32[32,1,128]{2,1,0:T(1,128)} %get-tuple-element.18, f32[]{:T(128)} %constant.33.clone.1), dimensions={1,2}, to_apply=%region_3.4 | reduce | flops 4064 | bytes 16516 | tf_op jit(solution)/shard_map/reduce_sum | solution.py:463
  80.2 0.1 select_reduce_fusion
  80.3 0.1 all_to_all.17
  80.5 22.7 %all_to_all.21 = f32[256,1,2]{2,1,0:T(1,128)S(1)} all-to-all(f32[256,1,2]{2,1,0:T(1,128)S(1)} %bitcast.90), channel_id=1, replica_groups=mesh['blk'=64,'par'=4] {'blk','par'}, dimensions={0} | all-to-all | bytes 4096 | tf_op jit(solution)/shard_map/all_to_all | solution.py:467
  103.2 0.3 reduce_sum.55
  103.4 0.5 multiply_divide_fusion
  (47 shorter events, 0.9 us)
Async XLA Ops:
  0.6 16.6 %copy-start = (s32[2048]{0:T(1024)S(1)}, s32[2048]{0:T(1024)}, u32[]{:S(2)}) copy-start(s32[2048]{0:T(1024)} %param.14) | copy-start | bytes 24580
  0.6 11.3 %copy-start.1 = (f32[32,8,1024]{2,1,0:T(8,128)S(1)}, f32[32,8,1024]{2,1,0:T(8,128)}, u32[]{:S(2)}) copy-start(f32[32,8,1024]{2,1,0:T(8,128)} %u_ref.3) | copy-start | bytes 3145732
  0.7 19.4 %collective-permute-start.1 = (f32[2]{0:T(128)}, f32[2]{0:T(128)S(1)}, u32[]{:S(2)}, u32[]{:S(2)}) collective-permute-start(f32[2]{0:T(128)} %param.13), channel_id=1, source_target_pairs={{0,2},{1,3},{2,0},{3,1},{4,6},{5,7},{6,4},{7,5},{8,10},{9,11},{10,... | collective-permute-start | bytes 32 | tf_op jit(solution)/shard_map/ppermute | solution.py:430
  4.3 15.8 %collective-permute-start = (f32[2]{0:T(128)}, f32[2]{0:T(128)S(1)}, u32[]{:S(2)}, u32[]{:S(2)}) collective-permute-start(f32[2]{0:T(128)} %param.13), channel_id=1, source_target_pairs={{0,1},{1,2},{2,3},{3,0},{4,5},{5,6},{6,7},{7,4},{8,9},{9,10},{10,1... | collective-permute-start | bytes 32 | tf_op jit(solution)/shard_map/ppermute | solution.py:430
  4.6 15.5 %collective-permute-start.2 = (f32[2]{0:T(128)}, f32[2]{0:T(128)S(1)}, u32[]{:S(2)}, u32[]{:S(2)}) collective-permute-start(f32[2]{0:T(128)} %param.13), channel_id=1, source_target_pairs={{0,3},{1,0},{2,1},{3,2},{4,7},{5,4},{6,5},{7,6},{8,11},{9,8},{10,9... | collective-permute-start | bytes 32 | tf_op jit(solution)/shard_map/ppermute | solution.py:430
  9.6 3.2 %copy-start.4 = (bf16[32,8,1024]{2,1,0:T(8,128)(2,1)S(1)}, bf16[32,8,1024]{2,1,0:T(8,128)(2,1)}, u32[]{:S(2)}) copy-start(bf16[32,8,1024]{2,1,0:T(8,128)(2,1)} %angle_ref.1) | copy-start | bytes 1572868
  10.4 3.1 %copy-start.3 = (s32[32,8,1024]{2,1,0:T(8,128)S(1)}, s32[32,8,1024]{2,1,0:T(8,128)}, u32[]{:S(2)}) copy-start(s32[32,8,1024]{2,1,0:T(8,128)} %tissue_ref.1) | copy-start | bytes 3145732
  18.4 1.7 %copy-start.6 = (f32[2]{0:T(128)S(1)}, f32[2]{0:T(128)}, u32[]{:S(2)}) copy-start(f32[2]{0:T(128)} %param.13) | copy-start | bytes 28
  20.9 16.5 %copy-start.2 = (bf16[32,8,1024]{2,1,0:T(8,128)(2,1)S(1)}, bf16[32,8,1024]{2,1,0:T(8,128)(2,1)}, u32[]{:S(2)}) copy-start(bf16[32,8,1024]{2,1,0:T(8,128)(2,1)} %l_ref.3) | copy-start | bytes 1572868
  22.4 36.8 %all-to-all-start = ((f32[64,1,3200]{2,1,0:T(1,128)}), f32[64,1,3200]{2,1,0:T(1,128)S(1)}, u32[]{:S(2)}, u32[]{:S(2)}) async-start(f32[64,1,3200]{2,1,0:T(1,128)} %all_to_all.14), calls=%async_computation | async-start | bytes 1638400 | tf_op jit(solution)/shard_map/all_to_all | solution.py:441
  38.1 17.4 %collective-permute-start.4 = (f32[32,3,1024]{2,1,0:T(4,128)S(1)}, f32[32,3,1024]{2,1,0:T(4,128)S(1)}, u32[]{:S(2)}, u32[]{:S(2)}) collective-permute-start(f32[32,3,1024]{2,1,0:T(4,128)S(1)} %pad_maximum_fusion.4), channel_id=1, source_target_pairs={{1,0},{2,1},{3,2},{5,4},{6,5},{7,6},{9,8},{10,9},{11,10},{13,12},{... | collective-permute-start | bytes 1179656 | tf_op jit(solution)/shard_map/ppermute | solution.py:455
  39.7 15.7 %collective-permute-start.3 = (f32[32,3,1024]{2,1,0:T(4,128)S(1)}, f32[32,3,1024]{2,1,0:T(4,128)S(1)}, u32[]{:S(2)}, u32[]{:S(2)}) collective-permute-start(f32[32,3,1024]{2,1,0:T(4,128)S(1)} %pad_maximum_fusion.3), channel_id=1, source_target_pairs={{0,1},{1,2},{2,3},{4,5},{5,6},{6,7},{8,9},{9,10},{10,11},{12,13},{... | collective-permute-start | bytes 1179656 | tf_op jit(solution)/shard_map/ppermute | solution.py:455
  66.5 13.7 %copy-start.5 = (s32[32]{0:T(128)S(1)}, s32[32]{0:T(128)}, u32[]{:S(2)}) copy-start(s32[32]{0:T(128)} %param.16) | copy-start | bytes 388

commit v7 on v6

--- a/solution.py
+++ b/solution.py
@@ -259,7 +259,7 @@
     lax.fori_loop(0, GROUP, one, 0)
 
 
-def outer_kernel(scale_ref, expand_ref, u_ref, l_ref, lu_ref, ll_ref, gx_ref, gy_ref, inner_ref, face_ref,
+def outer_kernel(cond_ref, cell_ref, own_ref, near_ref, expand_ref, u_ref, l_ref, lu_ref, ll_ref, gx_ref, gy_ref, inner_ref, face_ref,
                  halo_ref, u_out, l_out, part_out, ext_ref):
     g = pl.program_id(0)
     nz, cells = u_ref.shape[1], u_ref.shape[2]
@@ -287,7 +287,7 @@
 
     def one(i, carry):
         b = g * GROUP + i
-        th = scale_ref[b, 0]
+        th = cond_ref[own_ref[b]]
         u = u_ref[i]
         l = l_ref[i].astype(jnp.float32)
         gx = gx_ref[i]
@@ -314,7 +314,7 @@
             near_u = (ext[nz:2 * nz] + ext[3 * nz:4 * nz]) + ext[5 * nz:6 * nz]
             near_l = ext[6 * nz:7 * nz]
             g_self = gx if f < 2 else gy
-            conduct = jnp.where(masks[f], scale_ref[b, 1 + f] * (g_self * near_w), 0.0)
+            conduct = jnp.where(masks[f], cond_ref[cell_ref[near_ref[4 * b + f]]] * (g_self * near_w), 0.0)
             step_u = near_u - u
             step_l = conduct * (near_l - l)
             face_u = face_u + conduct * step_u
@@ -346,7 +346,7 @@
     )(tissue, angle, potential, sensitivity)
 
 
-def outer_step(scales, potential, sensitivity, inner, faces, halos, interpret=False):
+def outer_step(tables, potential, sensitivity, inner, faces, halos, interpret=False):
     bricks, nz, cells = potential.shape
     edge = faces.shape[-1]
     expand = expanders(edge, cells).astype(jnp.bfloat16)
@@ -355,8 +355,7 @@
     return pl.pallas_call(
         outer_kernel,
         grid=(bricks // GROUP,),
-        in_specs=[
-            pl.BlockSpec(memory_space=pltpu.SMEM),
+        in_specs=[pl.BlockSpec(memory_space=pltpu.SMEM) for _ in tables] + [
             pl.BlockSpec((4, edge, cells), lambda g: (0, 0, 0)),
             blk3(), blk3(), blk3(), blk3(), blk3(), blk3(),
             pl.BlockSpec((GROUP, 1, 128), lambda g: (g, 0, 0)),
@@ -372,7 +371,7 @@
         scratch_shapes=[pltpu.VMEM((4, GROUP * 8 * nz, cells), jnp.float32)],
         compiler_params=pltpu.CompilerParams(dimension_semantics=("parallel",)),
         interpret=interpret,
-    )(scales, expand, potential, sensitivity, lap_u, lap_l, gx, gy, inner_part, faces, halos)
+    )(*tables, expand, potential, sensitivity, lap_u, lap_l, gx, gy, inner_part, faces, halos)
 
 
 def body(
@@ -454,12 +453,8 @@
     initial = jnp.stack([tissue[:, 0].astype(jnp.float32), potential[:, 0], adjoint[:, 0]], axis=1)
     halos = jnp.concatenate([lax.ppermute(last, "par", up), lax.ppermute(initial, "par", down)], axis=1)
 
-    theta = cond_all[brick_cell]
-    theta_near = cond_all[cell_all[near_slot]]
-    scales = jnp.concatenate(
-        [theta[:, None], theta_near, jnp.zeros((bricks, 3), jnp.float32)], axis=1
-    )
-    final, adjoint, parts_out = outer_step(scales, potential, sensitivity, inner, faces, halos)
+    tables = (cond_all, cell_all, brick_cell, near_slot.reshape(-1))
+    final, adjoint, parts_out = outer_step(tables, potential, sensitivity, inner, faces, halos)
     brick_part = jnp.sum(parts_out, axis=(1, 2))
     onehot_cells = brick_cell[:, None] == jnp.arange(cell_count, dtype=jnp.int32)[None, :]
     shares = jnp.sum(jnp.where(onehot_cells, brick_part[:, None], 0.0), axis=0)

time: 104 us -> 101 us (0.971)
  local copies, waits for them, and re-layouts: 14.8 us -> 12.2 us
    gather x5 -> x0, local copies, waits for them, and re-layouts: 3.31 us -> none  [the longest x4 2.6 us: body(): theta_near = cond_all[cell_all[near_slot]]]
where the time goes in v7:
time: 101 us
  starting transfers between devices  25 us (25%)
  Pallas kernels  23.9 us (24%)
  blocking collectives  22.7 us (22%)
  local copies, waits for them, and re-layouts  12.2 us (12%)
  other arithmetic  9.63 us (10%)
  matrix products  3.59 us (4%)
  waiting for transfers between devices  2.82 us (3%)
  between operations  1.08 us (1%)
    all_to_all x1, blocking collectives, body(): lax.all_to_all(shares.reshape(devices, own_cells), ('blk', 'par'), split_...  22.7 us
    all_to_all x1, starting transfers between devices, body(): lax.all_to_all(sending, 'blk', split_axis=0, concat_axis=0, tiled=True)  13.2 us
    pallas_call x1, Pallas kernels, outer_step(): pl.pallas_call(outer_kernel, grid=(bricks // GROUP,), in_specs=[pl.BlockS...  12.7 us
    pallas_call x1, Pallas kernels, inner_step(): pl.pallas_call(inner_kernel, grid=(bricks // GROUP,), in_specs=[blk3(), b...  11.2 us
    ppermute x3, starting transfers between devices, body(): lax.ppermute(conductance, 'par', [(i, (i + s) % parts) for i in range(par...  6.32 us
    ppermute x1, starting transfers between devices, body(): lax.ppermute(last, 'par', up)  4.2 us
    dot_general x4, matrix products, boundary(): jnp.dot(values.astype(jnp.float32).reshape(bricks * z_layers, plane_cells...  3.59 us
    all_to_all x1, waiting for transfers between devices, body(): lax.all_to_all(sending, 'blk', split_axis=0, concat_axis=0, tiled=True)  2.81 us
  transfers between devices with their start and end apart: 6, of which 1 were waited for; matrix products, arithmetic and copies ran while one was open for 17% of the time, Pallas kernels for 11%

profile of v7, /device:TPU:1, one launch (start us, length us, event | category | flops | bytes accessed | tf_op | source)
XLA Modules:
  0.0 100.9 jit_solution(8052433354456893630)
XLA Ops:
  0.6 0.0 copy-start
  0.7 3.6 %collective-permute-start.1 = (f32[2]{0:T(128)}, f32[2]{0:T(128)S(1)}, u32[]{:S(2)}, u32[]{:S(2)}) collective-permute-start(f32[2]{0:T(128)} %param.13), channel_id=1, source_target_pairs={{0,2},{1,3},{2,0},{3,1},{4,6},{5,7},{6,4},{7,5},{8,10},{9,11},{10,... | collective-permute-start | bytes 32 | tf_op jit(solution)/shard_map/ppermute | solution.py:429
  4.3 0.3 collective-permute-start
  4.6 2.4 %collective-permute-start.2 = (f32[2]{0:T(128)}, f32[2]{0:T(128)S(1)}, u32[]{:S(2)}, u32[]{:S(2)}) collective-permute-start(f32[2]{0:T(128)} %param.13), channel_id=1, source_target_pairs={{0,3},{1,0},{2,1},{3,2},{4,7},{5,4},{6,5},{7,6},{8,11},{9,8},{10,9... | collective-permute-start | bytes 32 | tf_op jit(solution)/shard_map/ppermute | solution.py:429
  7.0 0.7 convert_element_type.38
  7.7 0.7 compare_select_fusion
  8.4 0.1 copy.26
  8.5 0.1 reshape.461
  8.6 0.7 add.160
  9.2 0.1 add.161
  9.3 0.1 iota_compare_fusion.2
  9.4 0.1 iota_compare_fusion
  9.6 0.8 fusion.21
  10.3 1.4 %convolution_bitcast_fusion = f32[256,128]{0,1:T(8,128)S(1)} fusion(pred[128,1024]{1,0:T(32,128)(4,1)S(1)} %bitcast.78, bf16[32,8,1024]{2,1,0:T(8,128)(2,1)} %l_ref.3), kind=kOutput, calls=%fused_computation.5 | convolution fusion | flops 67108864 | bytes 786432 | tf_op jit(solution)/shard_map/dot_general | solution.py:407
  11.8 0.1 copy.30
  11.9 0.7 convolution_bitcast_fusion.1
  12.6 0.1 copy.29
  12.7 0.7 fusion.1
  13.4 0.7 convolution_bitcast_fusion.2
  14.2 0.1 copy.27
  14.3 0.1 copy.28
  14.4 0.3 integer_pow.14
  14.7 0.4 fusion.12
  15.1 0.3 reshape.447
  15.3 0.3 reshape.450
  15.6 0.3 reshape.452
  15.9 0.3 fusion.5
  16.2 0.4 pad_maximum_fusion
  16.6 0.1 copy.31
  16.7 0.4 reshape.487
  17.2 1.1 %gather_fusion = s32[128]{0:T(128)S(1)} fusion(s32[2048]{0:T(1024)S(1)} %copy-done, s32[1024]{0:T(1024)S(1)} %pad_clamp_fusion.2), kind=kCustom, calls=%fused_computation | custom fusion | bytes 1536 | tf_op jit(solution)/shard_map/gather | solution.py:392
  18.4 0.2 convert_reduce_fusion
  18.6 1.2 %scatter_custom_fusion = f32[256,768]{1,0:T(8,128)S(1)} fusion(s32[128]{0:T(128)S(1)} %get-tuple-element.32, f32[128,768]{1,0:T(8,128)S(1)} %reshape.487, f32[]{:T(128)} %constant.36.clone.1), kind=kCustom, calls=%fused_computation.24 | custom fusion | bytes 786436 | tf_op jit(solution)/shard_map/scatter | solution.py:427
  19.8 0.2 reshape.454
  20.1 0.6 gather_fusion.1
  20.6 0.1 reshape.455
  20.7 0.1 fusion.13
  20.8 0.1 pad_maximum_fusion.2
  20.9 1.5 %all_to_all.14 = f32[64,1,3200]{2,1,0:T(1,128)} reshape(f32[64,3200]{1,0:T(8,128)S(1)} %pad_maximum_fusion.2) | data formatting | bytes 1638400 | tf_op jit(solution)/shard_map/all_to_all | solution.py:440
  22.3 13.2 %all-to-all-start = ((f32[64,1,3200]{2,1,0:T(1,128)}), f32[64,1,3200]{2,1,0:T(1,128)S(1)}, u32[]{:S(2)}, u32[]{:S(2)}) async-start(f32[64,1,3200]{2,1,0:T(1,128)} %all_to_all.14), calls=%async_computation | async-start | bytes 1638400 | tf_op jit(solution)/shard_map/all_to_all | solution.py:440
  35.5 1.8 %slice_convert_fusion.1 = (f32[32,1,1024]{2,1,0:T(1,128)S(1)}, f32[32,1,1024]{2,1,0:T(1,128)S(1)}) fusion(s32[32,8,1024]{2,1,0:T(8,128)} %tissue_ref.1), kind=kLoop, calls=%fused_computation.32 | loop fusion | flops 65536 | bytes 524288 | tf_op jit(solution)/shard_map/convert_element_type | solution.py:452
  37.3 0.3 fusion.22
  37.7 0.3 pad_maximum_fusion.4
  38.0 1.3 %collective-permute-start.4 = (f32[32,3,1024]{2,1,0:T(4,128)S(1)}, f32[32,3,1024]{2,1,0:T(4,128)S(1)}, u32[]{:S(2)}, u32[]{:S(2)}) collective-permute-start(f32[32,3,1024]{2,1,0:T(4,128)S(1)} %pad_maximum_fusion.4), channel_id=1, source_target_pairs={{1,0},{2,1},{3,2},{5,4},{6,5},{7,6},{9,8},{10,9},{11,10},{13,12},{... | collective-permute-start | bytes 1179656 | tf_op jit(solution)/shard_map/ppermute | solution.py:454
  39.3 0.3 pad_maximum_fusion.3
  39.7 4.2 %collective-permute-start.3 = (f32[32,3,1024]{2,1,0:T(4,128)S(1)}, f32[32,3,1024]{2,1,0:T(4,128)S(1)}, u32[]{:S(2)}, u32[]{:S(2)}) collective-permute-start(f32[32,3,1024]{2,1,0:T(4,128)S(1)} %pad_maximum_fusion.3), channel_id=1, source_target_pairs={{0,1},{1,2},{2,3},{4,5},{5,6},{6,7},{8,9},{9,10},{10,11},{12,13},{... | collective-permute-start | bytes 1179656 | tf_op jit(solution)/shard_map/ppermute | solution.py:454
  43.9 11.2 %shard_map.112 = (f32[32,8,1024]{2,1,0:T(8,128)}, f32[32,8,1024]{2,1,0:T(8,128)}, f32[32,8,1024]{2,1,0:T(8,128)}, f32[32,8,1024]{2,1,0:T(8,128)}, f32[32,1,128]{2,1,0:T(1,128)}) custom-call(s32[32,8,1024]{2,1,0:T(8,128)} %tissue_ref.1, bf16[32,8,1024]{2,1,0:T(8,128)(2,1)} %angle_ref.1, f32[32,8,1024]{2,1,0:T(8,128)} %u_ref.3, bf16[32,8,1024]{2,1,0:T(8,128)(2,1)} %l_ref.3), custom_call_target="tpu_custom_call" | custom-call | tf_op jit(solution)/shard_map/pallas_call | solution.py:338
  55.1 1.2 %pad_maximum_fusion.1.halo_ref = f32[32,6,1024]{2,1,0:T(8,128)} fusion(f32[32,3,1024]{2,1,0:T(4,128)S(1)} %collective-permute-done.4, f32[32,3,1024]{2,1,0:T(4,128)S(1)} %collective-permute-done.3), kind=kLoop, calls=%fused_computation.11 | loop fusion | flops 196608 | bytes 1572864 | tf_op jit(solution)/shard_map/concatenate | solution.py:454
  56.4 2.8 %all-to-all-done = f32[64,1,3200]{2,1,0:T(1,128)S(1)} async-done(((f32[64,1,3200]{2,1,0:T(1,128)}), f32[64,1,3200]{2,1,0:T(1,128)S(1)}, u32[]{:S(2)}, u32[]{:S(2)}) %all-to-all-start) | async-done | bytes 819232 | tf_op jit(solution)/shard_map/all_to_all | solution.py:440
  59.2 0.1 copy.35
  59.2 0.1 slice_convert_fusion.2
  59.3 0.1 slice.54
  59.4 0.7 convert_element_type.40.cell_ref
  60.0 0.7 reshape.456.cond_ref
  60.7 0.2 reshape.457
  60.9 0.8 gather_fusion.2
  61.8 1.6 %reshape.458.face_ref = f32[32,4,24,32]{3,2,1,0:T(8,128)} reshape(f32[128,768]{1,0:T(8,128)S(1)} %gather_fusion.2) | data formatting | bytes 786432 | tf_op jit(solution)/shard_map/reshape | solution.py:445
  63.4 12.7 %shard_map.113 = (f32[32,8,1024]{2,1,0:T(8,128)}, f32[32,8,1024]{2,1,0:T(8,128)}, f32[32,1,128]{2,1,0:T(1,128)}) custom-call(f32[512]{0:T(512)} %reshape.456.cond_ref, s32[2048]{0:T(1024)} %convert_element_type.40.cell_ref, s32[32]{0:T(128)} %own_ref.1, s32[128]{0:T(128)} %copy-done.5, bf16[4,32,1024]{2,1,0:T(8,128)(2,1)} %get-tuple-element.21.expand_ref, ...), custom_call_target="tpu_custom_call" | custom-call | tf_op jit(solution)/shard_map/pallas_call | solution.py:355
  76.1 1.0 %reduce_sum.53 = f32[32]{0:T(128)S(1)} reduce(f32[32,1,128]{2,1,0:T(1,128)} %get-tuple-element.18, f32[]{:T(128)} %constant.36.clone.1), dimensions={1,2}, to_apply=%region_3.4 | reduce | flops 4064 | bytes 16516 | tf_op jit(solution)/shard_map/reduce_sum | solution.py:458
  77.2 0.1 select_reduce_fusion
  77.3 0.1 all_to_all.17
  77.4 22.7 %all_to_all.21 = f32[256,1,2]{2,1,0:T(1,128)S(1)} all-to-all(f32[256,1,2]{2,1,0:T(1,128)S(1)} %bitcast.85), channel_id=1, replica_groups=mesh['blk'=64,'par'=4] {'blk','par'}, dimensions={0} | all-to-all | bytes 4096 | tf_op jit(solution)/shard_map/all_to_all | solution.py:462
  100.1 0.3 reduce_sum.55
  100.4 0.5 multiply_divide_fusion
  (32 shorter events, 0.1 us)
Async XLA Ops:
  0.6 16.5 %copy-start = (s32[2048]{0:T(1024)S(1)}, s32[2048]{0:T(1024)}, u32[]{:S(2)}) copy-start(s32[2048]{0:T(1024)} %param.14) | copy-start | bytes 24580
  0.6 11.2 %copy-start.1 = (f32[32,8,1024]{2,1,0:T(8,128)S(1)}, f32[32,8,1024]{2,1,0:T(8,128)}, u32[]{:S(2)}) copy-start(f32[32,8,1024]{2,1,0:T(8,128)} %u_ref.3) | copy-start | bytes 3145732
  0.7 19.3 %collective-permute-start.1 = (f32[2]{0:T(128)}, f32[2]{0:T(128)S(1)}, u32[]{:S(2)}, u32[]{:S(2)}) collective-permute-start(f32[2]{0:T(128)} %param.13), channel_id=1, source_target_pairs={{0,2},{1,3},{2,0},{3,1},{4,6},{5,7},{6,4},{7,5},{8,10},{9,11},{10,... | collective-permute-start | bytes 32 | tf_op jit(solution)/shard_map/ppermute | solution.py:429
  4.3 15.7 %collective-permute-start = (f32[2]{0:T(128)}, f32[2]{0:T(128)S(1)}, u32[]{:S(2)}, u32[]{:S(2)}) collective-permute-start(f32[2]{0:T(128)} %param.13), channel_id=1, source_target_pairs={{0,1},{1,2},{2,3},{3,0},{4,5},{5,6},{6,7},{7,4},{8,9},{9,10},{10,1... | collective-permute-start | bytes 32 | tf_op jit(solution)/shard_map/ppermute | solution.py:429
  4.6 15.4 %collective-permute-start.2 = (f32[2]{0:T(128)}, f32[2]{0:T(128)S(1)}, u32[]{:S(2)}, u32[]{:S(2)}) collective-permute-start(f32[2]{0:T(128)} %param.13), channel_id=1, source_target_pairs={{0,3},{1,0},{2,1},{3,2},{4,7},{5,4},{6,5},{7,6},{8,11},{9,8},{10,9... | collective-permute-start | bytes 32 | tf_op jit(solution)/shard_map/ppermute | solution.py:429
  9.5 3.2 %copy-start.4 = (bf16[32,8,1024]{2,1,0:T(8,128)(2,1)S(1)}, bf16[32,8,1024]{2,1,0:T(8,128)(2,1)}, u32[]{:S(2)}) copy-start(bf16[32,8,1024]{2,1,0:T(8,128)(2,1)} %angle_ref.1) | copy-start | bytes 1572868
  10.3 3.1 %copy-start.3 = (s32[32,8,1024]{2,1,0:T(8,128)S(1)}, s32[32,8,1024]{2,1,0:T(8,128)}, u32[]{:S(2)}) copy-start(s32[32,8,1024]{2,1,0:T(8,128)} %tissue_ref.1) | copy-start | bytes 3145732
  18.3 2.5 %copy-start.5 = (s32[128]{0:T(128)}, s32[128]{0:T(128)S(1)}, u32[]{:S(2)}) copy-start(s32[128]{0:T(128)S(1)} %gather_fusion) | copy-start | bytes 1540
  18.3 1.7 %copy-start.7 = (f32[2]{0:T(128)S(1)}, f32[2]{0:T(128)}, u32[]{:S(2)}) copy-start(f32[2]{0:T(128)} %param.13) | copy-start | bytes 28
  20.9 16.5 %copy-start.2 = (bf16[32,8,1024]{2,1,0:T(8,128)(2,1)S(1)}, bf16[32,8,1024]{2,1,0:T(8,128)(2,1)}, u32[]{:S(2)}) copy-start(bf16[32,8,1024]{2,1,0:T(8,128)(2,1)} %l_ref.3) | copy-start | bytes 1572868
  22.3 36.8 %all-to-all-start = ((f32[64,1,3200]{2,1,0:T(1,128)}), f32[64,1,3200]{2,1,0:T(1,128)S(1)}, u32[]{:S(2)}, u32[]{:S(2)}) async-start(f32[64,1,3200]{2,1,0:T(1,128)} %all_to_all.14), calls=%async_computation | async-start | bytes 1638400 | tf_op jit(solution)/shard_map/all_to_all | solution.py:440
  38.0 17.1 %collective-permute-start.4 = (f32[32,3,1024]{2,1,0:T(4,128)S(1)}, f32[32,3,1024]{2,1,0:T(4,128)S(1)}, u32[]{:S(2)}, u32[]{:S(2)}) collective-permute-start(f32[32,3,1024]{2,1,0:T(4,128)S(1)} %pad_maximum_fusion.4), channel_id=1, source_target_pairs={{1,0},{2,1},{3,2},{5,4},{6,5},{7,6},{9,8},{10,9},{11,10},{13,12},{... | collective-permute-start | bytes 1179656 | tf_op jit(solution)/shard_map/ppermute | solution.py:454
  39.7 15.4 %collective-permute-start.3 = (f32[32,3,1024]{2,1,0:T(4,128)S(1)}, f32[32,3,1024]{2,1,0:T(4,128)S(1)}, u32[]{:S(2)}, u32[]{:S(2)}) collective-permute-start(f32[32,3,1024]{2,1,0:T(4,128)S(1)} %pad_maximum_fusion.3), channel_id=1, source_target_pairs={{0,1},{1,2},{2,3},{4,5},{5,6},{6,7},{8,9},{9,10},{10,11},{12,13},{... | collective-permute-start | bytes 1179656 | tf_op jit(solution)/shard_map/ppermute | solution.py:454
  63.4 13.8 %copy-start.6 = (s32[32]{0:T(128)S(1)}, s32[32]{0:T(128)}, u32[]{:S(2)}) copy-start(s32[32]{0:T(128)} %own_ref.1) | copy-start | bytes 388

commit v8 on v7

--- a/solution.py
+++ b/solution.py
@@ -458,12 +458,16 @@
     brick_part = jnp.sum(parts_out, axis=(1, 2))
     onehot_cells = brick_cell[:, None] == jnp.arange(cell_count, dtype=jnp.int32)[None, :]
     shares = jnp.sum(jnp.where(onehot_cells, brick_part[:, None], 0.0), axis=0)
-    grad_share = jnp.sum(
+    column = jnp.sum(
         lax.all_to_all(
-            shares.reshape(devices, own_cells), ("blk", "par"), split_axis=0, concat_axis=0, tiled=True
+            shares.reshape(blocks, parts * own_cells), "blk", split_axis=0, concat_axis=0, tiled=True
         ),
         axis=0,
     )
+    summed = column
+    for s in range(1, parts):
+        summed = summed + lax.ppermute(column, "par", [(i, (i + s) % parts) for i in range(parts)])
+    grad_share = lax.dynamic_slice(summed, (lax.axis_index("par") * own_cells,), (own_cells,))
     cell_gradient = TIMESTEP * grad_share / (conductance * float(BX) ** 1.5)
     return (final, adjoint, cell_gradient)
 

time: 101 us -> 104 us (1.030)
  blocking collectives: 22.7 us -> 0 us
  waiting for transfers between devices: 2.82 us -> 15.9 us
  starting transfers between devices: 25 us -> 36.8 us
    all_to_all x1 -> x0, blocking collectives: 22.7 us -> none  [body(): lax.all_to_all(shares.reshape(devices, own_cells), ('blk', 'par'), split_...]
    all_to_all x0 -> x1, waiting for transfers between devices: none -> 9.4 us  [body(): lax.all_to_all(shares.reshape(blocks, parts * own_cells), 'blk', split_ax...]
    all_to_all x0 -> x1, starting transfers between devices: none -> 8.02 us  [body(): lax.all_to_all(shares.reshape(blocks, parts * own_cells), 'blk', split_ax...]
    ppermute x0 -> x3, starting transfers between devices: none -> 3.83 us  [body(): lax.ppermute(column, 'par', [(i, (i + s) % parts) for i in range(parts)])]
    ppermute x0 -> x3, waiting for transfers between devices: none -> 3.63 us  [body(): lax.ppermute(column, 'par', [(i, (i + s) % parts) for i in range(parts)])]
  transfers between devices with their start and end apart: 6 -> 10, of which waited for: 1 -> 4; matrix products, arithmetic and copies ran while one was open for 17% -> 16% of each run, Pallas kernels for 11% -> 11%
where the time goes in v8:
time: 104 us
  starting transfers between devices  36.8 us (35%)
  Pallas kernels  23.9 us (23%)
  waiting for transfers between devices  15.9 us (15%)
  local copies, waits for them, and re-layouts  12.8 us (12%)
  other arithmetic  9.5 us (9%)
  matrix products  3.59 us (3%)
  between operations  1.09 us (1%)
    all_to_all x1, starting transfers between devices, body(): lax.all_to_all(sending, 'blk', split_axis=0, concat_axis=0, tiled=True)  13.2 us
    pallas_call x1, Pallas kernels, outer_step(): pl.pallas_call(outer_kernel, grid=(bricks // GROUP,), in_specs=[pl.BlockS...  12.7 us
    pallas_call x1, Pallas kernels, inner_step(): pl.pallas_call(inner_kernel, grid=(bricks // GROUP,), in_specs=[blk3(), b...  11.2 us
    all_to_all x1, waiting for transfers between devices, body(): lax.all_to_all(shares.reshape(blocks, parts * own_cells), 'blk', split_ax...  9.4 us
    all_to_all x1, starting transfers between devices, body(): lax.all_to_all(shares.reshape(blocks, parts * own_cells), 'blk', split_ax...  8.02 us
    ppermute x3, starting transfers between devices, body(): lax.ppermute(conductance, 'par', [(i, (i + s) % parts) for i in range(par...  6.32 us
    ppermute x1, starting transfers between devices, body(): lax.ppermute(last, 'par', up)  4.2 us
    ppermute x3, starting transfers between devices, body(): lax.ppermute(column, 'par', [(i, (i + s) % parts) for i in range(parts)])  3.83 us
  transfers between devices with their start and end apart: 10, of which 4 were waited for; matrix products, arithmetic and copies ran while one was open for 16% of the time, Pallas kernels for 11%

profile of v8, /device:TPU:1, one launch (start us, length us, event | category | flops | bytes accessed | tf_op | source)
XLA Modules:
  0.0 103.5 jit_solution(960892401779418916)
XLA Ops:
  0.7 3.6 %collective-permute-start.1 = (f32[2]{0:T(128)}, f32[2]{0:T(128)S(1)}, u32[]{:S(2)}, u32[]{:S(2)}) collective-permute-start(f32[2]{0:T(128)} %param.13), channel_id=1, source_target_pairs={{0,2},{1,3},{2,0},{3,1},{4,6},{5,7},{6,4},{7,5},{8,10},{9,11},{10,... | collective-permute-start | bytes 32 | tf_op jit(solution)/shard_map/ppermute | solution.py:429
  4.3 0.3 collective-permute-start
  4.6 2.4 %collective-permute-start.2 = (f32[2]{0:T(128)}, f32[2]{0:T(128)S(1)}, u32[]{:S(2)}, u32[]{:S(2)}) collective-permute-start(f32[2]{0:T(128)} %param.13), channel_id=1, source_target_pairs={{0,3},{1,0},{2,1},{3,2},{4,7},{5,4},{6,5},{7,6},{8,11},{9,8},{10,9... | collective-permute-start | bytes 32 | tf_op jit(solution)/shard_map/ppermute | solution.py:429
  7.0 0.7 convert_element_type.38
  7.7 0.7 compare_select_fusion
  8.4 0.1 copy.26
  8.4 0.1 reshape.461
  8.6 0.7 add.172
  9.2 0.1 add.173
  9.3 0.1 iota_compare_fusion.2
  9.4 0.1 iota_compare_fusion
  9.6 0.8 fusion.21
  10.3 1.4 %convolution_bitcast_fusion = f32[256,128]{0,1:T(8,128)S(1)} fusion(pred[128,1024]{1,0:T(32,128)(4,1)S(1)} %bitcast.78, bf16[32,8,1024]{2,1,0:T(8,128)(2,1)} %l_ref.3), kind=kOutput, calls=%fused_computation.5 | convolution fusion | flops 67108864 | bytes 786432 | tf_op jit(solution)/shard_map/dot_general | solution.py:407
  11.8 0.1 copy.30
  11.9 0.7 convolution_bitcast_fusion.1
  12.6 0.1 copy.29
  12.7 0.7 fusion.1
  13.4 0.7 convolution_bitcast_fusion.2
  14.2 0.1 copy.27
  14.3 0.1 copy.28
  14.4 0.3 integer_pow.14
  14.7 0.4 fusion.12
  15.1 0.3 reshape.447
  15.3 0.3 reshape.450
  15.6 0.3 reshape.452
  15.9 0.3 fusion.5
  16.2 0.4 pad_maximum_fusion
  16.6 0.1 copy.31
  16.8 0.4 reshape.487
  17.2 1.1 %gather_fusion = s32[128]{0:T(128)S(1)} fusion(s32[2048]{0:T(1024)S(1)} %copy-done, s32[1024]{0:T(1024)S(1)} %pad_clamp_fusion.2), kind=kCustom, calls=%fused_computation | custom fusion | bytes 1536 | tf_op jit(solution)/shard_map/gather | solution.py:392
  18.4 0.2 convert_reduce_fusion
  18.6 1.2 %scatter_custom_fusion = f32[256,768]{1,0:T(8,128)S(1)} fusion(s32[128]{0:T(128)S(1)} %get-tuple-element.32, f32[128,768]{1,0:T(8,128)S(1)} %reshape.487, f32[]{:T(128)} %constant.36.clone.1), kind=kCustom, calls=%fused_computation.24 | custom fusion | bytes 786436 | tf_op jit(solution)/shard_map/scatter | solution.py:427
  19.8 0.2 reshape.454
  20.1 0.6 gather_fusion.1
  20.6 0.1 reshape.455
  20.7 0.1 fusion.13
  20.9 1.5 %all_to_all.14 = f32[64,1,3200]{2,1,0:T(1,128)} reshape(f32[64,3200]{1,0:T(8,128)S(1)} %pad_maximum_fusion.2) | data formatting | bytes 1638400 | tf_op jit(solution)/shard_map/all_to_all | solution.py:440
  22.3 13.2 %all-to-all-start = ((f32[64,1,3200]{2,1,0:T(1,128)}), f32[64,1,3200]{2,1,0:T(1,128)S(1)}, u32[]{:S(2)}, u32[]{:S(2)}) async-start(f32[64,1,3200]{2,1,0:T(1,128)} %all_to_all.14), calls=%async_computation | async-start | bytes 1638400 | tf_op jit(solution)/shard_map/all_to_all | solution.py:440
  35.5 1.8 %slice_convert_fusion.1 = (f32[32,1,1024]{2,1,0:T(1,128)S(1)}, f32[32,1,1024]{2,1,0:T(1,128)S(1)}) fusion(s32[32,8,1024]{2,1,0:T(8,128)} %tissue_ref.1), kind=kLoop, calls=%fused_computation.32 | loop fusion | flops 65536 | bytes 524288 | tf_op jit(solution)/shard_map/convert_element_type | solution.py:452
  37.4 0.3 fusion.22
  37.7 0.3 pad_maximum_fusion.4
  38.0 1.3 %collective-permute-start.4 = (f32[32,3,1024]{2,1,0:T(4,128)S(1)}, f32[32,3,1024]{2,1,0:T(4,128)S(1)}, u32[]{:S(2)}, u32[]{:S(2)}) collective-permute-start(f32[32,3,1024]{2,1,0:T(4,128)S(1)} %pad_maximum_fusion.4), channel_id=1, source_target_pairs={{1,0},{2,1},{3,2},{5,4},{6,5},{7,6},{9,8},{10,9},{11,10},{13,12},{... | collective-permute-start | bytes 1179656 | tf_op jit(solution)/shard_map/ppermute | solution.py:454
  39.3 0.3 pad_maximum_fusion.3
  39.7 4.2 %collective-permute-start.3 = (f32[32,3,1024]{2,1,0:T(4,128)S(1)}, f32[32,3,1024]{2,1,0:T(4,128)S(1)}, u32[]{:S(2)}, u32[]{:S(2)}) collective-permute-start(f32[32,3,1024]{2,1,0:T(4,128)S(1)} %pad_maximum_fusion.3), channel_id=1, source_target_pairs={{0,1},{1,2},{2,3},{4,5},{5,6},{6,7},{8,9},{9,10},{10,11},{12,13},{... | collective-permute-start | bytes 1179656 | tf_op jit(solution)/shard_map/ppermute | solution.py:454
  43.9 11.2 %shard_map.112 = (f32[32,8,1024]{2,1,0:T(8,128)}, f32[32,8,1024]{2,1,0:T(8,128)}, f32[32,8,1024]{2,1,0:T(8,128)}, f32[32,8,1024]{2,1,0:T(8,128)}, f32[32,1,128]{2,1,0:T(1,128)}) custom-call(s32[32,8,1024]{2,1,0:T(8,128)} %tissue_ref.1, bf16[32,8,1024]{2,1,0:T(8,128)(2,1)} %angle_ref.1, f32[32,8,1024]{2,1,0:T(8,128)} %u_ref.3, bf16[32,8,1024]{2,1,0:T(8,128)(2,1)} %l_ref.3), custom_call_target="tpu_custom_call" | custom-call | tf_op jit(solution)/shard_map/pallas_call | solution.py:338
  55.1 1.2 %pad_maximum_fusion.1.halo_ref = f32[32,6,1024]{2,1,0:T(8,128)} fusion(f32[32,3,1024]{2,1,0:T(4,128)S(1)} %collective-permute-done.4, f32[32,3,1024]{2,1,0:T(4,128)S(1)} %collective-permute-done.3), kind=kLoop, calls=%fused_computation.11 | loop fusion | flops 196608 | bytes 1572864 | tf_op jit(solution)/shard_map/concatenate | solution.py:454
  56.3 2.8 %all-to-all-done = f32[64,1,3200]{2,1,0:T(1,128)S(1)} async-done(((f32[64,1,3200]{2,1,0:T(1,128)}), f32[64,1,3200]{2,1,0:T(1,128)S(1)}, u32[]{:S(2)}, u32[]{:S(2)}) %all-to-all-start) | async-done | bytes 819232 | tf_op jit(solution)/shard_map/all_to_all | solution.py:440
  59.4 0.7 convert_element_type.40.cell_ref
  60.0 0.7 reshape.456.cond_ref
  60.7 0.2 reshape.457
  60.9 0.8 gather_fusion.2
  61.7 1.6 %reshape.458.face_ref = f32[32,4,24,32]{3,2,1,0:T(8,128)} reshape(f32[128,768]{1,0:T(8,128)S(1)} %gather_fusion.2) | data formatting | bytes 786432 | tf_op jit(solution)/shard_map/reshape | solution.py:445
  63.4 12.7 %shard_map.113 = (f32[32,8,1024]{2,1,0:T(8,128)}, f32[32,8,1024]{2,1,0:T(8,128)}, f32[32,1,128]{2,1,0:T(1,128)}) custom-call(f32[512]{0:T(512)} %reshape.456.cond_ref, s32[2048]{0:T(1024)} %convert_element_type.40.cell_ref, s32[32]{0:T(128)} %own_ref.1, s32[128]{0:T(128)} %copy-done.5, bf16[4,32,1024]{2,1,0:T(8,128)(2,1)} %get-tuple-element.21.expand_ref, ...), custom_call_target="tpu_custom_call" | custom-call | tf_op jit(solution)/shard_map/pallas_call | solution.py:355
  76.1 1.0 %reduce_sum.53 = f32[32]{0:T(128)S(1)} reduce(f32[32,1,128]{2,1,0:T(1,128)} %get-tuple-element.18, f32[]{:T(128)} %constant.36.clone.1), dimensions={1,2}, to_apply=%region_3.4 | reduce | flops 4064 | bytes 16516 | tf_op jit(solution)/shard_map/reduce_sum | solution.py:458
  77.2 0.1 select_reduce_fusion
  77.3 0.7 all_to_all.17
  78.0 8.0 %all-to-all-start.1 = ((f32[64,1,8]{2,1,0:T(1,128)}), f32[64,1,8]{2,1,0:T(1,128)S(1)}, u32[]{:S(2)}, u32[]{:S(2)}) async-start(f32[64,1,8]{2,1,0:T(1,128)} %bitcast.26), calls=%async_computation.1 | async-start | bytes 65536 | tf_op jit(solution)/shard_map/all_to_all | solution.py:462
  86.0 9.4 %all-to-all-done.1 = f32[64,1,8]{2,1,0:T(1,128)S(1)} async-done(((f32[64,1,8]{2,1,0:T(1,128)}), f32[64,1,8]{2,1,0:T(1,128)S(1)}, u32[]{:S(2)}, u32[]{:S(2)}) %all-to-all-start.1) | async-done | bytes 2080 | tf_op jit(solution)/shard_map/all_to_all | solution.py:462
  95.4 0.1 reduce_sum.55
  95.5 0.3 collective-permute-start.7
  95.8 3.5 %collective-permute-start.6 = (f32[8]{0:T(128)S(1)}, f32[8]{0:T(128)S(1)}, u32[]{:S(2)}, u32[]{:S(2)}) collective-permute-start(f32[8]{0:T(128)S(1)} %reduce_sum.55), channel_id=1, source_target_pairs={{0,2},{1,3},{2,0},{3,1},{4,6},{5,7},{6,4},{7,5},{8,10},{9,11},{10,... | collective-permute-start | bytes 104 | tf_op jit(solution)/shard_map/ppermute | solution.py:469
  99.3 0.9 collective-permute-done.6
  100.3 2.7 %collective-permute-done.5 = f32[8]{0:T(128)S(1)} collective-permute-done((f32[8]{0:T(128)S(1)}, f32[8]{0:T(128)S(1)}, u32[]{:S(2)}, u32[]{:S(2)}) %collective-permute-start.5) | collective-permute-done | bytes 64 | tf_op jit(solution)/shard_map/ppermute | solution.py:469
  103.0 0.6 multiply_divide_fusion
  (40 shorter events, 0.4 us)
Async XLA Ops:
  0.6 16.5 %copy-start = (s32[2048]{0:T(1024)S(1)}, s32[2048]{0:T(1024)}, u32[]{:S(2)}) copy-start(s32[2048]{0:T(1024)} %param.14) | copy-start | bytes 24580
  0.6 11.2 %copy-start.1 = (f32[32,8,1024]{2,1,0:T(8,128)S(1)}, f32[32,8,1024]{2,1,0:T(8,128)}, u32[]{:S(2)}) copy-start(f32[32,8,1024]{2,1,0:T(8,128)} %u_ref.3) | copy-start | bytes 3145732
  0.7 19.4 %collective-permute-start.1 = (f32[2]{0:T(128)}, f32[2]{0:T(128)S(1)}, u32[]{:S(2)}, u32[]{:S(2)}) collective-permute-start(f32[2]{0:T(128)} %param.13), channel_id=1, source_target_pairs={{0,2},{1,3},{2,0},{3,1},{4,6},{5,7},{6,4},{7,5},{8,10},{9,11},{10,... | collective-permute-start | bytes 32 | tf_op jit(solution)/shard_map/ppermute | solution.py:429
  4.3 15.7 %collective-permute-start = (f32[2]{0:T(128)}, f32[2]{0:T(128)S(1)}, u32[]{:S(2)}, u32[]{:S(2)}) collective-permute-start(f32[2]{0:T(128)} %param.13), channel_id=1, source_target_pairs={{0,1},{1,2},{2,3},{3,0},{4,5},{5,6},{6,7},{7,4},{8,9},{9,10},{10,1... | collective-permute-start | bytes 32 | tf_op jit(solution)/shard_map/ppermute | solution.py:429
  4.6 15.4 %collective-permute-start.2 = (f32[2]{0:T(128)}, f32[2]{0:T(128)S(1)}, u32[]{:S(2)}, u32[]{:S(2)}) collective-permute-start(f32[2]{0:T(128)} %param.13), channel_id=1, source_target_pairs={{0,3},{1,0},{2,1},{3,2},{4,7},{5,4},{6,5},{7,6},{8,11},{9,8},{10,9... | collective-permute-start | bytes 32 | tf_op jit(solution)/shard_map/ppermute | solution.py:429
  9.5 3.2 %copy-start.4 = (bf16[32,8,1024]{2,1,0:T(8,128)(2,1)S(1)}, bf16[32,8,1024]{2,1,0:T(8,128)(2,1)}, u32[]{:S(2)}) copy-start(bf16[32,8,1024]{2,1,0:T(8,128)(2,1)} %angle_ref.1) | copy-start | bytes 1572868
  10.3 3.1 %copy-start.3 = (s32[32,8,1024]{2,1,0:T(8,128)S(1)}, s32[32,8,1024]{2,1,0:T(8,128)}, u32[]{:S(2)}) copy-start(s32[32,8,1024]{2,1,0:T(8,128)} %tissue_ref.1) | copy-start | bytes 3145732
  18.3 2.5 %copy-start.5 = (s32[128]{0:T(128)}, s32[128]{0:T(128)S(1)}, u32[]{:S(2)}) copy-start(s32[128]{0:T(128)S(1)} %gather_fusion) | copy-start | bytes 1540
  18.3 1.7 %copy-start.7 = (f32[2]{0:T(128)S(1)}, f32[2]{0:T(128)}, u32[]{:S(2)}) copy-start(f32[2]{0:T(128)} %param.13) | copy-start | bytes 28
  20.9 16.5 %copy-start.2 = (bf16[32,8,1024]{2,1,0:T(8,128)(2,1)S(1)}, bf16[32,8,1024]{2,1,0:T(8,128)(2,1)}, u32[]{:S(2)}) copy-start(bf16[32,8,1024]{2,1,0:T(8,128)(2,1)} %l_ref.3) | copy-start | bytes 1572868
  22.3 36.8 %all-to-all-start = ((f32[64,1,3200]{2,1,0:T(1,128)}), f32[64,1,3200]{2,1,0:T(1,128)S(1)}, u32[]{:S(2)}, u32[]{:S(2)}) async-start(f32[64,1,3200]{2,1,0:T(1,128)} %all_to_all.14), calls=%async_computation | async-start | bytes 1638400 | tf_op jit(solution)/shard_map/all_to_all | solution.py:440
  38.0 17.0 %collective-permute-start.4 = (f32[32,3,1024]{2,1,0:T(4,128)S(1)}, f32[32,3,1024]{2,1,0:T(4,128)S(1)}, u32[]{:S(2)}, u32[]{:S(2)}) collective-permute-start(f32[32,3,1024]{2,1,0:T(4,128)S(1)} %pad_maximum_fusion.4), channel_id=1, source_target_pairs={{1,0},{2,1},{3,2},{5,4},{6,5},{7,6},{9,8},{10,9},{11,10},{13,12},{... | collective-permute-start | bytes 1179656 | tf_op jit(solution)/shard_map/ppermute | solution.py:454
  39.7 15.4 %collective-permute-start.3 = (f32[32,3,1024]{2,1,0:T(4,128)S(1)}, f32[32,3,1024]{2,1,0:T(4,128)S(1)}, u32[]{:S(2)}, u32[]{:S(2)}) collective-permute-start(f32[32,3,1024]{2,1,0:T(4,128)S(1)} %pad_maximum_fusion.3), channel_id=1, source_target_pairs={{0,1},{1,2},{2,3},{4,5},{5,6},{6,7},{8,9},{9,10},{10,11},{12,13},{... | collective-permute-start | bytes 1179656 | tf_op jit(solution)/shard_map/ppermute | solution.py:454
  63.4 13.8 %copy-start.6 = (s32[32]{0:T(128)S(1)}, s32[32]{0:T(128)}, u32[]{:S(2)}) copy-start(s32[32]{0:T(128)} %own_ref.1) | copy-start | bytes 388
  78.0 17.4 %all-to-all-start.1 = ((f32[64,1,8]{2,1,0:T(1,128)}), f32[64,1,8]{2,1,0:T(1,128)S(1)}, u32[]{:S(2)}, u32[]{:S(2)}) async-start(f32[64,1,8]{2,1,0:T(1,128)} %bitcast.26), calls=%async_computation.1 | async-start | bytes 65536 | tf_op jit(solution)/shard_map/all_to_all | solution.py:462
  95.5 3.8 %collective-permute-start.7 = (f32[8]{0:T(128)S(1)}, f32[8]{0:T(128)S(1)}, u32[]{:S(2)}, u32[]{:S(2)}) collective-permute-start(f32[8]{0:T(128)S(1)} %reduce_sum.55), channel_id=1, source_target_pairs={{0,3},{1,0},{2,1},{3,2},{4,7},{5,4},{6,5},{7,6},{8,11},{9,8},{10,9... | collective-permute-start | bytes 104 | tf_op jit(solution)/shard_map/ppermute | solution.py:469
  95.8 4.5 %collective-permute-start.6 = (f32[8]{0:T(128)S(1)}, f32[8]{0:T(128)S(1)}, u32[]{:S(2)}, u32[]{:S(2)}) collective-permute-start(f32[8]{0:T(128)S(1)} %reduce_sum.55), channel_id=1, source_target_pairs={{0,2},{1,3},{2,0},{3,1},{4,6},{5,7},{6,4},{7,5},{8,10},{9,11},{10,... | collective-permute-start | bytes 104 | tf_op jit(solution)/shard_map/ppermute | solution.py:469
  99.3 3.6 %collective-permute-start.5 = (f32[8]{0:T(128)S(1)}, f32[8]{0:T(128)S(1)}, u32[]{:S(2)}, u32[]{:S(2)}) collective-permute-start(f32[8]{0:T(128)S(1)} %reduce_sum.55), channel_id=1, source_target_pairs={{0,1},{1,2},{2,3},{3,0},{4,5},{5,6},{6,7},{7,4},{8,9},{9,10},{10,1... | collective-permute-start | bytes 104 | tf_op jit(solution)/shard_map/ppermute | solution.py:469

commit v9 on v7

--- a/solution.py
+++ b/solution.py
@@ -265,8 +265,15 @@
     nz, cells = u_ref.shape[1], u_ref.shape[2]
     edge = BX
     rows = 8 * nz
+    layer = nz * edge
+    spread = lax.broadcasted_iota(jnp.int32, (nz, layer), 1) // edge == lax.broadcasted_iota(
+        jnp.int32, (nz, layer), 0
+    )
     for f in range(4):
-        face = face_ref[:, f]
+        flat = face_ref[:, f]
+        face = jnp.concatenate(
+            [jnp.where(spread[None], flat[:, None, k * layer:(k + 1) * layer], 0.0) for k in range(3)], axis=1
+        )
         part = face[:, :2 * nz]
         high = part.astype(jnp.bfloat16).astype(jnp.float32)
         rest = part - high
@@ -276,7 +283,7 @@
             [high, middle, low, face[:, 2 * nz:3 * nz], jnp.zeros_like(face[:, :nz])], axis=1
         )
         ext_ref[f] = jnp.dot(
-            stacked.reshape(GROUP * rows, edge).astype(jnp.bfloat16),
+            stacked.reshape(GROUP * rows, layer).astype(jnp.bfloat16),
             expand_ref[f],
             preferred_element_type=jnp.float32,
         )
@@ -349,17 +356,18 @@
 def outer_step(tables, potential, sensitivity, inner, faces, halos, interpret=False):
     bricks, nz, cells = potential.shape
     edge = faces.shape[-1]
-    expand = expanders(edge, cells).astype(jnp.bfloat16)
+    edge = BX
+    expand = jnp.tile(expanders(edge, cells), (1, nz, 1)).astype(jnp.bfloat16)
     blk3 = lambda: pl.BlockSpec((GROUP, nz, cells), lambda g: (g, 0, 0))
     lap_u, lap_l, gx, gy, inner_part = inner
     return pl.pallas_call(
         outer_kernel,
         grid=(bricks // GROUP,),
         in_specs=[pl.BlockSpec(memory_space=pltpu.SMEM) for _ in tables] + [
-            pl.BlockSpec((4, edge, cells), lambda g: (0, 0, 0)),
+            pl.BlockSpec((4, nz * edge, cells), lambda g: (0, 0, 0)),
             blk3(), blk3(), blk3(), blk3(), blk3(), blk3(),
             pl.BlockSpec((GROUP, 1, 128), lambda g: (g, 0, 0)),
-            pl.BlockSpec((GROUP, 4, faces.shape[2], edge), lambda g: (g, 0, 0, 0)),
+            pl.BlockSpec((GROUP, 4, faces.shape[2]), lambda g: (g, 0, 0)),
             pl.BlockSpec((GROUP, 6, cells), lambda g: (g, 0, 0)),
         ],
         out_specs=[blk3(), blk3(), pl.BlockSpec((GROUP, 1, 128), lambda g: (g, 0, 0))],
@@ -443,7 +451,7 @@
     cond_all = arrived[:, width : width + par_cells].reshape(-1)
     cell_all = arrived[:, width + par_cells : width + par_cells + bricks].reshape(-1).astype(jnp.int32)
     faces = received.reshape(blocks * capacity, 3 * face_cells)[recv_slot].reshape(
-        bricks, 4, 3 * z_layers, brick_edge
+        bricks, 4, 3 * face_cells
     )
 
     size = lax.axis_size("par")

time: 101 us -> 105 us (1.040)
  local copies, waits for them, and re-layouts: 12.2 us -> 13.6 us
    another operation x0 -> x1, local copies, waits for them, and re-layouts: none -> 1.6 us  [outer_step(): expand = jnp.tile(expanders(edge, cells), (1, nz, 1)).astype(jnp.bfloat16)]
where the time goes in v9:
time: 105 us; the launch traced here: 104 us
  starting transfers between devices  25 us (24%)
  Pallas kernels  24.6 us (23%)
  blocking collectives  22.7 us (22%)
  local copies, waits for them, and re-layouts  13.6 us (13%)
  other arithmetic  10.1 us (10%)
  matrix products  4.26 us (4%)
  waiting for transfers between devices  2.82 us (3%)
  between operations  1.1 us (1%)
    all_to_all x1, blocking collectives, body(): lax.all_to_all(shares.reshape(devices, own_cells), ('blk', 'par'), split_...  22.7 us
    pallas_call x1, Pallas kernels, outer_step(): pl.pallas_call(outer_kernel, grid=(bricks // GROUP,), in_specs=[pl.BlockS...  13.4 us
    all_to_all x1, starting transfers between devices, body(): lax.all_to_all(sending, 'blk', split_axis=0, concat_axis=0, tiled=True)  13.2 us
    pallas_call x1, Pallas kernels, inner_step(): pl.pallas_call(inner_kernel, grid=(bricks // GROUP,), in_specs=[blk3(), b...  11.2 us
    ppermute x3, starting transfers between devices, body(): lax.ppermute(conductance, 'par', [(i, (i + s) % parts) for i in range(par...  6.32 us
    dot_general x4, matrix products, boundary(): jnp.dot(values.astype(jnp.float32).reshape(bricks * z_layers, plane_cells...  4.26 us
    ppermute x1, starting transfers between devices, body(): lax.ppermute(last, 'par', up)  4.2 us
    all_to_all x1, waiting for transfers between devices, body(): lax.all_to_all(sending, 'blk', split_axis=0, concat_axis=0, tiled=True)  2.81 us
  transfers between devices with their start and end apart: 6, of which 1 were waited for; matrix products, arithmetic and copies ran while one was open for 17% of the time, Pallas kernels for 11%

profile of v9, /device:TPU:1, one launch (start us, length us, event | category | flops | bytes accessed | tf_op | source)
XLA Modules:
  0.0 104.1 jit_solution(13866213303316696083)
XLA Ops:
  0.7 3.6 %collective-permute-start.1 = (f32[2]{0:T(128)}, f32[2]{0:T(128)}, u32[]{:S(2)}, u32[]{:S(2)}) collective-permute-start(f32[2]{0:T(128)} %param.13), channel_id=1, source_target_pairs={{0,2},{1,3},{2,0},{3,1},{4,6},{5,7},{6,4},{7,5},{8,10},{9,11},{10,... | collective-permute-start | bytes 32 | tf_op jit(solution)/shard_map/ppermute | solution.py:437
  4.3 0.3 collective-permute-start
  4.6 2.4 %collective-permute-start.2 = (f32[2]{0:T(128)}, f32[2]{0:T(128)}, u32[]{:S(2)}, u32[]{:S(2)}) collective-permute-start(f32[2]{0:T(128)} %param.13), channel_id=1, source_target_pairs={{0,3},{1,0},{2,1},{3,2},{4,7},{5,4},{6,5},{7,6},{8,11},{9,8},{10,9... | collective-permute-start | bytes 32 | tf_op jit(solution)/shard_map/ppermute | solution.py:437
  7.0 1.2 %convert_element_type.40 = f32[32]{0:T(128)} convert(s32[32]{0:T(128)} %own_ref.1) | non-fusion elementwise | flops 32 | bytes 256 | tf_op jit(solution)/shard_map/convert_element_type | solution.py:441
  8.2 0.7 compare_select_fusion
  8.9 0.1 copy.26
  9.0 0.1 reshape.466
  9.1 0.7 add.160
  9.7 0.6 add.161
  10.4 0.1 iota_compare_fusion.2
  10.5 0.1 iota_compare_fusion
  10.6 0.1 fusion.21
  10.7 1.5 %convolution_bitcast_fusion = f32[256,128]{0,1:T(8,128)S(1)} fusion(pred[128,1024]{1,0:T(32,128)(4,1)S(1)} %bitcast.80, bf16[32,8,1024]{2,1,0:T(8,128)(2,1)} %l_ref.3), kind=kOutput, calls=%fused_computation.5 | convolution fusion | flops 67108864 | bytes 786432 | tf_op jit(solution)/shard_map/dot_general | solution.py:415
  12.1 0.1 copy.30
  12.2 0.7 convolution_bitcast_fusion.1
  13.0 0.1 copy.29
  13.1 1.4 %fusion.1 = f32[256,128]{0,1:T(8,128)} fusion(pred[128,1024]{1,0:T(32,128)(4,1)S(1)} %bitcast.82, bf16[32,8,1024]{2,1,0:T(8,128)(2,1)S(1)} %copy-done.4), kind=kOutput, calls=%fused_computation.8 | convolution fusion | flops 67141632 | bytes 786432 | tf_op jit(solution)/shard_map/dot_general | solution.py:415
  14.4 0.7 convolution_bitcast_fusion.2
  15.2 0.1 copy.27
  15.3 0.1 copy-done.6
  15.3 0.1 copy.28
  15.4 0.3 integer_pow.14
  15.7 0.4 fusion.12
  16.1 0.3 reshape.452
  16.4 0.3 reshape.455
  16.6 0.3 reshape.457
  16.9 0.3 fusion.5
  17.3 0.4 pad_maximum_fusion
  17.7 0.1 copy.31
  17.8 0.4 reshape.492
  18.2 1.1 %gather_fusion = s32[128]{0:T(128)S(1)} fusion(s32[2048]{0:T(1024)S(1)} %copy-done, s32[1024]{0:T(1024)S(1)} %pad_clamp_fusion.2), kind=kCustom, calls=%fused_computation | custom fusion | bytes 1536 | tf_op jit(solution)/shard_map/gather | solution.py:400
  19.4 0.2 convert_reduce_fusion
  19.6 1.2 %scatter_custom_fusion = f32[256,768]{1,0:T(8,128)S(1)} fusion(s32[128]{0:T(128)S(1)} %get-tuple-element.32, f32[128,768]{1,0:T(8,128)S(1)} %reshape.492, f32[]{:T(128)} %constant.36.clone.1), kind=kCustom, calls=%fused_computation.24 | custom fusion | bytes 786436 | tf_op jit(solution)/shard_map/scatter | solution.py:435
  20.9 0.2 reshape.459
  21.1 0.7 pad_maximum_fusion.5
  21.8 0.6 gather_fusion.1
  22.3 0.1 reshape.460
  22.4 0.1 fusion.13
  22.5 0.1 pad_maximum_fusion.2
  22.6 1.5 %all_to_all.14 = f32[64,1,3200]{2,1,0:T(1,128)} reshape(f32[64,3200]{1,0:T(8,128)S(1)} %pad_maximum_fusion.2) | data formatting | bytes 1638400 | tf_op jit(solution)/shard_map/all_to_all | solution.py:448
  24.1 13.2 %all-to-all-start = ((f32[64,1,3200]{2,1,0:T(1,128)}), f32[64,1,3200]{2,1,0:T(1,128)S(1)}, u32[]{:S(2)}, u32[]{:S(2)}) async-start(f32[64,1,3200]{2,1,0:T(1,128)} %all_to_all.14), calls=%async_computation | async-start | bytes 1638400 | tf_op jit(solution)/shard_map/all_to_all | solution.py:448
  37.2 1.8 %slice_convert_fusion.1 = (f32[32,1,1024]{2,1,0:T(1,128)S(1)}, f32[32,1,1024]{2,1,0:T(1,128)S(1)}) fusion(s32[32,8,1024]{2,1,0:T(8,128)} %tissue_ref.1), kind=kLoop, calls=%fused_computation.32 | loop fusion | flops 65536 | bytes 524288 | tf_op jit(solution)/shard_map/convert_element_type | solution.py:460
  39.1 0.3 fusion.22
  39.4 0.3 pad_maximum_fusion.4
  39.8 1.3 %collective-permute-start.4 = (f32[32,3,1024]{2,1,0:T(4,128)S(1)}, f32[32,3,1024]{2,1,0:T(4,128)S(1)}, u32[]{:S(2)}, u32[]{:S(2)}) collective-permute-start(f32[32,3,1024]{2,1,0:T(4,128)S(1)} %pad_maximum_fusion.4), channel_id=1, source_target_pairs={{1,0},{2,1},{3,2},{5,4},{6,5},{7,6},{9,8},{10,9},{11,10},{13,12},{... | collective-permute-start | bytes 1179656 | tf_op jit(solution)/shard_map/ppermute | solution.py:462
  41.1 0.3 pad_maximum_fusion.3
  41.4 4.2 %collective-permute-start.3 = (f32[32,3,1024]{2,1,0:T(4,128)S(1)}, f32[32,3,1024]{2,1,0:T(4,128)S(1)}, u32[]{:S(2)}, u32[]{:S(2)}) collective-permute-start(f32[32,3,1024]{2,1,0:T(4,128)S(1)} %pad_maximum_fusion.3), channel_id=1, source_target_pairs={{0,1},{1,2},{2,3},{4,5},{5,6},{6,7},{8,9},{9,10},{10,11},{12,13},{... | collective-permute-start | bytes 1179656 | tf_op jit(solution)/shard_map/ppermute | solution.py:462
  45.6 11.2 %shard_map.112 = (f32[32,8,1024]{2,1,0:T(8,128)}, f32[32,8,1024]{2,1,0:T(8,128)}, f32[32,8,1024]{2,1,0:T(8,128)}, f32[32,8,1024]{2,1,0:T(8,128)}, f32[32,1,128]{2,1,0:T(1,128)}) custom-call(s32[32,8,1024]{2,1,0:T(8,128)} %tissue_ref.1, bf16[32,8,1024]{2,1,0:T(8,128)(2,1)} %angle_ref.1, f32[32,8,1024]{2,1,0:T(8,128)} %u_ref.3, bf16[32,8,1024]{2,1,0:T(8,128)(2,1)} %l_ref.3), custom_call_target="tpu_custom_call" | custom-call | tf_op jit(solution)/shard_map/pallas_call | solution.py:345
  56.8 1.2 %pad_maximum_fusion.1.halo_ref = f32[32,6,1024]{2,1,0:T(8,128)} fusion(f32[32,3,1024]{2,1,0:T(4,128)S(1)} %collective-permute-done.4, f32[32,3,1024]{2,1,0:T(4,128)S(1)} %collective-permute-done.3), kind=kLoop, calls=%fused_computation.11 | loop fusion | flops 196608 | bytes 1572864 | tf_op jit(solution)/shard_map/concatenate | solution.py:462
  58.1 2.8 %all-to-all-done = f32[64,1,3200]{2,1,0:T(1,128)S(1)} async-done(((f32[64,1,3200]{2,1,0:T(1,128)}), f32[64,1,3200]{2,1,0:T(1,128)S(1)}, u32[]{:S(2)}, u32[]{:S(2)}) %all-to-all-start) | async-done | bytes 819232 | tf_op jit(solution)/shard_map/all_to_all | solution.py:448
  60.9 0.1 slice_convert_fusion.2
  61.1 0.7 convert_element_type.42.cell_ref
  61.8 0.7 reshape.461.cond_ref
  62.4 0.2 reshape.462
  62.7 0.8 gather_fusion.2
  63.5 0.8 reshape.463.face_ref
  64.3 1.6 %tile.2 = bf16[4,8,32,1024]{3,2,1,0:T(8,128)(2,1)} broadcast(bf16[4,32,1024]{2,1,0:T(8,128)(2,1)S(1)} %get-tuple-element.21), dimensions={0,2,3} | broadcast | bytes 2359296 | tf_op jit(solution)/shard_map/tile | solution.py:360
  65.9 13.4 %shard_map.113 = (f32[32,8,1024]{2,1,0:T(8,128)}, f32[32,8,1024]{2,1,0:T(8,128)}, f32[32,1,128]{2,1,0:T(1,128)}) custom-call(f32[512]{0:T(512)} %reshape.461.cond_ref, s32[2048]{0:T(1024)} %convert_element_type.42.cell_ref, s32[32]{0:T(128)} %own_ref.1, s32[128]{0:T(128)} %copy-done.5, bf16[4,256,1024]{2,1,0:T(8,128)(2,1)} %bitcast.76, ...), custom_call_target="tpu_custom_call" | custom-call | tf_op jit(solution)/shard_map/pallas_call | solution.py:363
  79.3 1.0 reduce_sum.53
  80.4 0.1 select_reduce_fusion
  80.5 0.1 all_to_all.17
  80.6 22.7 %all_to_all.21 = f32[256,1,2]{2,1,0:T(1,128)S(1)} all-to-all(f32[256,1,2]{2,1,0:T(1,128)S(1)} %bitcast.87), channel_id=1, replica_groups=mesh['blk'=64,'par'=4] {'blk','par'}, dimensions={0} | all-to-all | bytes 4096 | tf_op jit(solution)/shard_map/all_to_all | solution.py:470
  103.3 0.3 reduce_sum.55
  103.6 0.5 multiply_divide_fusion
  (39 shorter events, 0.3 us)
Async XLA Ops:
  0.6 17.6 %copy-start = (s32[2048]{0:T(1024)S(1)}, s32[2048]{0:T(1024)}, u32[]{:S(2)}) copy-start(s32[2048]{0:T(1024)} %param.14) | copy-start | bytes 24580
  0.6 11.6 %copy-start.1 = (f32[32,8,1024]{2,1,0:T(8,128)S(1)}, f32[32,8,1024]{2,1,0:T(8,128)}, u32[]{:S(2)}) copy-start(f32[32,8,1024]{2,1,0:T(8,128)} %u_ref.3) | copy-start | bytes 3145732
  0.7 20.4 %collective-permute-start.1 = (f32[2]{0:T(128)}, f32[2]{0:T(128)}, u32[]{:S(2)}, u32[]{:S(2)}) collective-permute-start(f32[2]{0:T(128)} %param.13), channel_id=1, source_target_pairs={{0,2},{1,3},{2,0},{3,1},{4,6},{5,7},{6,4},{7,5},{8,10},{9,11},{10,... | collective-permute-start | bytes 32 | tf_op jit(solution)/shard_map/ppermute | solution.py:437
  4.3 16.8 %collective-permute-start = (f32[2]{0:T(128)}, f32[2]{0:T(128)}, u32[]{:S(2)}, u32[]{:S(2)}) collective-permute-start(f32[2]{0:T(128)} %param.13), channel_id=1, source_target_pairs={{0,1},{1,2},{2,3},{3,0},{4,5},{5,6},{6,7},{7,4},{8,9},{9,10},{10,1... | collective-permute-start | bytes 32 | tf_op jit(solution)/shard_map/ppermute | solution.py:437
  4.6 16.5 %collective-permute-start.2 = (f32[2]{0:T(128)}, f32[2]{0:T(128)}, u32[]{:S(2)}, u32[]{:S(2)}) collective-permute-start(f32[2]{0:T(128)} %param.13), channel_id=1, source_target_pairs={{0,3},{1,0},{2,1},{3,2},{4,7},{5,4},{6,5},{7,6},{8,11},{9,8},{10,9... | collective-permute-start | bytes 32 | tf_op jit(solution)/shard_map/ppermute | solution.py:437
  10.6 2.5 %copy-start.4 = (bf16[32,8,1024]{2,1,0:T(8,128)(2,1)S(1)}, bf16[32,8,1024]{2,1,0:T(8,128)(2,1)}, u32[]{:S(2)}) copy-start(bf16[32,8,1024]{2,1,0:T(8,128)(2,1)} %angle_ref.1) | copy-start | bytes 1572868
  10.7 3.8 %copy-start.3 = (s32[32,8,1024]{2,1,0:T(8,128)S(1)}, s32[32,8,1024]{2,1,0:T(8,128)}, u32[]{:S(2)}) copy-start(s32[32,8,1024]{2,1,0:T(8,128)} %tissue_ref.1) | copy-start | bytes 3145732
  14.4 0.9 copy-start.6
  18.2 1.2 %copy-start.8 = (s32[128]{0:T(128)S(1)}, s32[128]{0:T(128)}, u32[]{:S(2)}) copy-start(s32[128]{0:T(128)} %add.161) | copy-start | bytes 1540
  19.4 3.2 %copy-start.5 = (s32[128]{0:T(128)}, s32[128]{0:T(128)S(1)}, u32[]{:S(2)}) copy-start(s32[128]{0:T(128)S(1)} %gather_fusion) | copy-start | bytes 1540
  19.4 1.7 %copy-start.9 = (f32[2]{0:T(128)S(1)}, f32[2]{0:T(128)}, u32[]{:S(2)}) copy-start(f32[2]{0:T(128)} %param.13) | copy-start | bytes 28
  19.4 3.0 %copy-start.10 = (f32[32]{0:T(128)S(1)}, f32[32]{0:T(128)}, u32[]{:S(2)}) copy-start(f32[32]{0:T(128)} %convert_element_type.40) | copy-start | bytes 388
  22.6 16.5 %copy-start.2 = (bf16[32,8,1024]{2,1,0:T(8,128)(2,1)S(1)}, bf16[32,8,1024]{2,1,0:T(8,128)(2,1)}, u32[]{:S(2)}) copy-start(bf16[32,8,1024]{2,1,0:T(8,128)(2,1)} %l_ref.3) | copy-start | bytes 1572868
  24.1 36.8 %all-to-all-start = ((f32[64,1,3200]{2,1,0:T(1,128)}), f32[64,1,3200]{2,1,0:T(1,128)S(1)}, u32[]{:S(2)}, u32[]{:S(2)}) async-start(f32[64,1,3200]{2,1,0:T(1,128)} %all_to_all.14), calls=%async_computation | async-start | bytes 1638400 | tf_op jit(solution)/shard_map/all_to_all | solution.py:448
  39.8 17.1 %collective-permute-start.4 = (f32[32,3,1024]{2,1,0:T(4,128)S(1)}, f32[32,3,1024]{2,1,0:T(4,128)S(1)}, u32[]{:S(2)}, u32[]{:S(2)}) collective-permute-start(f32[32,3,1024]{2,1,0:T(4,128)S(1)} %pad_maximum_fusion.4), channel_id=1, source_target_pairs={{1,0},{2,1},{3,2},{5,4},{6,5},{7,6},{9,8},{10,9},{11,10},{13,12},{... | collective-permute-start | bytes 1179656 | tf_op jit(solution)/shard_map/ppermute | solution.py:462
  41.4 15.4 %collective-permute-start.3 = (f32[32,3,1024]{2,1,0:T(4,128)S(1)}, f32[32,3,1024]{2,1,0:T(4,128)S(1)}, u32[]{:S(2)}, u32[]{:S(2)}) collective-permute-start(f32[32,3,1024]{2,1,0:T(4,128)S(1)} %pad_maximum_fusion.3), channel_id=1, source_target_pairs={{0,1},{1,2},{2,3},{4,5},{5,6},{6,7},{8,9},{9,10},{10,11},{12,13},{... | collective-permute-start | bytes 1179656 | tf_op jit(solution)/shard_map/ppermute | solution.py:462
  65.9 14.5 %copy-start.7 = (s32[32]{0:T(128)S(1)}, s32[32]{0:T(128)}, u32[]{:S(2)}) copy-start(s32[32]{0:T(128)} %own_ref.1) | copy-start | bytes 388

commit v10 on v7

--- a/solution.py
+++ b/solution.py
@@ -285,47 +285,59 @@
     ycoord = lane % edge
     masks = (lane < edge, lane >= cells - edge, ycoord == 0, ycoord == edge - 1)
 
+    chunk = 256
+    lane = lax.broadcasted_iota(jnp.int32, (nz, chunk), 1)
+    row = lax.broadcasted_iota(jnp.int32, (nz, chunk), 0)
+    ycoord = lane % edge
+
     def one(i, carry):
         b = g * GROUP + i
         th = cond_ref[own_ref[b]]
-        u = u_ref[i]
-        l = l_ref[i].astype(jnp.float32)
-        gx = gx_ref[i]
-        gy = gy_ref[i]
-        halo = halo_ref[i]
-        edge_u, edge_l, edge_t = [], [], []
-        for side, r in ((0, 0), (1, nz - 1)):
-            own_z = (gx[r:r + 1] != 0.0).astype(jnp.float32) * VERTICAL
-            conduct = own_z * (halo[3 * side:3 * side + 1] * VERTICAL)
-            step_u = halo[3 * side + 1:3 * side + 2] - u[r:r + 1]
-            step_l = conduct * (halo[3 * side + 2:3 * side + 3] - l[r:r + 1])
-            edge_u.append(conduct * step_u)
-            edge_l.append(step_l)
-            edge_t.append(step_l * step_u)
-        lap_u = lu_ref[i] + jnp.where(row == 0, edge_u[0], 0.0) + jnp.where(row == nz - 1, edge_u[1], 0.0)
-        lap_l = ll_ref[i] + jnp.where(row == 0, edge_l[0], 0.0) + jnp.where(row == nz - 1, edge_l[1], 0.0)
-        inner = inner_ref[i] + group_sum(edge_t[0]) + group_sum(edge_t[1])
-        face_u = jnp.zeros_like(u)
-        face_l = jnp.zeros_like(u)
-        face_t = jnp.zeros_like(u)
-        for f in range(4):
-            ext = ext_ref[f, pl.ds(pl.multiple_of(i * rows, rows), rows), :]
-            near_w = (ext[0:nz] + ext[2 * nz:3 * nz]) + ext[4 * nz:5 * nz]
-            near_u = (ext[nz:2 * nz] + ext[3 * nz:4 * nz]) + ext[5 * nz:6 * nz]
-            near_l = ext[6 * nz:7 * nz]
-            g_self = gx if f < 2 else gy
-            conduct = jnp.where(masks[f], cond_ref[cell_ref[near_ref[4 * b + f]]] * (g_self * near_w), 0.0)
-            step_u = near_u - u
-            step_l = conduct * (near_l - l)
-            face_u = face_u + conduct * step_u
-            face_l = face_l + step_l
-            face_t = face_t + step_l * step_u
+        near_th = [cond_ref[cell_ref[near_ref[4 * b + f]]] for f in range(4)]
         square = th * th
-        ionic = u * (1.0 - u) * (u - THRESHOLD)
-        slope = -3.0 * u * u + 2.0 * (1.0 + THRESHOLD) * u - THRESHOLD
-        u_out[i] = u + TIMESTEP * ((square * lap_u + th * face_u) + ionic)
-        l_out[i] = l + TIMESTEP * ((square * lap_l + th * face_l) + slope * l)
-        part_out[i] = -(square * inner + th * group_sum(face_t))
+        base = pl.multiple_of(i * rows, rows)
+        total = -square * inner_ref[i]
+        for c in range(cells // chunk):
+            cols = slice(c * chunk, (c + 1) * chunk)
+            at = lane + c * chunk
+            masks = (at < edge, at >= cells - edge, ycoord == 0, ycoord == edge - 1)
+            u = u_ref[i, :, cols]
+            l = l_ref[i, :, cols].astype(jnp.float32)
+            gx = gx_ref[i, :, cols]
+            gy = gy_ref[i, :, cols]
+            halo = halo_ref[i, :, cols]
+            edge_u, edge_l, edge_t = [], [], []
+            for side, r in ((0, 0), (1, nz - 1)):
+                own_z = (gx[r:r + 1] != 0.0).astype(jnp.float32) * VERTICAL
+                conduct = own_z * (halo[3 * side:3 * side + 1] * VERTICAL)
+                step_u = halo[3 * side + 1:3 * side + 2] - u[r:r + 1]
+                step_l = conduct * (halo[3 * side + 2:3 * side + 3] - l[r:r + 1])
+                edge_u.append(conduct * step_u)
+                edge_l.append(step_l)
+                edge_t.append(step_l * step_u)
+            lap_u = lu_ref[i, :, cols] + jnp.where(row == 0, edge_u[0], 0.0) + jnp.where(row == nz - 1, edge_u[1], 0.0)
+            lap_l = ll_ref[i, :, cols] + jnp.where(row == 0, edge_l[0], 0.0) + jnp.where(row == nz - 1, edge_l[1], 0.0)
+            face_u = jnp.zeros_like(u)
+            face_l = jnp.zeros_like(u)
+            face_t = jnp.zeros_like(u)
+            for f in range(4):
+                piece = lambda k: ext_ref[f, pl.ds(base + k * nz, nz), cols]
+                near_w = (piece(0) + piece(2)) + piece(4)
+                near_u = (piece(1) + piece(3)) + piece(5)
+                near_l = piece(6)
+                g_self = gx if f < 2 else gy
+                conduct = jnp.where(masks[f], near_th[f] * (g_self * near_w), 0.0)
+                step_u = near_u - u
+                step_l = conduct * (near_l - l)
+                face_u = face_u + conduct * step_u
+                face_l = face_l + step_l
+                face_t = face_t + step_l * step_u
+            ionic = u * (1.0 - u) * (u - THRESHOLD)
+            slope = -3.0 * u * u + 2.0 * (1.0 + THRESHOLD) * u - THRESHOLD
+            u_out[i, :, cols] = u + TIMESTEP * ((square * lap_u + th * face_u) + ionic)
+            l_out[i, :, cols] = l + TIMESTEP * ((square * lap_l + th * face_l) + slope * l)
+            total = total - (square * (group_sum(edge_t[0]) + group_sum(edge_t[1])) + th * group_sum(face_t))
+        part_out[i] = total
         return carry
 
     lax.fori_loop(0, GROUP, one, 0)

time: 101 us -> 101 us (level)
  no operation moved by 1% of the time
where the time goes in v10:
time: 101 us
  starting transfers between devices  25 us (25%)
  Pallas kernels  23.9 us (24%)
  blocking collectives  22.7 us (22%)
  local copies, waits for them, and re-layouts  12.2 us (12%)
  other arithmetic  9.63 us (10%)
  matrix products  3.59 us (4%)
  waiting for transfers between devices  2.82 us (3%)
  between operations  1.08 us (1%)
    all_to_all x1, blocking collectives, body(): lax.all_to_all(shares.reshape(devices, own_cells), ('blk', 'par'), split_...  22.7 us
    all_to_all x1, starting transfers between devices, body(): lax.all_to_all(sending, 'blk', split_axis=0, concat_axis=0, tiled=True)  13.2 us
    pallas_call x1, Pallas kernels, outer_step(): pl.pallas_call(outer_kernel, grid=(bricks // GROUP,), in_specs=[pl.BlockS...  12.7 us
    pallas_call x1, Pallas kernels, inner_step(): pl.pallas_call(inner_kernel, grid=(bricks // GROUP,), in_specs=[blk3(), b...  11.2 us
    ppermute x3, starting transfers between devices, body(): lax.ppermute(conductance, 'par', [(i, (i + s) % parts) for i in range(par...  6.32 us
    ppermute x1, starting transfers between devices, body(): lax.ppermute(last, 'par', up)  4.2 us
    dot_general x4, matrix products, boundary(): jnp.dot(values.astype(jnp.float32).reshape(bricks * z_layers, plane_cells...  3.59 us
    all_to_all x1, waiting for transfers between devices, body(): lax.all_to_all(sending, 'blk', split_axis=0, concat_axis=0, tiled=True)  2.81 us
  transfers between devices with their start and end apart: 6, of which 1 were waited for; matrix products, arithmetic and copies ran while one was open for 17% of the time, Pallas kernels for 11%

profile of v10, /device:TPU:1, one launch (start us, length us, event | category | flops | bytes accessed | tf_op | source)
XLA Modules:
  0.0 100.9 jit_solution(3749664132285457330)
XLA Ops:
  0.6 0.0 copy-start
  0.7 3.6 %collective-permute-start.1 = (f32[2]{0:T(128)}, f32[2]{0:T(128)S(1)}, u32[]{:S(2)}, u32[]{:S(2)}) collective-permute-start(f32[2]{0:T(128)} %param.13), channel_id=1, source_target_pairs={{0,2},{1,3},{2,0},{3,1},{4,6},{5,7},{6,4},{7,5},{8,10},{9,11},{10,... | collective-permute-start | bytes 32 | tf_op jit(solution)/shard_map/ppermute | solution.py:441
  4.3 0.3 collective-permute-start
  4.6 2.4 %collective-permute-start.2 = (f32[2]{0:T(128)}, f32[2]{0:T(128)S(1)}, u32[]{:S(2)}, u32[]{:S(2)}) collective-permute-start(f32[2]{0:T(128)} %param.13), channel_id=1, source_target_pairs={{0,3},{1,0},{2,1},{3,2},{4,7},{5,4},{6,5},{7,6},{8,11},{9,8},{10,9... | collective-permute-start | bytes 32 | tf_op jit(solution)/shard_map/ppermute | solution.py:441
  7.0 0.7 convert_element_type.38
  7.7 0.7 compare_select_fusion
  8.4 0.1 copy.26
  8.5 0.1 reshape.461
  8.6 0.7 add.160
  9.2 0.1 add.161
  9.3 0.1 iota_compare_fusion.2
  9.4 0.1 iota_compare_fusion
  9.6 0.8 fusion.21
  10.3 1.4 %convolution_bitcast_fusion = f32[256,128]{0,1:T(8,128)S(1)} fusion(pred[128,1024]{1,0:T(32,128)(4,1)S(1)} %bitcast.78, bf16[32,8,1024]{2,1,0:T(8,128)(2,1)} %l_ref.3), kind=kOutput, calls=%fused_computation.5 | convolution fusion | flops 67108864 | bytes 786432 | tf_op jit(solution)/shard_map/dot_general | solution.py:419
  11.8 0.1 copy.30
  11.9 0.7 convolution_bitcast_fusion.1
  12.6 0.1 copy.29
  12.7 0.7 fusion.1
  13.4 0.7 convolution_bitcast_fusion.2
  14.2 0.1 copy.27
  14.3 0.1 copy.28
  14.4 0.3 integer_pow.14
  14.7 0.4 fusion.12
  15.1 0.3 reshape.447
  15.3 0.3 reshape.450
  15.6 0.3 reshape.452
  15.9 0.3 fusion.5
  16.2 0.4 pad_maximum_fusion
  16.6 0.1 copy.31
  16.7 0.4 reshape.487
  17.2 1.1 %gather_fusion = s32[128]{0:T(128)S(1)} fusion(s32[2048]{0:T(1024)S(1)} %copy-done, s32[1024]{0:T(1024)S(1)} %pad_clamp_fusion.2), kind=kCustom, calls=%fused_computation | custom fusion | bytes 1536 | tf_op jit(solution)/shard_map/gather | solution.py:404
  18.4 0.2 convert_reduce_fusion
  18.6 1.2 %scatter_custom_fusion = f32[256,768]{1,0:T(8,128)S(1)} fusion(s32[128]{0:T(128)S(1)} %get-tuple-element.32, f32[128,768]{1,0:T(8,128)S(1)} %reshape.487, f32[]{:T(128)} %constant.36.clone.1), kind=kCustom, calls=%fused_computation.24 | custom fusion | bytes 786436 | tf_op jit(solution)/shard_map/scatter | solution.py:439
  19.8 0.2 reshape.454
  20.1 0.6 gather_fusion.1
  20.6 0.1 reshape.455
  20.7 0.1 fusion.13
  20.8 0.1 pad_maximum_fusion.2
  20.9 1.5 %all_to_all.14 = f32[64,1,3200]{2,1,0:T(1,128)} reshape(f32[64,3200]{1,0:T(8,128)S(1)} %pad_maximum_fusion.2) | data formatting | bytes 1638400 | tf_op jit(solution)/shard_map/all_to_all | solution.py:452
  22.3 13.2 %all-to-all-start = ((f32[64,1,3200]{2,1,0:T(1,128)}), f32[64,1,3200]{2,1,0:T(1,128)S(1)}, u32[]{:S(2)}, u32[]{:S(2)}) async-start(f32[64,1,3200]{2,1,0:T(1,128)} %all_to_all.14), calls=%async_computation | async-start | bytes 1638400 | tf_op jit(solution)/shard_map/all_to_all | solution.py:452
  35.5 1.8 %slice_convert_fusion.1 = (f32[32,1,1024]{2,1,0:T(1,128)S(1)}, f32[32,1,1024]{2,1,0:T(1,128)S(1)}) fusion(s32[32,8,1024]{2,1,0:T(8,128)} %tissue_ref.1), kind=kLoop, calls=%fused_computation.32 | loop fusion | flops 65536 | bytes 524288 | tf_op jit(solution)/shard_map/convert_element_type | solution.py:464
  37.3 0.3 fusion.22
  37.7 0.3 pad_maximum_fusion.4
  38.0 1.3 %collective-permute-start.4 = (f32[32,3,1024]{2,1,0:T(4,128)S(1)}, f32[32,3,1024]{2,1,0:T(4,128)S(1)}, u32[]{:S(2)}, u32[]{:S(2)}) collective-permute-start(f32[32,3,1024]{2,1,0:T(4,128)S(1)} %pad_maximum_fusion.4), channel_id=1, source_target_pairs={{1,0},{2,1},{3,2},{5,4},{6,5},{7,6},{9,8},{10,9},{11,10},{13,12},{... | collective-permute-start | bytes 1179656 | tf_op jit(solution)/shard_map/ppermute | solution.py:466
  39.3 0.3 pad_maximum_fusion.3
  39.7 4.2 %collective-permute-start.3 = (f32[32,3,1024]{2,1,0:T(4,128)S(1)}, f32[32,3,1024]{2,1,0:T(4,128)S(1)}, u32[]{:S(2)}, u32[]{:S(2)}) collective-permute-start(f32[32,3,1024]{2,1,0:T(4,128)S(1)} %pad_maximum_fusion.3), channel_id=1, source_target_pairs={{0,1},{1,2},{2,3},{4,5},{5,6},{6,7},{8,9},{9,10},{10,11},{12,13},{... | collective-permute-start | bytes 1179656 | tf_op jit(solution)/shard_map/ppermute | solution.py:466
  43.9 11.2 %shard_map.112 = (f32[32,8,1024]{2,1,0:T(8,128)}, f32[32,8,1024]{2,1,0:T(8,128)}, f32[32,8,1024]{2,1,0:T(8,128)}, f32[32,8,1024]{2,1,0:T(8,128)}, f32[32,1,128]{2,1,0:T(1,128)}) custom-call(s32[32,8,1024]{2,1,0:T(8,128)} %tissue_ref.1, bf16[32,8,1024]{2,1,0:T(8,128)(2,1)} %angle_ref.1, f32[32,8,1024]{2,1,0:T(8,128)} %u_ref.3, bf16[32,8,1024]{2,1,0:T(8,128)(2,1)} %l_ref.3), custom_call_target="tpu_custom_call" | custom-call | tf_op jit(solution)/shard_map/pallas_call | solution.py:350
  55.1 1.2 %pad_maximum_fusion.1.halo_ref = f32[32,6,1024]{2,1,0:T(8,128)} fusion(f32[32,3,1024]{2,1,0:T(4,128)S(1)} %collective-permute-done.4, f32[32,3,1024]{2,1,0:T(4,128)S(1)} %collective-permute-done.3), kind=kLoop, calls=%fused_computation.11 | loop fusion | flops 196608 | bytes 1572864 | tf_op jit(solution)/shard_map/concatenate | solution.py:466
  56.4 2.8 %all-to-all-done = f32[64,1,3200]{2,1,0:T(1,128)S(1)} async-done(((f32[64,1,3200]{2,1,0:T(1,128)}), f32[64,1,3200]{2,1,0:T(1,128)S(1)}, u32[]{:S(2)}, u32[]{:S(2)}) %all-to-all-start) | async-done | bytes 819232 | tf_op jit(solution)/shard_map/all_to_all | solution.py:452
  59.2 0.1 copy.35
  59.2 0.1 slice_convert_fusion.2
  59.3 0.1 slice.54
  59.4 0.7 convert_element_type.40.cell_ref
  60.0 0.7 reshape.456.cond_ref
  60.7 0.2 reshape.457
  60.9 0.8 gather_fusion.2
  61.8 1.6 %reshape.458.face_ref = f32[32,4,24,32]{3,2,1,0:T(8,128)} reshape(f32[128,768]{1,0:T(8,128)S(1)} %gather_fusion.2) | data formatting | bytes 786432 | tf_op jit(solution)/shard_map/reshape | solution.py:457
  63.4 12.7 %shard_map.113 = (f32[32,8,1024]{2,1,0:T(8,128)}, f32[32,8,1024]{2,1,0:T(8,128)}, f32[32,1,128]{2,1,0:T(1,128)}) custom-call(f32[512]{0:T(512)} %reshape.456.cond_ref, s32[2048]{0:T(1024)} %convert_element_type.40.cell_ref, s32[32]{0:T(128)} %own_ref.1, s32[128]{0:T(128)} %copy-done.5, bf16[4,32,1024]{2,1,0:T(8,128)(2,1)} %get-tuple-element.21.expand_ref, ...), custom_call_target="tpu_custom_call" | custom-call | tf_op jit(solution)/shard_map/pallas_call | solution.py:367
  76.1 1.0 %reduce_sum.53 = f32[32]{0:T(128)S(1)} reduce(f32[32,1,128]{2,1,0:T(1,128)} %get-tuple-element.18, f32[]{:T(128)} %constant.36.clone.1), dimensions={1,2}, to_apply=%region_3.4 | reduce | flops 4064 | bytes 16516 | tf_op jit(solution)/shard_map/reduce_sum | solution.py:470
  77.2 0.1 select_reduce_fusion
  77.3 0.1 all_to_all.17
  77.4 22.7 %all_to_all.21 = f32[256,1,2]{2,1,0:T(1,128)S(1)} all-to-all(f32[256,1,2]{2,1,0:T(1,128)S(1)} %bitcast.85), channel_id=1, replica_groups=mesh['blk'=64,'par'=4] {'blk','par'}, dimensions={0} | all-to-all | bytes 4096 | tf_op jit(solution)/shard_map/all_to_all | solution.py:474
  100.1 0.3 reduce_sum.55
  100.4 0.5 multiply_divide_fusion
  (32 shorter events, 0.1 us)
Async XLA Ops:
  0.6 16.5 %copy-start = (s32[2048]{0:T(1024)S(1)}, s32[2048]{0:T(1024)}, u32[]{:S(2)}) copy-start(s32[2048]{0:T(1024)} %param.14) | copy-start | bytes 24580
  0.6 11.2 %copy-start.1 = (f32[32,8,1024]{2,1,0:T(8,128)S(1)}, f32[32,8,1024]{2,1,0:T(8,128)}, u32[]{:S(2)}) copy-start(f32[32,8,1024]{2,1,0:T(8,128)} %u_ref.3) | copy-start | bytes 3145732
  0.7 19.3 %collective-permute-start.1 = (f32[2]{0:T(128)}, f32[2]{0:T(128)S(1)}, u32[]{:S(2)}, u32[]{:S(2)}) collective-permute-start(f32[2]{0:T(128)} %param.13), channel_id=1, source_target_pairs={{0,2},{1,3},{2,0},{3,1},{4,6},{5,7},{6,4},{7,5},{8,10},{9,11},{10,... | collective-permute-start | bytes 32 | tf_op jit(solution)/shard_map/ppermute | solution.py:441
  4.3 15.7 %collective-permute-start = (f32[2]{0:T(128)}, f32[2]{0:T(128)S(1)}, u32[]{:S(2)}, u32[]{:S(2)}) collective-permute-start(f32[2]{0:T(128)} %param.13), channel_id=1, source_target_pairs={{0,1},{1,2},{2,3},{3,0},{4,5},{5,6},{6,7},{7,4},{8,9},{9,10},{10,1... | collective-permute-start | bytes 32 | tf_op jit(solution)/shard_map/ppermute | solution.py:441
  4.6 15.4 %collective-permute-start.2 = (f32[2]{0:T(128)}, f32[2]{0:T(128)S(1)}, u32[]{:S(2)}, u32[]{:S(2)}) collective-permute-start(f32[2]{0:T(128)} %param.13), channel_id=1, source_target_pairs={{0,3},{1,0},{2,1},{3,2},{4,7},{5,4},{6,5},{7,6},{8,11},{9,8},{10,9... | collective-permute-start | bytes 32 | tf_op jit(solution)/shard_map/ppermute | solution.py:441
  9.5 3.2 %copy-start.4 = (bf16[32,8,1024]{2,1,0:T(8,128)(2,1)S(1)}, bf16[32,8,1024]{2,1,0:T(8,128)(2,1)}, u32[]{:S(2)}) copy-start(bf16[32,8,1024]{2,1,0:T(8,128)(2,1)} %angle_ref.1) | copy-start | bytes 1572868
  10.3 3.1 %copy-start.3 = (s32[32,8,1024]{2,1,0:T(8,128)S(1)}, s32[32,8,1024]{2,1,0:T(8,128)}, u32[]{:S(2)}) copy-start(s32[32,8,1024]{2,1,0:T(8,128)} %tissue_ref.1) | copy-start | bytes 3145732
  18.3 2.5 %copy-start.5 = (s32[128]{0:T(128)}, s32[128]{0:T(128)S(1)}, u32[]{:S(2)}) copy-start(s32[128]{0:T(128)S(1)} %gather_fusion) | copy-start | bytes 1540
  18.3 1.7 %copy-start.7 = (f32[2]{0:T(128)S(1)}, f32[2]{0:T(128)}, u32[]{:S(2)}) copy-start(f32[2]{0:T(128)} %param.13) | copy-start | bytes 28
  20.9 16.5 %copy-start.2 = (bf16[32,8,1024]{2,1,0:T(8,128)(2,1)S(1)}, bf16[32,8,1024]{2,1,0:T(8,128)(2,1)}, u32[]{:S(2)}) copy-start(bf16[32,8,1024]{2,1,0:T(8,128)(2,1)} %l_ref.3) | copy-start | bytes 1572868
  22.3 36.8 %all-to-all-start = ((f32[64,1,3200]{2,1,0:T(1,128)}), f32[64,1,3200]{2,1,0:T(1,128)S(1)}, u32[]{:S(2)}, u32[]{:S(2)}) async-start(f32[64,1,3200]{2,1,0:T(1,128)} %all_to_all.14), calls=%async_computation | async-start | bytes 1638400 | tf_op jit(solution)/shard_map/all_to_all | solution.py:452
  38.0 17.1 %collective-permute-start.4 = (f32[32,3,1024]{2,1,0:T(4,128)S(1)}, f32[32,3,1024]{2,1,0:T(4,128)S(1)}, u32[]{:S(2)}, u32[]{:S(2)}) collective-permute-start(f32[32,3,1024]{2,1,0:T(4,128)S(1)} %pad_maximum_fusion.4), channel_id=1, source_target_pairs={{1,0},{2,1},{3,2},{5,4},{6,5},{7,6},{9,8},{10,9},{11,10},{13,12},{... | collective-permute-start | bytes 1179656 | tf_op jit(solution)/shard_map/ppermute | solution.py:466
  39.7 15.4 %collective-permute-start.3 = (f32[32,3,1024]{2,1,0:T(4,128)S(1)}, f32[32,3,1024]{2,1,0:T(4,128)S(1)}, u32[]{:S(2)}, u32[]{:S(2)}) collective-permute-start(f32[32,3,1024]{2,1,0:T(4,128)S(1)} %pad_maximum_fusion.3), channel_id=1, source_target_pairs={{0,1},{1,2},{2,3},{4,5},{5,6},{6,7},{8,9},{9,10},{10,11},{12,13},{... | collective-permute-start | bytes 1179656 | tf_op jit(solution)/shard_map/ppermute | solution.py:466
  63.4 13.8 %copy-start.6 = (s32[32]{0:T(128)S(1)}, s32[32]{0:T(128)}, u32[]{:S(2)}) copy-start(s32[32]{0:T(128)} %own_ref.1) | copy-start | bytes 388

commit v11 on v10

--- a/solution.py
+++ b/solution.py
@@ -219,7 +219,7 @@
     return acc
 
 
-def inner_kernel(tissue_ref, angle_ref, u_ref, l_ref, lu_out, ll_out, gx_out, gy_out, part_out):
+def inner_kernel(tissue_ref, angle_ref, u_ref, l_ref, lu_out, ll_out, gx_out, part_out):
     nz, cells = u_ref.shape[1], u_ref.shape[2]
     edge = BX
     lane = lax.broadcasted_iota(jnp.int32, (nz, cells), 1)
@@ -252,14 +252,13 @@
         lu_out[i] = lap_u
         ll_out[i] = lap_l
         gx_out[i] = gx
-        gy_out[i] = gy
         part_out[i] = group_sum(terms)
         return carry
 
     lax.fori_loop(0, GROUP, one, 0)
 
 
-def outer_kernel(cond_ref, cell_ref, own_ref, near_ref, expand_ref, u_ref, l_ref, lu_ref, ll_ref, gx_ref, gy_ref, inner_ref, face_ref,
+def outer_kernel(cond_ref, cell_ref, own_ref, near_ref, expand_ref, u_ref, l_ref, lu_ref, ll_ref, gx_ref, inner_ref, face_ref,
                  halo_ref, u_out, l_out, part_out, ext_ref):
     g = pl.program_id(0)
     nz, cells = u_ref.shape[1], u_ref.shape[2]
@@ -304,7 +303,7 @@
             u = u_ref[i, :, cols]
             l = l_ref[i, :, cols].astype(jnp.float32)
             gx = gx_ref[i, :, cols]
-            gy = gy_ref[i, :, cols]
+            gy = jnp.where(gx != 0.0, (ALONG + ACROSS) - gx, 0.0)
             halo = halo_ref[i, :, cols]
             edge_u, edge_l, edge_t = [], [], []
             for side, r in ((0, 0), (1, nz - 1)):
@@ -351,8 +350,8 @@
         inner_kernel,
         grid=(bricks // GROUP,),
         in_specs=[blk3(), blk3(), blk3(), blk3()],
-        out_specs=[blk3(), blk3(), blk3(), blk3(), pl.BlockSpec((GROUP, 1, 128), lambda g: (g, 0, 0))],
-        out_shape=[full, full, full, full, jax.ShapeDtypeStruct((bricks, 1, 128), jnp.float32)],
+        out_specs=[blk3(), blk3(), blk3(), pl.BlockSpec((GROUP, 1, 128), lambda g: (g, 0, 0))],
+        out_shape=[full, full, full, jax.ShapeDtypeStruct((bricks, 1, 128), jnp.float32)],
         compiler_params=pltpu.CompilerParams(dimension_semantics=("parallel",)),
         interpret=interpret,
     )(tissue, angle, potential, sensitivity)
@@ -363,13 +362,13 @@
     edge = faces.shape[-1]
     expand = expanders(edge, cells).astype(jnp.bfloat16)
     blk3 = lambda: pl.BlockSpec((GROUP, nz, cells), lambda g: (g, 0, 0))
-    lap_u, lap_l, gx, gy, inner_part = inner
+    lap_u, lap_l, gx, inner_part = inner
     return pl.pallas_call(
         outer_kernel,
         grid=(bricks // GROUP,),
         in_specs=[pl.BlockSpec(memory_space=pltpu.SMEM) for _ in tables] + [
             pl.BlockSpec((4, edge, cells), lambda g: (0, 0, 0)),
-            blk3(), blk3(), blk3(), blk3(), blk3(), blk3(),
+            blk3(), blk3(), blk3(), blk3(), blk3(),
             pl.BlockSpec((GROUP, 1, 128), lambda g: (g, 0, 0)),
             pl.BlockSpec((GROUP, 4, faces.shape[2], edge), lambda g: (g, 0, 0, 0)),
             pl.BlockSpec((GROUP, 6, cells), lambda g: (g, 0, 0)),
@@ -383,7 +382,7 @@
         scratch_shapes=[pltpu.VMEM((4, GROUP * 8 * nz, cells), jnp.float32)],
         compiler_params=pltpu.CompilerParams(dimension_semantics=("parallel",)),
         interpret=interpret,
-    )(*tables, expand, potential, sensitivity, lap_u, lap_l, gx, gy, inner_part, faces, halos)
+    )(*tables, expand, potential, sensitivity, lap_u, lap_l, gx, inner_part, faces, halos)
 
 
 def body(

time: 101 us -> 101 us (level)
  no operation moved by 1% of the time
where the time goes in v11:
time: 101 us
  starting transfers between devices  25 us (25%)
  Pallas kernels  23.5 us (23%)
  blocking collectives  22.7 us (22%)
  local copies, waits for them, and re-layouts  12.2 us (12%)
  other arithmetic  9.61 us (10%)
  matrix products  3.59 us (4%)
  waiting for transfers between devices  2.98 us (3%)
  between operations  1.08 us (1%)
    all_to_all x1, blocking collectives, body(): lax.all_to_all(shares.reshape(devices, own_cells), ('blk', 'par'), split_...  22.7 us
    all_to_all x1, starting transfers between devices, body(): lax.all_to_all(sending, 'blk', split_axis=0, concat_axis=0, tiled=True)  13.2 us
    pallas_call x1, Pallas kernels, outer_step(): pl.pallas_call(outer_kernel, grid=(bricks // GROUP,), in_specs=[pl.BlockS...  12.4 us
    pallas_call x1, Pallas kernels, inner_step(): pl.pallas_call(inner_kernel, grid=(bricks // GROUP,), in_specs=[blk3(), b...  11 us
    ppermute x3, starting transfers between devices, body(): lax.ppermute(conductance, 'par', [(i, (i + s) % parts) for i in range(par...  6.32 us
    ppermute x1, starting transfers between devices, body(): lax.ppermute(last, 'par', up)  4.2 us
    dot_general x4, matrix products, boundary(): jnp.dot(values.astype(jnp.float32).reshape(bricks * z_layers, plane_cells...  3.59 us
    all_to_all x1, waiting for transfers between devices, body(): lax.all_to_all(sending, 'blk', split_axis=0, concat_axis=0, tiled=True)  2.97 us
  transfers between devices with their start and end apart: 6, of which 1 were waited for; matrix products, arithmetic and copies ran while one was open for 17% of the time, Pallas kernels for 11%

profile of v11, /device:TPU:1, one launch (start us, length us, event | category | flops | bytes accessed | tf_op | source)
XLA Modules:
  0.0 100.6 jit_solution(12347261959462579190)
XLA Ops:
  0.6 0.0 copy-start
  0.7 3.6 %collective-permute-start.1 = (f32[2]{0:T(128)}, f32[2]{0:T(128)S(1)}, u32[]{:S(2)}, u32[]{:S(2)}) collective-permute-start(f32[2]{0:T(128)} %param.13), channel_id=1, source_target_pairs={{0,2},{1,3},{2,0},{3,1},{4,6},{5,7},{6,4},{7,5},{8,10},{9,11},{10,... | collective-permute-start | bytes 32 | tf_op jit(solution)/shard_map/ppermute | solution.py:440
  4.3 0.3 collective-permute-start
  4.6 2.4 %collective-permute-start.2 = (f32[2]{0:T(128)}, f32[2]{0:T(128)S(1)}, u32[]{:S(2)}, u32[]{:S(2)}) collective-permute-start(f32[2]{0:T(128)} %param.13), channel_id=1, source_target_pairs={{0,3},{1,0},{2,1},{3,2},{4,7},{5,4},{6,5},{7,6},{8,11},{9,8},{10,9... | collective-permute-start | bytes 32 | tf_op jit(solution)/shard_map/ppermute | solution.py:440
  7.0 0.7 convert_element_type.38
  7.7 0.7 compare_select_fusion
  8.4 0.1 copy.26
  8.5 0.1 reshape.461
  8.6 0.7 add.160
  9.2 0.1 add.161
  9.3 0.1 iota_compare_fusion.2
  9.4 0.1 iota_compare_fusion
  9.6 0.8 fusion.21
  10.3 1.4 %convolution_bitcast_fusion = f32[256,128]{0,1:T(8,128)S(1)} fusion(pred[128,1024]{1,0:T(32,128)(4,1)S(1)} %bitcast.78, bf16[32,8,1024]{2,1,0:T(8,128)(2,1)} %l_ref.3), kind=kOutput, calls=%fused_computation.5 | convolution fusion | flops 67108864 | bytes 786432 | tf_op jit(solution)/shard_map/dot_general | solution.py:418
  11.8 0.1 copy.30
  11.9 0.7 convolution_bitcast_fusion.1
  12.6 0.1 copy.29
  12.7 0.7 fusion.1
  13.4 0.7 convolution_bitcast_fusion.2
  14.2 0.1 copy.27
  14.3 0.1 copy.28
  14.4 0.3 integer_pow.14
  14.6 0.4 fusion.12
  15.1 0.3 reshape.447
  15.3 0.3 reshape.450
  15.6 0.3 reshape.452
  15.9 0.3 fusion.5
  16.2 0.4 pad_maximum_fusion
  16.6 0.1 copy.31
  16.7 0.4 reshape.487
  17.2 1.1 %gather_fusion = s32[128]{0:T(128)S(1)} fusion(s32[2048]{0:T(1024)S(1)} %copy-done, s32[1024]{0:T(1024)S(1)} %pad_clamp_fusion.2), kind=kCustom, calls=%fused_computation | custom fusion | bytes 1536 | tf_op jit(solution)/shard_map/gather | solution.py:403
  18.4 0.2 convert_reduce_fusion
  18.6 1.2 %scatter_custom_fusion = f32[256,768]{1,0:T(8,128)S(1)} fusion(s32[128]{0:T(128)S(1)} %get-tuple-element.30, f32[128,768]{1,0:T(8,128)S(1)} %reshape.487, f32[]{:T(128)} %constant.36.clone.1), kind=kCustom, calls=%fused_computation.24 | custom fusion | bytes 786436 | tf_op jit(solution)/shard_map/scatter | solution.py:438
  19.8 0.2 reshape.454
  20.1 0.6 gather_fusion.1
  20.6 0.1 reshape.455
  20.7 0.1 fusion.13
  20.8 0.1 pad_maximum_fusion.2
  20.9 1.5 %all_to_all.14 = f32[64,1,3200]{2,1,0:T(1,128)} reshape(f32[64,3200]{1,0:T(8,128)S(1)} %pad_maximum_fusion.2) | data formatting | bytes 1638400 | tf_op jit(solution)/shard_map/all_to_all | solution.py:451
  22.3 13.2 %all-to-all-start = ((f32[64,1,3200]{2,1,0:T(1,128)}), f32[64,1,3200]{2,1,0:T(1,128)S(1)}, u32[]{:S(2)}, u32[]{:S(2)}) async-start(f32[64,1,3200]{2,1,0:T(1,128)} %all_to_all.14), calls=%async_computation | async-start | bytes 1638400 | tf_op jit(solution)/shard_map/all_to_all | solution.py:451
  35.5 1.8 %slice_convert_fusion.1 = (f32[32,1,1024]{2,1,0:T(1,128)S(1)}, f32[32,1,1024]{2,1,0:T(1,128)S(1)}) fusion(s32[32,8,1024]{2,1,0:T(8,128)} %tissue_ref.1), kind=kLoop, calls=%fused_computation.32 | loop fusion | flops 65536 | bytes 524288 | tf_op jit(solution)/shard_map/convert_element_type | solution.py:463
  37.3 0.3 fusion.22
  37.6 0.3 pad_maximum_fusion.4
  38.0 1.3 %collective-permute-start.4 = (f32[32,3,1024]{2,1,0:T(4,128)S(1)}, f32[32,3,1024]{2,1,0:T(4,128)S(1)}, u32[]{:S(2)}, u32[]{:S(2)}) collective-permute-start(f32[32,3,1024]{2,1,0:T(4,128)S(1)} %pad_maximum_fusion.4), channel_id=1, source_target_pairs={{1,0},{2,1},{3,2},{5,4},{6,5},{7,6},{9,8},{10,9},{11,10},{13,12},{... | collective-permute-start | bytes 1179656 | tf_op jit(solution)/shard_map/ppermute | solution.py:465
  39.3 0.3 pad_maximum_fusion.3
  39.6 4.2 %collective-permute-start.3 = (f32[32,3,1024]{2,1,0:T(4,128)S(1)}, f32[32,3,1024]{2,1,0:T(4,128)S(1)}, u32[]{:S(2)}, u32[]{:S(2)}) collective-permute-start(f32[32,3,1024]{2,1,0:T(4,128)S(1)} %pad_maximum_fusion.3), channel_id=1, source_target_pairs={{0,1},{1,2},{2,3},{4,5},{5,6},{6,7},{8,9},{9,10},{10,11},{12,13},{... | collective-permute-start | bytes 1179656 | tf_op jit(solution)/shard_map/ppermute | solution.py:465
  43.9 11.0 %shard_map.112 = (f32[32,8,1024]{2,1,0:T(8,128)}, f32[32,8,1024]{2,1,0:T(8,128)}, f32[32,8,1024]{2,1,0:T(8,128)}, f32[32,1,128]{2,1,0:T(1,128)}) custom-call(s32[32,8,1024]{2,1,0:T(8,128)} %tissue_ref.1, bf16[32,8,1024]{2,1,0:T(8,128)(2,1)} %angle_ref.1, f32[32,8,1024]{2,1,0:T(8,128)} %u_ref.3, bf16[32,8,1024]{2,1,0:T(8,128)(2,1)} %l_ref.3), custom_call_target="tpu_custom_call" | custom-call | tf_op jit(solution)/shard_map/pallas_call | solution.py:349
  54.9 1.3 %pad_maximum_fusion.1.halo_ref = f32[32,6,1024]{2,1,0:T(8,128)} fusion(f32[32,3,1024]{2,1,0:T(4,128)S(1)} %collective-permute-done.4, f32[32,3,1024]{2,1,0:T(4,128)S(1)} %collective-permute-done.3), kind=kLoop, calls=%fused_computation.11 | loop fusion | flops 196608 | bytes 1572864 | tf_op jit(solution)/shard_map/concatenate | solution.py:465
  56.2 3.0 %all-to-all-done = f32[64,1,3200]{2,1,0:T(1,128)S(1)} async-done(((f32[64,1,3200]{2,1,0:T(1,128)}), f32[64,1,3200]{2,1,0:T(1,128)S(1)}, u32[]{:S(2)}, u32[]{:S(2)}) %all-to-all-start) | async-done | bytes 819232 | tf_op jit(solution)/shard_map/all_to_all | solution.py:451
  59.2 0.1 copy.35
  59.2 0.1 slice_convert_fusion.2
  59.3 0.1 slice.54
  59.4 0.7 convert_element_type.40.cell_ref
  60.0 0.7 reshape.456.cond_ref
  60.7 0.2 reshape.457
  60.9 0.8 gather_fusion.2
  61.7 1.6 %reshape.458.face_ref = f32[32,4,24,32]{3,2,1,0:T(8,128)} reshape(f32[128,768]{1,0:T(8,128)S(1)} %gather_fusion.2) | data formatting | bytes 786432 | tf_op jit(solution)/shard_map/reshape | solution.py:456
  63.4 12.4 %shard_map.113 = (f32[32,8,1024]{2,1,0:T(8,128)}, f32[32,8,1024]{2,1,0:T(8,128)}, f32[32,1,128]{2,1,0:T(1,128)}) custom-call(f32[512]{0:T(512)} %reshape.456.cond_ref, s32[2048]{0:T(1024)} %convert_element_type.40.cell_ref, s32[32]{0:T(128)} %own_ref.1, s32[128]{0:T(128)} %copy-done.5, bf16[4,32,1024]{2,1,0:T(8,128)(2,1)} %get-tuple-element.19.expand_ref, ...), custom_call_target="tpu_custom_call" | custom-call | tf_op jit(solution)/shard_map/pallas_call | solution.py:366
  75.8 1.0 %reduce_sum.53 = f32[32]{0:T(128)S(1)} reduce(f32[32,1,128]{2,1,0:T(1,128)} %get-tuple-element.16, f32[]{:T(128)} %constant.36.clone.1), dimensions={1,2}, to_apply=%region_3.4 | reduce | flops 4064 | bytes 16516 | tf_op jit(solution)/shard_map/reduce_sum | solution.py:469
  76.8 0.1 select_reduce_fusion
  76.9 0.1 all_to_all.17
  77.1 22.7 %all_to_all.21 = f32[256,1,2]{2,1,0:T(1,128)S(1)} all-to-all(f32[256,1,2]{2,1,0:T(1,128)S(1)} %bitcast.85), channel_id=1, replica_groups=mesh['blk'=64,'par'=4] {'blk','par'}, dimensions={0} | all-to-all | bytes 4096 | tf_op jit(solution)/shard_map/all_to_all | solution.py:473
  99.7 0.3 reduce_sum.55
  100.0 0.5 multiply_divide_fusion
  (32 shorter events, 0.1 us)
Async XLA Ops:
  0.6 16.5 %copy-start = (s32[2048]{0:T(1024)S(1)}, s32[2048]{0:T(1024)}, u32[]{:S(2)}) copy-start(s32[2048]{0:T(1024)} %param.14) | copy-start | bytes 24580
  0.6 11.2 %copy-start.1 = (f32[32,8,1024]{2,1,0:T(8,128)S(1)}, f32[32,8,1024]{2,1,0:T(8,128)}, u32[]{:S(2)}) copy-start(f32[32,8,1024]{2,1,0:T(8,128)} %u_ref.3) | copy-start | bytes 3145732
  0.7 19.3 %collective-permute-start.1 = (f32[2]{0:T(128)}, f32[2]{0:T(128)S(1)}, u32[]{:S(2)}, u32[]{:S(2)}) collective-permute-start(f32[2]{0:T(128)} %param.13), channel_id=1, source_target_pairs={{0,2},{1,3},{2,0},{3,1},{4,6},{5,7},{6,4},{7,5},{8,10},{9,11},{10,... | collective-permute-start | bytes 32 | tf_op jit(solution)/shard_map/ppermute | solution.py:440
  4.3 15.7 %collective-permute-start = (f32[2]{0:T(128)}, f32[2]{0:T(128)S(1)}, u32[]{:S(2)}, u32[]{:S(2)}) collective-permute-start(f32[2]{0:T(128)} %param.13), channel_id=1, source_target_pairs={{0,1},{1,2},{2,3},{3,0},{4,5},{5,6},{6,7},{7,4},{8,9},{9,10},{10,1... | collective-permute-start | bytes 32 | tf_op jit(solution)/shard_map/ppermute | solution.py:440
  4.6 15.4 %collective-permute-start.2 = (f32[2]{0:T(128)}, f32[2]{0:T(128)S(1)}, u32[]{:S(2)}, u32[]{:S(2)}) collective-permute-start(f32[2]{0:T(128)} %param.13), channel_id=1, source_target_pairs={{0,3},{1,0},{2,1},{3,2},{4,7},{5,4},{6,5},{7,6},{8,11},{9,8},{10,9... | collective-permute-start | bytes 32 | tf_op jit(solution)/shard_map/ppermute | solution.py:440
  9.5 3.2 %copy-start.4 = (bf16[32,8,1024]{2,1,0:T(8,128)(2,1)S(1)}, bf16[32,8,1024]{2,1,0:T(8,128)(2,1)}, u32[]{:S(2)}) copy-start(bf16[32,8,1024]{2,1,0:T(8,128)(2,1)} %angle_ref.1) | copy-start | bytes 1572868
  10.3 3.1 %copy-start.3 = (s32[32,8,1024]{2,1,0:T(8,128)S(1)}, s32[32,8,1024]{2,1,0:T(8,128)}, u32[]{:S(2)}) copy-start(s32[32,8,1024]{2,1,0:T(8,128)} %tissue_ref.1) | copy-start | bytes 3145732
  18.3 2.5 %copy-start.5 = (s32[128]{0:T(128)}, s32[128]{0:T(128)S(1)}, u32[]{:S(2)}) copy-start(s32[128]{0:T(128)S(1)} %gather_fusion) | copy-start | bytes 1540
  18.3 1.7 %copy-start.7 = (f32[2]{0:T(128)S(1)}, f32[2]{0:T(128)}, u32[]{:S(2)}) copy-start(f32[2]{0:T(128)} %param.13) | copy-start | bytes 28
  20.9 16.4 %copy-start.2 = (bf16[32,8,1024]{2,1,0:T(8,128)(2,1)S(1)}, bf16[32,8,1024]{2,1,0:T(8,128)(2,1)}, u32[]{:S(2)}) copy-start(bf16[32,8,1024]{2,1,0:T(8,128)(2,1)} %l_ref.3) | copy-start | bytes 1572868
  22.3 36.8 %all-to-all-start = ((f32[64,1,3200]{2,1,0:T(1,128)}), f32[64,1,3200]{2,1,0:T(1,128)S(1)}, u32[]{:S(2)}, u32[]{:S(2)}) async-start(f32[64,1,3200]{2,1,0:T(1,128)} %all_to_all.14), calls=%async_computation | async-start | bytes 1638400 | tf_op jit(solution)/shard_map/all_to_all | solution.py:451
  38.0 16.9 %collective-permute-start.4 = (f32[32,3,1024]{2,1,0:T(4,128)S(1)}, f32[32,3,1024]{2,1,0:T(4,128)S(1)}, u32[]{:S(2)}, u32[]{:S(2)}) collective-permute-start(f32[32,3,1024]{2,1,0:T(4,128)S(1)} %pad_maximum_fusion.4), channel_id=1, source_target_pairs={{1,0},{2,1},{3,2},{5,4},{6,5},{7,6},{9,8},{10,9},{11,10},{13,12},{... | collective-permute-start | bytes 1179656 | tf_op jit(solution)/shard_map/ppermute | solution.py:465
  39.6 15.3 %collective-permute-start.3 = (f32[32,3,1024]{2,1,0:T(4,128)S(1)}, f32[32,3,1024]{2,1,0:T(4,128)S(1)}, u32[]{:S(2)}, u32[]{:S(2)}) collective-permute-start(f32[32,3,1024]{2,1,0:T(4,128)S(1)} %pad_maximum_fusion.3), channel_id=1, source_target_pairs={{0,1},{1,2},{2,3},{4,5},{5,6},{6,7},{8,9},{9,10},{10,11},{12,13},{... | collective-permute-start | bytes 1179656 | tf_op jit(solution)/shard_map/ppermute | solution.py:465
  63.4 13.5 %copy-start.6 = (s32[32]{0:T(128)S(1)}, s32[32]{0:T(128)}, u32[]{:S(2)}) copy-start(s32[32]{0:T(128)} %own_ref.1) | copy-start | bytes 388

commit v12 on v11

--- a/solution.py
+++ b/solution.py
@@ -258,7 +258,7 @@
     lax.fori_loop(0, GROUP, one, 0)
 
 
-def outer_kernel(cond_ref, cell_ref, own_ref, near_ref, expand_ref, u_ref, l_ref, lu_ref, ll_ref, gx_ref, inner_ref, face_ref,
+def outer_kernel(table_ref, own_ref, near_ref, expand_ref, u_ref, l_ref, lu_ref, ll_ref, gx_ref, inner_ref, face_ref,
                  halo_ref, u_out, l_out, part_out, ext_ref):
     g = pl.program_id(0)
     nz, cells = u_ref.shape[1], u_ref.shape[2]
@@ -291,8 +291,16 @@
 
     def one(i, carry):
         b = g * GROUP + i
-        th = cond_ref[own_ref[b]]
-        near_th = [cond_ref[cell_ref[near_ref[4 * b + f]]] for f in range(4)]
+        width = table_ref.shape[1] - own_ref.shape[0]
+
+        def cond_of(q):
+            return table_ref[q // width, q % width]
+
+        def cell_of(s):
+            return table_ref[s // own_ref.shape[0], width + s % own_ref.shape[0]].astype(jnp.int32)
+
+        th = cond_of(own_ref[b])
+        near_th = [cond_of(cell_of(near_ref[4 * b + f])) for f in range(4)]
         square = th * th
         base = pl.multiple_of(i * rows, rows)
         total = -square * inner_ref[i]
@@ -464,7 +472,7 @@
     initial = jnp.stack([tissue[:, 0].astype(jnp.float32), potential[:, 0], adjoint[:, 0]], axis=1)
     halos = jnp.concatenate([lax.ppermute(last, "par", up), lax.ppermute(initial, "par", down)], axis=1)
 
-    tables = (cond_all, cell_all, brick_cell, near_slot.reshape(-1))
+    tables = (arrived[:, width : width + par_cells + bricks], brick_cell, near_slot.reshape(-1))
     final, adjoint, parts_out = outer_step(tables, potential, sensitivity, inner, faces, halos)
     brick_part = jnp.sum(parts_out, axis=(1, 2))
     onehot_cells = brick_cell[:, None] == jnp.arange(cell_count, dtype=jnp.int32)[None, :]

time: 101 us -> 101 us (level)
  Pallas kernels: 23.5 us -> 24.6 us
    pallas_call x1, Pallas kernels: 12.4 us -> 13.6 us  [outer_step(): pl.pallas_call(outer_kernel, grid=(bricks // GROUP,), in_specs=[pl.BlockS...]
where the time goes in v12:
time: 101 us
  starting transfers between devices  25 us (25%)
  Pallas kernels  24.6 us (24%)
  blocking collectives  22.7 us (22%)
  local copies, waits for them, and re-layouts  11.5 us (11%)
  other arithmetic  9.53 us (9%)
  matrix products  3.59 us (4%)
  waiting for transfers between devices  2.98 us (3%)
  between operations  1.07 us (1%)
    all_to_all x1, blocking collectives, body(): lax.all_to_all(shares.reshape(devices, own_cells), ('blk', 'par'), split_...  22.7 us
    pallas_call x1, Pallas kernels, outer_step(): pl.pallas_call(outer_kernel, grid=(bricks // GROUP,), in_specs=[pl.BlockS...  13.6 us
    all_to_all x1, starting transfers between devices, body(): lax.all_to_all(sending, 'blk', split_axis=0, concat_axis=0, tiled=True)  13.2 us
    pallas_call x1, Pallas kernels, inner_step(): pl.pallas_call(inner_kernel, grid=(bricks // GROUP,), in_specs=[blk3(), b...  11 us
    ppermute x3, starting transfers between devices, body(): lax.ppermute(conductance, 'par', [(i, (i + s) % parts) for i in range(par...  6.32 us
    ppermute x1, starting transfers between devices, body(): lax.ppermute(last, 'par', up)  4.2 us
    dot_general x4, matrix products, boundary(): jnp.dot(values.astype(jnp.float32).reshape(bricks * z_layers, plane_cells...  3.59 us
    all_to_all x1, waiting for transfers between devices, body(): lax.all_to_all(sending, 'blk', split_axis=0, concat_axis=0, tiled=True)  2.97 us
  transfers between devices with their start and end apart: 6, of which 1 were waited for; matrix products, arithmetic and copies ran while one was open for 17% of the time, Pallas kernels for 11%

profile of v12, /device:TPU:1, one launch (start us, length us, event | category | flops | bytes accessed | tf_op | source)
XLA Modules:
  0.0 100.9 jit_solution(16236513472372391946)
XLA Ops:
  0.6 0.0 copy-start
  0.6 0.0 copy-start.1
  0.7 3.6 %collective-permute-start.1 = (f32[2]{0:T(128)}, f32[2]{0:T(128)S(1)}, u32[]{:S(2)}, u32[]{:S(2)}) collective-permute-start(f32[2]{0:T(128)} %param.13), channel_id=1, source_target_pairs={{0,2},{1,3},{2,0},{3,1},{4,6},{5,7},{6,4},{7,5},{8,10},{9,11},{10,... | collective-permute-start | bytes 32 | tf_op jit(solution)/shard_map/ppermute | solution.py:448
  4.3 0.3 collective-permute-start
  4.6 2.4 %collective-permute-start.2 = (f32[2]{0:T(128)}, f32[2]{0:T(128)S(1)}, u32[]{:S(2)}, u32[]{:S(2)}) collective-permute-start(f32[2]{0:T(128)} %param.13), channel_id=1, source_target_pairs={{0,3},{1,0},{2,1},{3,2},{4,7},{5,4},{6,5},{7,6},{8,11},{9,8},{10,9... | collective-permute-start | bytes 32 | tf_op jit(solution)/shard_map/ppermute | solution.py:448
  7.0 0.7 convert_element_type.33
  7.7 0.7 compare_select_fusion
  8.4 0.1 copy.32
  8.5 0.1 reshape.455
  8.6 0.7 add.160
  9.2 0.1 add.161
  9.3 0.1 iota_compare_fusion.2
  9.4 0.1 iota_compare_fusion
  9.5 0.0 copy-start.4
  9.6 0.8 fusion.21
  10.3 1.4 %convolution_bitcast_fusion = f32[256,128]{0,1:T(8,128)S(1)} fusion(pred[128,1024]{1,0:T(32,128)(4,1)S(1)} %bitcast.77, bf16[32,8,1024]{2,1,0:T(8,128)(2,1)} %l_ref.3), kind=kOutput, calls=%fused_computation.5 | convolution fusion | flops 67108864 | bytes 786432 | tf_op jit(solution)/shard_map/dot_general | solution.py:426
  11.8 0.1 copy.36
  11.9 0.7 convolution_bitcast_fusion.1
  12.6 0.1 copy.35
  12.7 0.7 fusion.1
  13.4 0.7 convolution_bitcast_fusion.2
  14.2 0.1 copy.33
  14.3 0.1 copy.34
  14.4 0.3 integer_pow.14
  14.6 0.4 fusion.12
  15.1 0.3 reshape.442
  15.3 0.3 reshape.445
  15.6 0.3 reshape.447
  15.9 0.3 fusion.5
  16.2 0.4 pad_maximum_fusion
  16.6 0.1 copy.37
  16.7 0.4 reshape.481
  17.2 1.1 %gather_fusion = s32[128]{0:T(128)S(1)} fusion(s32[2048]{0:T(1024)S(1)} %copy-done, s32[1024]{0:T(1024)S(1)} %pad_clamp_fusion.2), kind=kCustom, calls=%fused_computation | custom fusion | bytes 1536 | tf_op jit(solution)/shard_map/gather | solution.py:411
  18.4 0.2 convert_reduce_fusion
  18.6 1.2 %scatter_custom_fusion = f32[256,768]{1,0:T(8,128)S(1)} fusion(s32[128]{0:T(128)S(1)} %get-tuple-element.30, f32[128,768]{1,0:T(8,128)S(1)} %reshape.481, f32[]{:T(128)} %constant.36.clone.1), kind=kCustom, calls=%fused_computation.24 | custom fusion | bytes 786436 | tf_op jit(solution)/shard_map/scatter | solution.py:446
  19.8 0.2 reshape.449
  20.1 0.6 gather_fusion.1
  20.6 0.1 reshape.450
  20.7 0.1 fusion.13
  20.8 0.1 pad_maximum_fusion.2
  20.9 1.5 %all_to_all.14 = f32[64,1,3200]{2,1,0:T(1,128)} reshape(f32[64,3200]{1,0:T(8,128)S(1)} %pad_maximum_fusion.2) | data formatting | bytes 1638400 | tf_op jit(solution)/shard_map/all_to_all | solution.py:459
  22.3 13.2 %all-to-all-start = ((f32[64,1,3200]{2,1,0:T(1,128)}), f32[64,1,3200]{2,1,0:T(1,128)S(1)}, u32[]{:S(2)}, u32[]{:S(2)}) async-start(f32[64,1,3200]{2,1,0:T(1,128)} %all_to_all.14), calls=%async_computation | async-start | bytes 1638400 | tf_op jit(solution)/shard_map/all_to_all | solution.py:459
  35.5 1.8 %slice_convert_fusion.1 = (f32[32,1,1024]{2,1,0:T(1,128)S(1)}, f32[32,1,1024]{2,1,0:T(1,128)S(1)}) fusion(s32[32,8,1024]{2,1,0:T(8,128)} %tissue_ref.1), kind=kLoop, calls=%fused_computation.32 | loop fusion | flops 65536 | bytes 524288 | tf_op jit(solution)/shard_map/convert_element_type | solution.py:471
  37.3 0.3 fusion.22
  37.6 0.3 pad_maximum_fusion.4
  38.0 1.3 %collective-permute-start.4 = (f32[32,3,1024]{2,1,0:T(4,128)S(1)}, f32[32,3,1024]{2,1,0:T(4,128)S(1)}, u32[]{:S(2)}, u32[]{:S(2)}) collective-permute-start(f32[32,3,1024]{2,1,0:T(4,128)S(1)} %pad_maximum_fusion.4), channel_id=1, source_target_pairs={{1,0},{2,1},{3,2},{5,4},{6,5},{7,6},{9,8},{10,9},{11,10},{13,12},{... | collective-permute-start | bytes 1179656 | tf_op jit(solution)/shard_map/ppermute | solution.py:473
  39.3 0.3 pad_maximum_fusion.3
  39.6 4.2 %collective-permute-start.3 = (f32[32,3,1024]{2,1,0:T(4,128)S(1)}, f32[32,3,1024]{2,1,0:T(4,128)S(1)}, u32[]{:S(2)}, u32[]{:S(2)}) collective-permute-start(f32[32,3,1024]{2,1,0:T(4,128)S(1)} %pad_maximum_fusion.3), channel_id=1, source_target_pairs={{0,1},{1,2},{2,3},{4,5},{5,6},{6,7},{8,9},{9,10},{10,11},{12,13},{... | collective-permute-start | bytes 1179656 | tf_op jit(solution)/shard_map/ppermute | solution.py:473
  43.9 11.0 %shard_map.112 = (f32[32,8,1024]{2,1,0:T(8,128)}, f32[32,8,1024]{2,1,0:T(8,128)}, f32[32,8,1024]{2,1,0:T(8,128)}, f32[32,1,128]{2,1,0:T(1,128)}) custom-call(s32[32,8,1024]{2,1,0:T(8,128)} %tissue_ref.1, bf16[32,8,1024]{2,1,0:T(8,128)(2,1)} %angle_ref.1, f32[32,8,1024]{2,1,0:T(8,128)} %u_ref.3, bf16[32,8,1024]{2,1,0:T(8,128)(2,1)} %l_ref.3), custom_call_target="tpu_custom_call" | custom-call | tf_op jit(solution)/shard_map/pallas_call | solution.py:357
  54.9 1.3 %pad_maximum_fusion.1.halo_ref = f32[32,6,1024]{2,1,0:T(8,128)} fusion(f32[32,3,1024]{2,1,0:T(4,128)S(1)} %collective-permute-done.4, f32[32,3,1024]{2,1,0:T(4,128)S(1)} %collective-permute-done.3), kind=kLoop, calls=%fused_computation.11 | loop fusion | flops 196608 | bytes 1572864 | tf_op jit(solution)/shard_map/concatenate | solution.py:473
  56.2 3.0 %all-to-all-done = f32[64,1,3200]{2,1,0:T(1,128)S(1)} async-done(((f32[64,1,3200]{2,1,0:T(1,128)}), f32[64,1,3200]{2,1,0:T(1,128)S(1)}, u32[]{:S(2)}, u32[]{:S(2)}) %all-to-all-start) | async-done | bytes 819232 | tf_op jit(solution)/shard_map/all_to_all | solution.py:459
  59.2 0.1 copy.41
  59.2 0.6 slice.48.table_ref
  59.8 0.1 slice.49
  59.9 0.2 reshape.451
  60.1 0.8 gather_fusion.2
  60.9 1.6 %reshape.452.face_ref = f32[32,4,24,32]{3,2,1,0:T(8,128)} reshape(f32[128,768]{1,0:T(8,128)S(1)} %gather_fusion.2) | data formatting | bytes 786432 | tf_op jit(solution)/shard_map/reshape | solution.py:464
  62.5 13.6 %shard_map.113 = (f32[32,8,1024]{2,1,0:T(8,128)}, f32[32,8,1024]{2,1,0:T(8,128)}, f32[32,1,128]{2,1,0:T(1,128)}) custom-call(f32[64,40]{1,0:T(8,128)} %slice.48.table_ref, s32[32]{0:T(128)} %own_ref.1, s32[128]{0:T(128)} %copy-done.5, bf16[4,32,1024]{2,1,0:T(8,128)(2,1)} %get-tuple-element.19.expand_ref, f32[32,8,1024]{2,1,0:T(8,128)} %u_ref.3, ...), custom_call_target="tpu_custom_call" | custom-call | tf_op jit(solution)/shard_map/pallas_call | solution.py:374
  76.1 1.0 %reduce_sum.53 = f32[32]{0:T(128)S(1)} reduce(f32[32,1,128]{2,1,0:T(1,128)} %get-tuple-element.16, f32[]{:T(128)} %constant.36.clone.1), dimensions={1,2}, to_apply=%region_3.4 | reduce | flops 4064 | bytes 16516 | tf_op jit(solution)/shard_map/reduce_sum | solution.py:477
  77.2 0.1 select_reduce_fusion
  77.3 0.1 all_to_all.17
  77.4 22.7 %all_to_all.21 = f32[256,1,2]{2,1,0:T(1,128)S(1)} all-to-all(f32[256,1,2]{2,1,0:T(1,128)S(1)} %bitcast.84), channel_id=1, replica_groups=mesh['blk'=64,'par'=4] {'blk','par'}, dimensions={0} | all-to-all | bytes 4096 | tf_op jit(solution)/shard_map/all_to_all | solution.py:481
  100.1 0.3 reduce_sum.55
  100.4 0.5 multiply_divide_fusion
  (29 shorter events, 0.1 us)
Async XLA Ops:
  0.6 16.5 %copy-start = (s32[2048]{0:T(1024)S(1)}, s32[2048]{0:T(1024)}, u32[]{:S(2)}) copy-start(s32[2048]{0:T(1024)} %param.14) | copy-start | bytes 24580
  0.6 11.2 %copy-start.1 = (f32[32,8,1024]{2,1,0:T(8,128)S(1)}, f32[32,8,1024]{2,1,0:T(8,128)}, u32[]{:S(2)}) copy-start(f32[32,8,1024]{2,1,0:T(8,128)} %u_ref.3) | copy-start | bytes 3145732
  0.7 19.3 %collective-permute-start.1 = (f32[2]{0:T(128)}, f32[2]{0:T(128)S(1)}, u32[]{:S(2)}, u32[]{:S(2)}) collective-permute-start(f32[2]{0:T(128)} %param.13), channel_id=1, source_target_pairs={{0,2},{1,3},{2,0},{3,1},{4,6},{5,7},{6,4},{7,5},{8,10},{9,11},{10,... | collective-permute-start | bytes 32 | tf_op jit(solution)/shard_map/ppermute | solution.py:448
  4.3 15.7 %collective-permute-start = (f32[2]{0:T(128)}, f32[2]{0:T(128)S(1)}, u32[]{:S(2)}, u32[]{:S(2)}) collective-permute-start(f32[2]{0:T(128)} %param.13), channel_id=1, source_target_pairs={{0,1},{1,2},{2,3},{3,0},{4,5},{5,6},{6,7},{7,4},{8,9},{9,10},{10,1... | collective-permute-start | bytes 32 | tf_op jit(solution)/shard_map/ppermute | solution.py:448
  4.6 15.4 %collective-permute-start.2 = (f32[2]{0:T(128)}, f32[2]{0:T(128)S(1)}, u32[]{:S(2)}, u32[]{:S(2)}) collective-permute-start(f32[2]{0:T(128)} %param.13), channel_id=1, source_target_pairs={{0,3},{1,0},{2,1},{3,2},{4,7},{5,4},{6,5},{7,6},{8,11},{9,8},{10,9... | collective-permute-start | bytes 32 | tf_op jit(solution)/shard_map/ppermute | solution.py:448
  9.5 3.2 %copy-start.4 = (bf16[32,8,1024]{2,1,0:T(8,128)(2,1)S(1)}, bf16[32,8,1024]{2,1,0:T(8,128)(2,1)}, u32[]{:S(2)}) copy-start(bf16[32,8,1024]{2,1,0:T(8,128)(2,1)} %angle_ref.1) | copy-start | bytes 1572868
  10.3 3.1 %copy-start.3 = (s32[32,8,1024]{2,1,0:T(8,128)S(1)}, s32[32,8,1024]{2,1,0:T(8,128)}, u32[]{:S(2)}) copy-start(s32[32,8,1024]{2,1,0:T(8,128)} %tissue_ref.1) | copy-start | bytes 3145732
  18.3 2.5 %copy-start.5 = (s32[128]{0:T(128)}, s32[128]{0:T(128)S(1)}, u32[]{:S(2)}) copy-start(s32[128]{0:T(128)S(1)} %gather_fusion) | copy-start | bytes 1540
  18.3 1.7 %copy-start.7 = (f32[2]{0:T(128)S(1)}, f32[2]{0:T(128)}, u32[]{:S(2)}) copy-start(f32[2]{0:T(128)} %param.13) | copy-start | bytes 28
  20.9 16.4 %copy-start.2 = (bf16[32,8,1024]{2,1,0:T(8,128)(2,1)S(1)}, bf16[32,8,1024]{2,1,0:T(8,128)(2,1)}, u32[]{:S(2)}) copy-start(bf16[32,8,1024]{2,1,0:T(8,128)(2,1)} %l_ref.3) | copy-start | bytes 1572868
  22.3 36.8 %all-to-all-start = ((f32[64,1,3200]{2,1,0:T(1,128)}), f32[64,1,3200]{2,1,0:T(1,128)S(1)}, u32[]{:S(2)}, u32[]{:S(2)}) async-start(f32[64,1,3200]{2,1,0:T(1,128)} %all_to_all.14), calls=%async_computation | async-start | bytes 1638400 | tf_op jit(solution)/shard_map/all_to_all | solution.py:459
  38.0 16.9 %collective-permute-start.4 = (f32[32,3,1024]{2,1,0:T(4,128)S(1)}, f32[32,3,1024]{2,1,0:T(4,128)S(1)}, u32[]{:S(2)}, u32[]{:S(2)}) collective-permute-start(f32[32,3,1024]{2,1,0:T(4,128)S(1)} %pad_maximum_fusion.4), channel_id=1, source_target_pairs={{1,0},{2,1},{3,2},{5,4},{6,5},{7,6},{9,8},{10,9},{11,10},{13,12},{... | collective-permute-start | bytes 1179656 | tf_op jit(solution)/shard_map/ppermute | solution.py:473
  39.6 15.3 %collective-permute-start.3 = (f32[32,3,1024]{2,1,0:T(4,128)S(1)}, f32[32,3,1024]{2,1,0:T(4,128)S(1)}, u32[]{:S(2)}, u32[]{:S(2)}) collective-permute-start(f32[32,3,1024]{2,1,0:T(4,128)S(1)} %pad_maximum_fusion.3), channel_id=1, source_target_pairs={{0,1},{1,2},{2,3},{4,5},{5,6},{6,7},{8,9},{9,10},{10,11},{12,13},{... | collective-permute-start | bytes 1179656 | tf_op jit(solution)/shard_map/ppermute | solution.py:473
  62.5 14.6 %copy-start.6 = (s32[32]{0:T(128)S(1)}, s32[32]{0:T(128)}, u32[]{:S(2)}) copy-start(s32[32]{0:T(128)} %own_ref.1) | copy-start | bytes 388

commit v13 on v11

--- a/solution.py
+++ b/solution.py
@@ -106,6 +106,7 @@
 
 
 GROUP = 8
+OUTER = 4
 
 
 def expanders(edge, cells):
@@ -275,7 +276,7 @@
             [high, middle, low, face[:, 2 * nz:3 * nz], jnp.zeros_like(face[:, :nz])], axis=1
         )
         ext_ref[f] = jnp.dot(
-            stacked.reshape(GROUP * rows, edge).astype(jnp.bfloat16),
+            stacked.reshape(OUTER * rows, edge).astype(jnp.bfloat16),
             expand_ref[f],
             preferred_element_type=jnp.float32,
         )
@@ -290,7 +291,7 @@
     ycoord = lane % edge
 
     def one(i, carry):
-        b = g * GROUP + i
+        b = g * OUTER + i
         th = cond_ref[own_ref[b]]
         near_th = [cond_ref[cell_ref[near_ref[4 * b + f]]] for f in range(4)]
         square = th * th
@@ -339,7 +340,7 @@
         part_out[i] = total
         return carry
 
-    lax.fori_loop(0, GROUP, one, 0)
+    lax.fori_loop(0, OUTER, one, 0)
 
 
 def inner_step(tissue, angle, potential, sensitivity, interpret=False):
@@ -361,25 +362,25 @@
     bricks, nz, cells = potential.shape
     edge = faces.shape[-1]
     expand = expanders(edge, cells).astype(jnp.bfloat16)
-    blk3 = lambda: pl.BlockSpec((GROUP, nz, cells), lambda g: (g, 0, 0))
+    blk3 = lambda: pl.BlockSpec((OUTER, nz, cells), lambda g: (g, 0, 0))
     lap_u, lap_l, gx, inner_part = inner
     return pl.pallas_call(
         outer_kernel,
-        grid=(bricks // GROUP,),
+        grid=(bricks // OUTER,),
         in_specs=[pl.BlockSpec(memory_space=pltpu.SMEM) for _ in tables] + [
             pl.BlockSpec((4, edge, cells), lambda g: (0, 0, 0)),
             blk3(), blk3(), blk3(), blk3(), blk3(),
-            pl.BlockSpec((GROUP, 1, 128), lambda g: (g, 0, 0)),
-            pl.BlockSpec((GROUP, 4, faces.shape[2], edge), lambda g: (g, 0, 0, 0)),
-            pl.BlockSpec((GROUP, 6, cells), lambda g: (g, 0, 0)),
+            pl.BlockSpec((OUTER, 1, 128), lambda g: (g, 0, 0)),
+            pl.BlockSpec((OUTER, 4, faces.shape[2], edge), lambda g: (g, 0, 0, 0)),
+            pl.BlockSpec((OUTER, 6, cells), lambda g: (g, 0, 0)),
         ],
-        out_specs=[blk3(), blk3(), pl.BlockSpec((GROUP, 1, 128), lambda g: (g, 0, 0))],
+        out_specs=[blk3(), blk3(), pl.BlockSpec((OUTER, 1, 128), lambda g: (g, 0, 0))],
         out_shape=[
             jax.ShapeDtypeStruct((bricks, nz, cells), jnp.float32),
             jax.ShapeDtypeStruct((bricks, nz, cells), jnp.float32),
             jax.ShapeDtypeStruct((bricks, 1, 128), jnp.float32),
         ],
-        scratch_shapes=[pltpu.VMEM((4, GROUP * 8 * nz, cells), jnp.float32)],
+        scratch_shapes=[pltpu.VMEM((4, OUTER * 8 * nz, cells), jnp.float32)],
         compiler_params=pltpu.CompilerParams(dimension_semantics=("parallel",)),
         interpret=interpret,
     )(*tables, expand, potential, sensitivity, lap_u, lap_l, gx, inner_part, faces, halos)

time: 101 us -> 102 us (level)
  no operation moved by 1% of the time
where the time goes in v13:
time: 102 us; the launch traced here: 101 us
  starting transfers between devices  25 us (25%)
  Pallas kernels  23.9 us (23%)
  blocking collectives  22.7 us (22%)
  local copies, waits for them, and re-layouts  12.2 us (12%)
  other arithmetic  9.61 us (9%)
  matrix products  3.59 us (4%)
  waiting for transfers between devices  2.98 us (3%)
  between operations  1.08 us (1%)
    all_to_all x1, blocking collectives, body(): lax.all_to_all(shares.reshape(devices, own_cells), ('blk', 'par'), split_...  22.7 us
    all_to_all x1, starting transfers between devices, body(): lax.all_to_all(sending, 'blk', split_axis=0, concat_axis=0, tiled=True)  13.2 us
    pallas_call x1, Pallas kernels, outer_step(): pl.pallas_call(outer_kernel, grid=(bricks // OUTER,), in_specs=[pl.BlockS...  12.9 us
    pallas_call x1, Pallas kernels, inner_step(): pl.pallas_call(inner_kernel, grid=(bricks // GROUP,), in_specs=[blk3(), b...  11 us
    ppermute x3, starting transfers between devices, body(): lax.ppermute(conductance, 'par', [(i, (i + s) % parts) for i in range(par...  6.32 us
    ppermute x1, starting transfers between devices, body(): lax.ppermute(last, 'par', up)  4.2 us
    dot_general x4, matrix products, boundary(): jnp.dot(values.astype(jnp.float32).reshape(bricks * z_layers, plane_cells...  3.59 us
    all_to_all x1, waiting for transfers between devices, body(): lax.all_to_all(sending, 'blk', split_axis=0, concat_axis=0, tiled=True)  2.97 us
  transfers between devices with their start and end apart: 6, of which 1 were waited for; matrix products, arithmetic and copies ran while one was open for 17% of the time, Pallas kernels for 11%

profile of v13, /device:TPU:1, one launch (start us, length us, event | category | flops | bytes accessed | tf_op | source)
XLA Modules:
  0.0 101.0 jit_solution(17895311726545523190)
XLA Ops:
  0.6 0.0 copy-start
  0.7 3.6 %collective-permute-start.1 = (f32[2]{0:T(128)}, f32[2]{0:T(128)S(1)}, u32[]{:S(2)}, u32[]{:S(2)}) collective-permute-start(f32[2]{0:T(128)} %param.13), channel_id=1, source_target_pairs={{0,2},{1,3},{2,0},{3,1},{4,6},{5,7},{6,4},{7,5},{8,10},{9,11},{10,... | collective-permute-start | bytes 32 | tf_op jit(solution)/shard_map/ppermute | solution.py:441
  4.3 0.3 collective-permute-start
  4.6 2.4 %collective-permute-start.2 = (f32[2]{0:T(128)}, f32[2]{0:T(128)S(1)}, u32[]{:S(2)}, u32[]{:S(2)}) collective-permute-start(f32[2]{0:T(128)} %param.13), channel_id=1, source_target_pairs={{0,3},{1,0},{2,1},{3,2},{4,7},{5,4},{6,5},{7,6},{8,11},{9,8},{10,9... | collective-permute-start | bytes 32 | tf_op jit(solution)/shard_map/ppermute | solution.py:441
  7.0 0.7 convert_element_type.38
  7.7 0.7 compare_select_fusion
  8.4 0.1 copy.26
  8.5 0.1 reshape.461
  8.6 0.7 add.160
  9.2 0.1 add.161
  9.3 0.1 iota_compare_fusion.2
  9.4 0.1 iota_compare_fusion
  9.6 0.8 fusion.21
  10.3 1.4 %convolution_bitcast_fusion = f32[256,128]{0,1:T(8,128)S(1)} fusion(pred[128,1024]{1,0:T(32,128)(4,1)S(1)} %bitcast.78, bf16[32,8,1024]{2,1,0:T(8,128)(2,1)} %l_ref.3), kind=kOutput, calls=%fused_computation.5 | convolution fusion | flops 67108864 | bytes 786432 | tf_op jit(solution)/shard_map/dot_general | solution.py:419
  11.8 0.1 copy.30
  11.9 0.7 convolution_bitcast_fusion.1
  12.6 0.1 copy.29
  12.7 0.7 fusion.1
  13.4 0.7 convolution_bitcast_fusion.2
  14.2 0.1 copy.27
  14.3 0.1 copy.28
  14.4 0.3 integer_pow.14
  14.6 0.4 fusion.12
  15.1 0.3 reshape.447
  15.3 0.3 reshape.450
  15.6 0.3 reshape.452
  15.9 0.3 fusion.5
  16.2 0.4 pad_maximum_fusion
  16.6 0.1 copy.31
  16.7 0.4 reshape.487
  17.2 1.1 %gather_fusion = s32[128]{0:T(128)S(1)} fusion(s32[2048]{0:T(1024)S(1)} %copy-done, s32[1024]{0:T(1024)S(1)} %pad_clamp_fusion.2), kind=kCustom, calls=%fused_computation | custom fusion | bytes 1536 | tf_op jit(solution)/shard_map/gather | solution.py:404
  18.4 0.2 convert_reduce_fusion
  18.6 1.2 %scatter_custom_fusion = f32[256,768]{1,0:T(8,128)S(1)} fusion(s32[128]{0:T(128)S(1)} %get-tuple-element.30, f32[128,768]{1,0:T(8,128)S(1)} %reshape.487, f32[]{:T(128)} %constant.36.clone.1), kind=kCustom, calls=%fused_computation.24 | custom fusion | bytes 786436 | tf_op jit(solution)/shard_map/scatter | solution.py:439
  19.8 0.2 reshape.454
  20.1 0.6 gather_fusion.1
  20.6 0.1 reshape.455
  20.7 0.1 fusion.13
  20.8 0.1 pad_maximum_fusion.2
  20.9 1.5 %all_to_all.14 = f32[64,1,3200]{2,1,0:T(1,128)} reshape(f32[64,3200]{1,0:T(8,128)S(1)} %pad_maximum_fusion.2) | data formatting | bytes 1638400 | tf_op jit(solution)/shard_map/all_to_all | solution.py:452
  22.3 13.2 %all-to-all-start = ((f32[64,1,3200]{2,1,0:T(1,128)}), f32[64,1,3200]{2,1,0:T(1,128)S(1)}, u32[]{:S(2)}, u32[]{:S(2)}) async-start(f32[64,1,3200]{2,1,0:T(1,128)} %all_to_all.14), calls=%async_computation | async-start | bytes 1638400 | tf_op jit(solution)/shard_map/all_to_all | solution.py:452
  35.5 1.8 %slice_convert_fusion.1 = (f32[32,1,1024]{2,1,0:T(1,128)S(1)}, f32[32,1,1024]{2,1,0:T(1,128)S(1)}) fusion(s32[32,8,1024]{2,1,0:T(8,128)} %tissue_ref.1), kind=kLoop, calls=%fused_computation.32 | loop fusion | flops 65536 | bytes 524288 | tf_op jit(solution)/shard_map/convert_element_type | solution.py:464
  37.3 0.3 fusion.22
  37.6 0.3 pad_maximum_fusion.4
  38.0 1.3 %collective-permute-start.4 = (f32[32,3,1024]{2,1,0:T(4,128)S(1)}, f32[32,3,1024]{2,1,0:T(4,128)S(1)}, u32[]{:S(2)}, u32[]{:S(2)}) collective-permute-start(f32[32,3,1024]{2,1,0:T(4,128)S(1)} %pad_maximum_fusion.4), channel_id=1, source_target_pairs={{1,0},{2,1},{3,2},{5,4},{6,5},{7,6},{9,8},{10,9},{11,10},{13,12},{... | collective-permute-start | bytes 1179656 | tf_op jit(solution)/shard_map/ppermute | solution.py:466
  39.3 0.3 pad_maximum_fusion.3
  39.6 4.2 %collective-permute-start.3 = (f32[32,3,1024]{2,1,0:T(4,128)S(1)}, f32[32,3,1024]{2,1,0:T(4,128)S(1)}, u32[]{:S(2)}, u32[]{:S(2)}) collective-permute-start(f32[32,3,1024]{2,1,0:T(4,128)S(1)} %pad_maximum_fusion.3), channel_id=1, source_target_pairs={{0,1},{1,2},{2,3},{4,5},{5,6},{6,7},{8,9},{9,10},{10,11},{12,13},{... | collective-permute-start | bytes 1179656 | tf_op jit(solution)/shard_map/ppermute | solution.py:466
  43.9 11.0 %shard_map.112 = (f32[32,8,1024]{2,1,0:T(8,128)}, f32[32,8,1024]{2,1,0:T(8,128)}, f32[32,8,1024]{2,1,0:T(8,128)}, f32[32,1,128]{2,1,0:T(1,128)}) custom-call(s32[32,8,1024]{2,1,0:T(8,128)} %tissue_ref.1, bf16[32,8,1024]{2,1,0:T(8,128)(2,1)} %angle_ref.1, f32[32,8,1024]{2,1,0:T(8,128)} %u_ref.3, bf16[32,8,1024]{2,1,0:T(8,128)(2,1)} %l_ref.3), custom_call_target="tpu_custom_call" | custom-call | tf_op jit(solution)/shard_map/pallas_call | solution.py:350
  54.9 1.3 %pad_maximum_fusion.1.halo_ref = f32[32,6,1024]{2,1,0:T(8,128)} fusion(f32[32,3,1024]{2,1,0:T(4,128)S(1)} %collective-permute-done.4, f32[32,3,1024]{2,1,0:T(4,128)S(1)} %collective-permute-done.3), kind=kLoop, calls=%fused_computation.11 | loop fusion | flops 196608 | bytes 1572864 | tf_op jit(solution)/shard_map/concatenate | solution.py:466
  56.2 3.0 %all-to-all-done = f32[64,1,3200]{2,1,0:T(1,128)S(1)} async-done(((f32[64,1,3200]{2,1,0:T(1,128)}), f32[64,1,3200]{2,1,0:T(1,128)S(1)}, u32[]{:S(2)}, u32[]{:S(2)}) %all-to-all-start) | async-done | bytes 819232 | tf_op jit(solution)/shard_map/all_to_all | solution.py:452
  59.2 0.1 copy.35
  59.2 0.1 slice_convert_fusion.2
  59.3 0.1 slice.54
  59.4 0.7 convert_element_type.40.cell_ref
  60.0 0.7 reshape.456.cond_ref
  60.7 0.2 reshape.457
  60.9 0.8 gather_fusion.2
  61.7 1.6 %reshape.458.face_ref = f32[32,4,24,32]{3,2,1,0:T(8,128)} reshape(f32[128,768]{1,0:T(8,128)S(1)} %gather_fusion.2) | data formatting | bytes 786432 | tf_op jit(solution)/shard_map/reshape | solution.py:457
  63.4 12.9 %shard_map.113 = (f32[32,8,1024]{2,1,0:T(8,128)}, f32[32,8,1024]{2,1,0:T(8,128)}, f32[32,1,128]{2,1,0:T(1,128)}) custom-call(f32[512]{0:T(512)} %reshape.456.cond_ref, s32[2048]{0:T(1024)} %convert_element_type.40.cell_ref, s32[32]{0:T(128)} %own_ref.1, s32[128]{0:T(128)} %copy-done.5, bf16[4,32,1024]{2,1,0:T(8,128)(2,1)} %get-tuple-element.19.expand_ref, ...), custom_call_target="tpu_custom_call" | custom-call | tf_op jit(solution)/shard_map/pallas_call | solution.py:367
  76.3 1.0 %reduce_sum.53 = f32[32]{0:T(128)S(1)} reduce(f32[32,1,128]{2,1,0:T(1,128)} %get-tuple-element.16, f32[]{:T(128)} %constant.36.clone.1), dimensions={1,2}, to_apply=%region_3.4 | reduce | flops 4064 | bytes 16516 | tf_op jit(solution)/shard_map/reduce_sum | solution.py:470
  77.3 0.1 select_reduce_fusion
  77.4 0.1 all_to_all.17
  77.5 22.7 %all_to_all.21 = f32[256,1,2]{2,1,0:T(1,128)S(1)} all-to-all(f32[256,1,2]{2,1,0:T(1,128)S(1)} %bitcast.85), channel_id=1, replica_groups=mesh['blk'=64,'par'=4] {'blk','par'}, dimensions={0} | all-to-all | bytes 4096 | tf_op jit(solution)/shard_map/all_to_all | solution.py:474
  100.2 0.3 reduce_sum.55
  100.5 0.5 multiply_divide_fusion
  (32 shorter events, 0.1 us)
Async XLA Ops:
  0.6 16.5 %copy-start = (s32[2048]{0:T(1024)S(1)}, s32[2048]{0:T(1024)}, u32[]{:S(2)}) copy-start(s32[2048]{0:T(1024)} %param.14) | copy-start | bytes 24580
  0.6 11.2 %copy-start.1 = (f32[32,8,1024]{2,1,0:T(8,128)S(1)}, f32[32,8,1024]{2,1,0:T(8,128)}, u32[]{:S(2)}) copy-start(f32[32,8,1024]{2,1,0:T(8,128)} %u_ref.3) | copy-start | bytes 3145732
  0.7 19.3 %collective-permute-start.1 = (f32[2]{0:T(128)}, f32[2]{0:T(128)S(1)}, u32[]{:S(2)}, u32[]{:S(2)}) collective-permute-start(f32[2]{0:T(128)} %param.13), channel_id=1, source_target_pairs={{0,2},{1,3},{2,0},{3,1},{4,6},{5,7},{6,4},{7,5},{8,10},{9,11},{10,... | collective-permute-start | bytes 32 | tf_op jit(solution)/shard_map/ppermute | solution.py:441
  4.3 15.7 %collective-permute-start = (f32[2]{0:T(128)}, f32[2]{0:T(128)S(1)}, u32[]{:S(2)}, u32[]{:S(2)}) collective-permute-start(f32[2]{0:T(128)} %param.13), channel_id=1, source_target_pairs={{0,1},{1,2},{2,3},{3,0},{4,5},{5,6},{6,7},{7,4},{8,9},{9,10},{10,1... | collective-permute-start | bytes 32 | tf_op jit(solution)/shard_map/ppermute | solution.py:441
  4.6 15.4 %collective-permute-start.2 = (f32[2]{0:T(128)}, f32[2]{0:T(128)S(1)}, u32[]{:S(2)}, u32[]{:S(2)}) collective-permute-start(f32[2]{0:T(128)} %param.13), channel_id=1, source_target_pairs={{0,3},{1,0},{2,1},{3,2},{4,7},{5,4},{6,5},{7,6},{8,11},{9,8},{10,9... | collective-permute-start | bytes 32 | tf_op jit(solution)/shard_map/ppermute | solution.py:441
  9.5 3.2 %copy-start.4 = (bf16[32,8,1024]{2,1,0:T(8,128)(2,1)S(1)}, bf16[32,8,1024]{2,1,0:T(8,128)(2,1)}, u32[]{:S(2)}) copy-start(bf16[32,8,1024]{2,1,0:T(8,128)(2,1)} %angle_ref.1) | copy-start | bytes 1572868
  10.3 3.1 %copy-start.3 = (s32[32,8,1024]{2,1,0:T(8,128)S(1)}, s32[32,8,1024]{2,1,0:T(8,128)}, u32[]{:S(2)}) copy-start(s32[32,8,1024]{2,1,0:T(8,128)} %tissue_ref.1) | copy-start | bytes 3145732
  18.3 2.5 %copy-start.5 = (s32[128]{0:T(128)}, s32[128]{0:T(128)S(1)}, u32[]{:S(2)}) copy-start(s32[128]{0:T(128)S(1)} %gather_fusion) | copy-start | bytes 1540
  18.3 1.7 %copy-start.7 = (f32[2]{0:T(128)S(1)}, f32[2]{0:T(128)}, u32[]{:S(2)}) copy-start(f32[2]{0:T(128)} %param.13) | copy-start | bytes 28
  20.9 16.4 %copy-start.2 = (bf16[32,8,1024]{2,1,0:T(8,128)(2,1)S(1)}, bf16[32,8,1024]{2,1,0:T(8,128)(2,1)}, u32[]{:S(2)}) copy-start(bf16[32,8,1024]{2,1,0:T(8,128)(2,1)} %l_ref.3) | copy-start | bytes 1572868
  22.3 36.8 %all-to-all-start = ((f32[64,1,3200]{2,1,0:T(1,128)}), f32[64,1,3200]{2,1,0:T(1,128)S(1)}, u32[]{:S(2)}, u32[]{:S(2)}) async-start(f32[64,1,3200]{2,1,0:T(1,128)} %all_to_all.14), calls=%async_computation | async-start | bytes 1638400 | tf_op jit(solution)/shard_map/all_to_all | solution.py:452
  38.0 16.9 %collective-permute-start.4 = (f32[32,3,1024]{2,1,0:T(4,128)S(1)}, f32[32,3,1024]{2,1,0:T(4,128)S(1)}, u32[]{:S(2)}, u32[]{:S(2)}) collective-permute-start(f32[32,3,1024]{2,1,0:T(4,128)S(1)} %pad_maximum_fusion.4), channel_id=1, source_target_pairs={{1,0},{2,1},{3,2},{5,4},{6,5},{7,6},{9,8},{10,9},{11,10},{13,12},{... | collective-permute-start | bytes 1179656 | tf_op jit(solution)/shard_map/ppermute | solution.py:466
  39.6 15.3 %collective-permute-start.3 = (f32[32,3,1024]{2,1,0:T(4,128)S(1)}, f32[32,3,1024]{2,1,0:T(4,128)S(1)}, u32[]{:S(2)}, u32[]{:S(2)}) collective-permute-start(f32[32,3,1024]{2,1,0:T(4,128)S(1)} %pad_maximum_fusion.3), channel_id=1, source_target_pairs={{0,1},{1,2},{2,3},{4,5},{5,6},{6,7},{8,9},{9,10},{10,11},{12,13},{... | collective-permute-start | bytes 1179656 | tf_op jit(solution)/shard_map/ppermute | solution.py:466
  63.4 13.9 %copy-start.6 = (s32[32]{0:T(128)S(1)}, s32[32]{0:T(128)}, u32[]{:S(2)}) copy-start(s32[32]{0:T(128)} %own_ref.1) | copy-start | bytes 388

commit v14 on v13

--- a/solution.py
+++ b/solution.py
@@ -106,7 +106,7 @@
 
 
 GROUP = 8
-OUTER = 4
+OUTER = 16
 
 
 def expanders(edge, cells):

time: 102 us -> 101 us (level)
  no operation moved by 1% of the time
where the time goes in v14:
time: 101 us
  starting transfers between devices  25 us (25%)
  Pallas kernels  23.9 us (24%)
  blocking collectives  22.7 us (22%)
  local copies, waits for them, and re-layouts  12.2 us (12%)
  other arithmetic  9.61 us (10%)
  matrix products  3.59 us (4%)
  waiting for transfers between devices  2.98 us (3%)
  between operations  1.08 us (1%)
    all_to_all x1, blocking collectives, body(): lax.all_to_all(shares.reshape(devices, own_cells), ('blk', 'par'), split_...  22.7 us
    all_to_all x1, starting transfers between devices, body(): lax.all_to_all(sending, 'blk', split_axis=0, concat_axis=0, tiled=True)  13.2 us
    pallas_call x1, Pallas kernels, outer_step(): pl.pallas_call(outer_kernel, grid=(bricks // OUTER,), in_specs=[pl.BlockS...  12.9 us
    pallas_call x1, Pallas kernels, inner_step(): pl.pallas_call(inner_kernel, grid=(bricks // GROUP,), in_specs=[blk3(), b...  11 us
    ppermute x3, starting transfers between devices, body(): lax.ppermute(conductance, 'par', [(i, (i + s) % parts) for i in range(par...  6.32 us
    ppermute x1, starting transfers between devices, body(): lax.ppermute(last, 'par', up)  4.2 us
    dot_general x4, matrix products, boundary(): jnp.dot(values.astype(jnp.float32).reshape(bricks * z_layers, plane_cells...  3.59 us
    all_to_all x1, waiting for transfers between devices, body(): lax.all_to_all(sending, 'blk', split_axis=0, concat_axis=0, tiled=True)  2.97 us
  transfers between devices with their start and end apart: 6, of which 1 were waited for; matrix products, arithmetic and copies ran while one was open for 17% of the time, Pallas kernels for 11%

profile of v14, /device:TPU:1, one launch (start us, length us, event | category | flops | bytes accessed | tf_op | source)
XLA Modules:
  0.0 101.0 jit_solution(14959260758284200238)
XLA Ops:
  0.6 0.0 copy-start
  0.7 3.6 %collective-permute-start.1 = (f32[2]{0:T(128)}, f32[2]{0:T(128)S(1)}, u32[]{:S(2)}, u32[]{:S(2)}) collective-permute-start(f32[2]{0:T(128)} %param.13), channel_id=1, source_target_pairs={{0,2},{1,3},{2,0},{3,1},{4,6},{5,7},{6,4},{7,5},{8,10},{9,11},{10,... | collective-permute-start | bytes 32 | tf_op jit(solution)/shard_map/ppermute | solution.py:441
  4.3 0.3 collective-permute-start
  4.6 2.4 %collective-permute-start.2 = (f32[2]{0:T(128)}, f32[2]{0:T(128)S(1)}, u32[]{:S(2)}, u32[]{:S(2)}) collective-permute-start(f32[2]{0:T(128)} %param.13), channel_id=1, source_target_pairs={{0,3},{1,0},{2,1},{3,2},{4,7},{5,4},{6,5},{7,6},{8,11},{9,8},{10,9... | collective-permute-start | bytes 32 | tf_op jit(solution)/shard_map/ppermute | solution.py:441
  7.0 0.7 convert_element_type.38
  7.7 0.7 compare_select_fusion
  8.4 0.1 copy.26
  8.5 0.1 reshape.461
  8.6 0.7 add.160
  9.2 0.1 add.161
  9.3 0.1 iota_compare_fusion.2
  9.4 0.1 iota_compare_fusion
  9.6 0.8 fusion.21
  10.3 1.4 %convolution_bitcast_fusion = f32[256,128]{0,1:T(8,128)S(1)} fusion(pred[128,1024]{1,0:T(32,128)(4,1)S(1)} %bitcast.78, bf16[32,8,1024]{2,1,0:T(8,128)(2,1)} %l_ref.3), kind=kOutput, calls=%fused_computation.5 | convolution fusion | flops 67108864 | bytes 786432 | tf_op jit(solution)/shard_map/dot_general | solution.py:419
  11.8 0.1 copy.30
  11.9 0.7 convolution_bitcast_fusion.1
  12.6 0.1 copy.29
  12.7 0.7 fusion.1
  13.4 0.7 convolution_bitcast_fusion.2
  14.2 0.1 copy.27
  14.3 0.1 copy.28
  14.4 0.3 integer_pow.14
  14.6 0.4 fusion.12
  15.1 0.3 reshape.447
  15.3 0.3 reshape.450
  15.6 0.3 reshape.452
  15.9 0.3 fusion.5
  16.2 0.4 pad_maximum_fusion
  16.6 0.1 copy.31
  16.7 0.4 reshape.487
  17.2 1.1 %gather_fusion = s32[128]{0:T(128)S(1)} fusion(s32[2048]{0:T(1024)S(1)} %copy-done, s32[1024]{0:T(1024)S(1)} %pad_clamp_fusion.2), kind=kCustom, calls=%fused_computation | custom fusion | bytes 1536 | tf_op jit(solution)/shard_map/gather | solution.py:404
  18.4 0.2 convert_reduce_fusion
  18.6 1.2 %scatter_custom_fusion = f32[256,768]{1,0:T(8,128)S(1)} fusion(s32[128]{0:T(128)S(1)} %get-tuple-element.30, f32[128,768]{1,0:T(8,128)S(1)} %reshape.487, f32[]{:T(128)} %constant.36.clone.1), kind=kCustom, calls=%fused_computation.24 | custom fusion | bytes 786436 | tf_op jit(solution)/shard_map/scatter | solution.py:439
  19.8 0.2 reshape.454
  20.1 0.6 gather_fusion.1
  20.6 0.1 reshape.455
  20.7 0.1 fusion.13
  20.8 0.1 pad_maximum_fusion.2
  20.9 1.5 %all_to_all.14 = f32[64,1,3200]{2,1,0:T(1,128)} reshape(f32[64,3200]{1,0:T(8,128)S(1)} %pad_maximum_fusion.2) | data formatting | bytes 1638400 | tf_op jit(solution)/shard_map/all_to_all | solution.py:452
  22.3 13.2 %all-to-all-start = ((f32[64,1,3200]{2,1,0:T(1,128)}), f32[64,1,3200]{2,1,0:T(1,128)S(1)}, u32[]{:S(2)}, u32[]{:S(2)}) async-start(f32[64,1,3200]{2,1,0:T(1,128)} %all_to_all.14), calls=%async_computation | async-start | bytes 1638400 | tf_op jit(solution)/shard_map/all_to_all | solution.py:452
  35.5 1.8 %slice_convert_fusion.1 = (f32[32,1,1024]{2,1,0:T(1,128)S(1)}, f32[32,1,1024]{2,1,0:T(1,128)S(1)}) fusion(s32[32,8,1024]{2,1,0:T(8,128)} %tissue_ref.1), kind=kLoop, calls=%fused_computation.32 | loop fusion | flops 65536 | bytes 524288 | tf_op jit(solution)/shard_map/convert_element_type | solution.py:464
  37.3 0.3 fusion.22
  37.6 0.3 pad_maximum_fusion.4
  38.0 1.3 %collective-permute-start.4 = (f32[32,3,1024]{2,1,0:T(4,128)S(1)}, f32[32,3,1024]{2,1,0:T(4,128)S(1)}, u32[]{:S(2)}, u32[]{:S(2)}) collective-permute-start(f32[32,3,1024]{2,1,0:T(4,128)S(1)} %pad_maximum_fusion.4), channel_id=1, source_target_pairs={{1,0},{2,1},{3,2},{5,4},{6,5},{7,6},{9,8},{10,9},{11,10},{13,12},{... | collective-permute-start | bytes 1179656 | tf_op jit(solution)/shard_map/ppermute | solution.py:466
  39.3 0.3 pad_maximum_fusion.3
  39.6 4.2 %collective-permute-start.3 = (f32[32,3,1024]{2,1,0:T(4,128)S(1)}, f32[32,3,1024]{2,1,0:T(4,128)S(1)}, u32[]{:S(2)}, u32[]{:S(2)}) collective-permute-start(f32[32,3,1024]{2,1,0:T(4,128)S(1)} %pad_maximum_fusion.3), channel_id=1, source_target_pairs={{0,1},{1,2},{2,3},{4,5},{5,6},{6,7},{8,9},{9,10},{10,11},{12,13},{... | collective-permute-start | bytes 1179656 | tf_op jit(solution)/shard_map/ppermute | solution.py:466
  43.9 11.0 %shard_map.112 = (f32[32,8,1024]{2,1,0:T(8,128)}, f32[32,8,1024]{2,1,0:T(8,128)}, f32[32,8,1024]{2,1,0:T(8,128)}, f32[32,1,128]{2,1,0:T(1,128)}) custom-call(s32[32,8,1024]{2,1,0:T(8,128)} %tissue_ref.1, bf16[32,8,1024]{2,1,0:T(8,128)(2,1)} %angle_ref.1, f32[32,8,1024]{2,1,0:T(8,128)} %u_ref.3, bf16[32,8,1024]{2,1,0:T(8,128)(2,1)} %l_ref.3), custom_call_target="tpu_custom_call" | custom-call | tf_op jit(solution)/shard_map/pallas_call | solution.py:350
  54.9 1.3 %pad_maximum_fusion.1.halo_ref = f32[32,6,1024]{2,1,0:T(8,128)} fusion(f32[32,3,1024]{2,1,0:T(4,128)S(1)} %collective-permute-done.4, f32[32,3,1024]{2,1,0:T(4,128)S(1)} %collective-permute-done.3), kind=kLoop, calls=%fused_computation.11 | loop fusion | flops 196608 | bytes 1572864 | tf_op jit(solution)/shard_map/concatenate | solution.py:466
  56.2 3.0 %all-to-all-done = f32[64,1,3200]{2,1,0:T(1,128)S(1)} async-done(((f32[64,1,3200]{2,1,0:T(1,128)}), f32[64,1,3200]{2,1,0:T(1,128)S(1)}, u32[]{:S(2)}, u32[]{:S(2)}) %all-to-all-start) | async-done | bytes 819232 | tf_op jit(solution)/shard_map/all_to_all | solution.py:452
  59.2 0.1 copy.35
  59.2 0.1 slice_convert_fusion.2
  59.3 0.1 slice.54
  59.4 0.7 convert_element_type.40.cell_ref
  60.0 0.7 reshape.456.cond_ref
  60.7 0.2 reshape.457
  60.9 0.8 gather_fusion.2
  61.7 1.6 %reshape.458.face_ref = f32[32,4,24,32]{3,2,1,0:T(8,128)} reshape(f32[128,768]{1,0:T(8,128)S(1)} %gather_fusion.2) | data formatting | bytes 786432 | tf_op jit(solution)/shard_map/reshape | solution.py:457
  63.4 12.9 %shard_map.113 = (f32[32,8,1024]{2,1,0:T(8,128)}, f32[32,8,1024]{2,1,0:T(8,128)}, f32[32,1,128]{2,1,0:T(1,128)}) custom-call(f32[512]{0:T(512)} %reshape.456.cond_ref, s32[2048]{0:T(1024)} %convert_element_type.40.cell_ref, s32[32]{0:T(128)} %own_ref.1, s32[128]{0:T(128)} %copy-done.5, bf16[4,32,1024]{2,1,0:T(8,128)(2,1)} %get-tuple-element.19.expand_ref, ...), custom_call_target="tpu_custom_call" | custom-call | tf_op jit(solution)/shard_map/pallas_call | solution.py:367
  76.2 1.0 %reduce_sum.53 = f32[32]{0:T(128)S(1)} reduce(f32[32,1,128]{2,1,0:T(1,128)} %get-tuple-element.16, f32[]{:T(128)} %constant.36.clone.1), dimensions={1,2}, to_apply=%region_3.4 | reduce | flops 4064 | bytes 16516 | tf_op jit(solution)/shard_map/reduce_sum | solution.py:470
  77.3 0.1 select_reduce_fusion
  77.4 0.1 all_to_all.17
  77.5 22.7 %all_to_all.21 = f32[256,1,2]{2,1,0:T(1,128)S(1)} all-to-all(f32[256,1,2]{2,1,0:T(1,128)S(1)} %bitcast.85), channel_id=1, replica_groups=mesh['blk'=64,'par'=4] {'blk','par'}, dimensions={0} | all-to-all | bytes 4096 | tf_op jit(solution)/shard_map/all_to_all | solution.py:474
  100.2 0.3 reduce_sum.55
  100.5 0.5 multiply_divide_fusion
  (32 shorter events, 0.1 us)
Async XLA Ops:
  0.6 16.5 %copy-start = (s32[2048]{0:T(1024)S(1)}, s32[2048]{0:T(1024)}, u32[]{:S(2)}) copy-start(s32[2048]{0:T(1024)} %param.14) | copy-start | bytes 24580
  0.6 11.2 %copy-start.1 = (f32[32,8,1024]{2,1,0:T(8,128)S(1)}, f32[32,8,1024]{2,1,0:T(8,128)}, u32[]{:S(2)}) copy-start(f32[32,8,1024]{2,1,0:T(8,128)} %u_ref.3) | copy-start | bytes 3145732
  0.7 19.3 %collective-permute-start.1 = (f32[2]{0:T(128)}, f32[2]{0:T(128)S(1)}, u32[]{:S(2)}, u32[]{:S(2)}) collective-permute-start(f32[2]{0:T(128)} %param.13), channel_id=1, source_target_pairs={{0,2},{1,3},{2,0},{3,1},{4,6},{5,7},{6,4},{7,5},{8,10},{9,11},{10,... | collective-permute-start | bytes 32 | tf_op jit(solution)/shard_map/ppermute | solution.py:441
  4.3 15.7 %collective-permute-start = (f32[2]{0:T(128)}, f32[2]{0:T(128)S(1)}, u32[]{:S(2)}, u32[]{:S(2)}) collective-permute-start(f32[2]{0:T(128)} %param.13), channel_id=1, source_target_pairs={{0,1},{1,2},{2,3},{3,0},{4,5},{5,6},{6,7},{7,4},{8,9},{9,10},{10,1... | collective-permute-start | bytes 32 | tf_op jit(solution)/shard_map/ppermute | solution.py:441
  4.6 15.4 %collective-permute-start.2 = (f32[2]{0:T(128)}, f32[2]{0:T(128)S(1)}, u32[]{:S(2)}, u32[]{:S(2)}) collective-permute-start(f32[2]{0:T(128)} %param.13), channel_id=1, source_target_pairs={{0,3},{1,0},{2,1},{3,2},{4,7},{5,4},{6,5},{7,6},{8,11},{9,8},{10,9... | collective-permute-start | bytes 32 | tf_op jit(solution)/shard_map/ppermute | solution.py:441
  9.5 3.2 %copy-start.4 = (bf16[32,8,1024]{2,1,0:T(8,128)(2,1)S(1)}, bf16[32,8,1024]{2,1,0:T(8,128)(2,1)}, u32[]{:S(2)}) copy-start(bf16[32,8,1024]{2,1,0:T(8,128)(2,1)} %angle_ref.1) | copy-start | bytes 1572868
  10.3 3.1 %copy-start.3 = (s32[32,8,1024]{2,1,0:T(8,128)S(1)}, s32[32,8,1024]{2,1,0:T(8,128)}, u32[]{:S(2)}) copy-start(s32[32,8,1024]{2,1,0:T(8,128)} %tissue_ref.1) | copy-start | bytes 3145732
  18.3 2.5 %copy-start.5 = (s32[128]{0:T(128)}, s32[128]{0:T(128)S(1)}, u32[]{:S(2)}) copy-start(s32[128]{0:T(128)S(1)} %gather_fusion) | copy-start | bytes 1540
  18.3 1.7 %copy-start.7 = (f32[2]{0:T(128)S(1)}, f32[2]{0:T(128)}, u32[]{:S(2)}) copy-start(f32[2]{0:T(128)} %param.13) | copy-start | bytes 28
  20.9 16.4 %copy-start.2 = (bf16[32,8,1024]{2,1,0:T(8,128)(2,1)S(1)}, bf16[32,8,1024]{2,1,0:T(8,128)(2,1)}, u32[]{:S(2)}) copy-start(bf16[32,8,1024]{2,1,0:T(8,128)(2,1)} %l_ref.3) | copy-start | bytes 1572868
  22.3 36.8 %all-to-all-start = ((f32[64,1,3200]{2,1,0:T(1,128)}), f32[64,1,3200]{2,1,0:T(1,128)S(1)}, u32[]{:S(2)}, u32[]{:S(2)}) async-start(f32[64,1,3200]{2,1,0:T(1,128)} %all_to_all.14), calls=%async_computation | async-start | bytes 1638400 | tf_op jit(solution)/shard_map/all_to_all | solution.py:452
  38.0 16.9 %collective-permute-start.4 = (f32[32,3,1024]{2,1,0:T(4,128)S(1)}, f32[32,3,1024]{2,1,0:T(4,128)S(1)}, u32[]{:S(2)}, u32[]{:S(2)}) collective-permute-start(f32[32,3,1024]{2,1,0:T(4,128)S(1)} %pad_maximum_fusion.4), channel_id=1, source_target_pairs={{1,0},{2,1},{3,2},{5,4},{6,5},{7,6},{9,8},{10,9},{11,10},{13,12},{... | collective-permute-start | bytes 1179656 | tf_op jit(solution)/shard_map/ppermute | solution.py:466
  39.6 15.3 %collective-permute-start.3 = (f32[32,3,1024]{2,1,0:T(4,128)S(1)}, f32[32,3,1024]{2,1,0:T(4,128)S(1)}, u32[]{:S(2)}, u32[]{:S(2)}) collective-permute-start(f32[32,3,1024]{2,1,0:T(4,128)S(1)} %pad_maximum_fusion.3), channel_id=1, source_target_pairs={{0,1},{1,2},{2,3},{4,5},{5,6},{6,7},{8,9},{9,10},{10,11},{12,13},{... | collective-permute-start | bytes 1179656 | tf_op jit(solution)/shard_map/ppermute | solution.py:466
  63.4 13.9 %copy-start.6 = (s32[32]{0:T(128)S(1)}, s32[32]{0:T(128)}, u32[]{:S(2)}) copy-start(s32[32]{0:T(128)} %own_ref.1) | copy-start | bytes 388
